TPU v7x, 32 devices: a whole 2x2x4 slice. The times are simulated.
32 devices in a mesh: site: 8 (over z, y), sp: 4 (over x, core).
Axes of the slice: x: 2, y: 2, z: 4, core: 2. Of those that a mesh axis runs over, the one named last changes fastest.
Arguments:
- counts: int32 [8, 5120, 2048], P('site', None, 'sp'), may hold values from 0 to 6
- factors: float32 [8, 16, 5120], P('site'), may hold values from -2.5 to 2.5
- loadings: float32 [2048, 16], P('sp'), may hold values from -0.4 to 0.4
- factor_momenta: float32 [8, 16, 5120], P('site'), may hold values from -6 to 6
- loading_momenta: float32 [2048, 16], P('sp'), may hold values from -6 to 6
- precision: float32 [16], replicated, may hold values from 0.5 to 4
- factor_step: float32 [1], replicated, may hold values from 0.03 to 0.07
- loading_step: float32 [1], replicated, may hold values from 0.0002 to 0.0008
Outputs:
- new_factors: float32 [8, 16, 5120], P('site')
- new_factor_momenta: float32 [8, 16, 5120], P('site')
- new_loadings: float32 [2048, 16], P('sp')
- new_loading_momenta: float32 [2048, 16], P('sp')
- energy: float32 [1], replicated
All inputs are finite; a program needn't handle non-finite values.
Results may differ from a plain program's by a relative error of at most 0.0001.
Values sent between devices are 32-bit elements; how exact they have to be, the bound alone decides.
No kernel may reach another device: no remote copies, remote signals or barrier semaphores. Data moves between devices by JAX's collectives and lax.ppermute only.
A program may use at most 128 MiB of HBM per device.

v0:
```python
import functools

import jax
import jax.numpy as jnp
from jax import lax
from jax.experimental import pallas as pl
from jax.experimental.pallas import tpu as pltpu
from jax.sharding import PartitionSpec as P


TY = 64
TGY = 8
LANES = 128

kappa_sq = 0.25
LOG2E = 1.4426950408889634
LN2 = 0.6931471805599453
f32, bf16 = jnp.float32, jnp.bfloat16


VMEM = pl.BlockSpec(memory_space=pltpu.VMEM)
SMEM = pl.BlockSpec(memory_space=pltpu.SMEM)
HBM = pl.BlockSpec(memory_space=pltpu.HBM)


def swap(block, axis, mask):
    return lax.ppermute(block, axis, [(i, i ^ mask) for i in range(lax.axis_size(axis))])


def from_behind(block, axis, distance):
    devices = range(lax.axis_size(axis))
    route = [(i - distance, i) for i in devices if i - distance in devices]
    return lax.ppermute(block, axis, route)


def mask_groups(n):
    groups, stride = [], 1
    while stride < n:
        radix = 2 if stride == 1 or n // stride == 2 else 4
        groups.append([stride * g for g in range(1, radix)])
        stride *= radix
    return groups


def add(terms):
    return functools.reduce(lambda a, b: a + b, terms)


def sum_terms(block, axis, groups):
    terms = [block]
    for masks in groups:
        total = add(terms)
        terms = [total] + [swap(total, axis, m) for m in masks]
    return terms


def call(kernel, in_specs, outs, scratch=(), limit=4, held=()):
    return pl.pallas_call(
        kernel,
        in_specs=in_specs,
        out_specs=[VMEM] * (len(outs) + len(held)),
        out_shape=[jax.ShapeDtypeStruct(s, f32) for s in outs]
        + [jax.ShapeDtypeStruct(s, jnp.int32) for s in held],
        scratch_shapes=list(scratch),
        compiler_params=pltpu.CompilerParams(vmem_limit_bytes=limit << 20),
    )


def core():
    return lax.rem(lax.axis_index("sp"), 2)


def split3(x):
    h = x.astype(bf16)
    r = x - h.astype(f32)
    m = r.astype(bf16)
    return h, m, (r - m.astype(f32)).astype(bf16)


def dotg(a, b, ca, cb):
    return lax.dot_general(a, b, (((ca,), (cb,)), ((), ())), preferred_element_type=f32)


def evaluate_block(zb, counts, ly, lg, k):
    h, m, l = split3(zb)
    y = dotg(jnp.concatenate([h, h, h, m, m, l], 0), ly, 0, 0)
    i = jnp.exp2(y)
    c = counts.astype(f32)
    r = c - i
    rh = r.astype(bf16)
    rl = (r - rh.astype(f32)).astype(bf16)
    a = dotg(lg, rh, 1, 1)
    b = dotg(lg[:k], rl, 1, 1)
    fac = a[:k] + a[k:] + b
    a = dotg(jnp.concatenate([h, m], 0), rh, 1, 0)
    b = dotg(h, rl, 1, 0)
    load = a[:k] + a[k:] + b
    return fac, load, c, y, i


def fill_loadings(lt, ly_ref, lg_ref):
    h, m, l = split3(lt * f32(LOG2E))
    ly_ref[...] = jnp.concatenate([h, m, l, h, m, h], 0)
    h, m, _ = split3(lt)
    lg_ref[...] = jnp.concatenate([h, m], 0)


def first_kernel(k, half, sub, z_ref, lt_ref, cnt_ref, own_ref, oth_ref, load_ref, buf_ref, ly_ref, lg_ref, sem):
    c = core()
    steps = half // sub

    def copy(i):
        rho = 1 - i // steps
        at = pl.multiple_of(lax.rem(rho + c, 2) * half + (i % steps) * sub, sub)
        return pltpu.make_async_copy(cnt_ref.at[0, pl.ds(at, sub)], buf_ref.at[pl.ds(i * sub, sub)], sem.at[i])

    for i in range(2 * steps):
        copy(i).start()
    fill_loadings(lt_ref[...], ly_ref, lg_ref)
    ly, lg = ly_ref[...], lg_ref[...]
    total = None
    for i in range(2 * steps):
        rho = 1 - i // steps
        at = pl.multiple_of(lax.rem(rho + c, 2) * half + (i % steps) * sub, sub)
        copy(i).wait()
        fac, load, _, _, _ = evaluate_block(z_ref[0, :, pl.ds(at, sub)], buf_ref[pl.ds(i * sub, sub), :], ly, lg, k)
        (oth_ref if rho else own_ref)[:, pl.ds((i % steps) * sub, sub)] = fac
        total = load if total is None else total + load
    load_ref[...] = total


def second_kernel(k, half, sub, n_terms, *refs):
    terms = refs[:n_terms]
    zown_ref, zoth_ref, lt_ref, lm_ref, sl_ref, cnt_ref = refs[n_terms : n_terms + 6]
    own_ref, oth_ref, load_ref, newl_ref, halfl_ref, ly_ref, lg_ref = refs[n_terms + 6 :]
    steps = half // sub
    step = sl_ref[0]
    grad = add([t[...] for t in terms]) - lt_ref[...]
    halfl = lm_ref[...] + 0.5 * step * grad
    newl = lt_ref[...] + step * halfl
    halfl_ref[...] = halfl
    newl_ref[...] = newl
    fill_loadings(newl, ly_ref, lg_ref)
    ly, lg = ly_ref[...], lg_ref[...]
    total = None
    lik = None
    for i in range(2 * steps):
        rho = 1 - i // steps
        z_ref = zoth_ref if rho else zown_ref
        here = pl.ds((i % steps) * sub, sub)
        fac, load, cf, y, inten = evaluate_block(z_ref[:, here], cnt_ref[pl.ds(i * sub, sub), :], ly, lg, k)
        (oth_ref if rho else own_ref)[:, here] = fac
        total = load if total is None else total + load
        term = jnp.sum((inten - (cf * f32(LN2)) * y).reshape(sub // 8, 8, y.shape[1]), 0)
        lik = term if lik is None else lik + term
    load_ref[:k, :] = total
    load_ref[k:, :] = lik


def lane(shape):
    return lax.broadcasted_iota(jnp.int32, shape, len(shape) - 1)


def pack_rims(vregs, k):
    q = lax.rem(lane((k, LANES)), TY)
    first = jnp.zeros((k, LANES), f32)
    last = jnp.zeros((k, LANES), f32)
    for j, v in enumerate(vregs):
        first = jnp.where(q == j, pltpu.roll(v, j, 1) if j else v, first)
        last = jnp.where(q == j, pltpu.roll(v, (j - TY + 1) % LANES, 1), last)
    return first, last


def prior_of(vregs, lo, hi, left, right, upper, lower, k):
    q = lax.rem(lane((k, LANES)), TY)
    n = len(vregs)
    wide = lane((k, LANES))
    out = []
    zero = jnp.zeros((k, LANES), f32)
    for j in range(lo, hi):
        v = vregs[j]
        back = pltpu.roll(v, 1, 1)
        ahead = pltpu.roll(v, LANES - 1, 1)
        lrim = pltpu.roll(left, (LANES - j) % LANES, 1) if j else left
        rrim = pltpu.roll(right, (TY - 1 - j) % LANES, 1)
        beside = jnp.where(q == 0, lrim, back) + jnp.where(q == TY - 1, rrim, ahead)
        prev = vregs[j - 1] if j else upper
        nxt = vregs[j + 1] if j + 1 < n else lower
        shift_down = pltpu.roll(v, TY, 1)
        above = jnp.where(wide < TY, pltpu.roll(prev, TY, 1), shift_down)
        below = jnp.where(wide >= LANES - TY, pltpu.roll(nxt, LANES - TY, 1), pltpu.roll(v, LANES - TY, 1))
        out.append((kappa_sq + 4.0) * v - (above + below + beside))
    return out


def vregs_of(array):
    return [array[:, j * LANES : (j + 1) * LANES] for j in range(array.shape[1] // LANES)]


def rims_kernel(k, z_ref, first_ref, last_ref):
    first_ref[...], last_ref[...] = pack_rims(vregs_of(z_ref[0]), k)


def ahead_kernel(k, half, z_ref, mom_ref, left_ref, right_ref, upper_ref, lower_ref, gain_ref, sf_ref, a_ref, z_own_ref, s_ref):
    c = core()
    step = sf_ref[0]
    out = prior_of(
        vregs_of(z_ref[0]), 0, 2 * half // LANES, left_ref[...], right_ref[...], upper_ref[...], lower_ref[...], k
    )
    n = half // LANES
    gain = gain_ref[...] * (0.5 * step)
    for j in range(n):
        at = pl.ds(j * LANES, LANES)
        own = jnp.where(c == 0, out[j], out[n + j])
        src = pl.ds(pl.multiple_of(c * half + j * LANES, LANES), LANES)
        a_ref[:, at] = mom_ref[0, :, src] - gain * own
        z_own_ref[:, at] = z_ref[0, :, src]
    s_ref[...] = jnp.full(s_ref.shape, step, f32)


def move_kernel(half, own_ref, other_ref, a_ref, z_ref, s_ref, half_ref, moved_ref):
    for j in range(half // LANES):
        at = pl.ds(j * LANES, LANES)
        h = a_ref[:, at] + (0.5 * s_ref[...]) * (own_ref[:, at] + other_ref[:, at])
        half_ref[:, at] = h
        moved_ref[:, at] = z_ref[:, at] + s_ref[...] * h


def join_kernel(k, own_ref, oth_ref, full_ref, first_ref, last_ref):
    c = core()
    own, oth = vregs_of(own_ref[...]), vregs_of(oth_ref[...])
    low = [jnp.where(c == 0, a, b) for a, b in zip(own, oth)]
    high = [jnp.where(c == 0, b, a) for a, b in zip(own, oth)]
    vregs = low + high
    for j, v in enumerate(vregs):
        full_ref[0, :, j * LANES : (j + 1) * LANES] = v
    first_ref[...], last_ref[...] = pack_rims(vregs, k)


def behind_kernel(k, half, z_ref, h_ref, left_ref, right_ref, upper_ref, lower_ref, gain_ref, s_ref, a_ref, e_ref):
    c = core()
    out = prior_of(
        vregs_of(z_ref[0]), 0, 2 * half // LANES, left_ref[...], right_ref[...], upper_ref[...], lower_ref[...], k
    )
    n = half // LANES
    gain = gain_ref[...]
    energy = jnp.zeros((k, LANES), f32)
    for j in range(n):
        at = pl.ds(j * LANES, LANES)
        own = gain * jnp.where(c == 0, out[j], out[n + j])
        src = pl.ds(pl.multiple_of(c * half + j * LANES, LANES), LANES)
        energy = energy + z_ref[0, :, src] * own
        a_ref[:, at] = h_ref[:, at] - (0.5 * s_ref[...]) * own
    e_ref[...] = energy


def end_kernel(k, half, own_ref, other_ref, a_ref, s_ref, pe_ref, end_ref, b_ref):
    energy = pe_ref[...]
    for j in range(half // LANES):
        at = pl.ds(j * LANES, LANES)
        e = a_ref[:, at] + (0.5 * s_ref[...]) * (own_ref[:, at] + other_ref[:, at])
        end_ref[:, at] = e
        energy = energy + e * e
    b_ref[...] = 0.5 * sum(energy[g * 8 : (g + 1) * 8] for g in range(k // 8))


def pair_kernel(half, own_ref, oth_ref, full_ref):
    c = core()
    own, oth = own_ref[...], oth_ref[...]
    full_ref[0, :, :half] = jnp.where(c == 0, own, oth)
    full_ref[0, :, half:] = jnp.where(c == 0, oth, own)


def loading_end_kernel(k, n_terms, *refs):
    terms = refs[:n_terms]
    newl_ref, halfl_ref, sl_ref, end_ref, s_ref = refs[n_terms:]
    total = add([t[...] for t in terms])
    newl = newl_ref[...]
    end = halfl_ref[...] + (0.5 * sl_ref[0]) * (total[:k] - newl)
    end_ref[...] = end
    squares = 0.5 * (end * end + newl * newl)
    energy = total[k:] + sum(squares[g * 8 : (g + 1) * 8] for g in range(k // 8))
    s_ref[...] = sum(energy[:, j * LANES : (j + 1) * LANES] for j in range(energy.shape[1] // LANES))


def local(
    counts, factors, loadings, factor_momenta, loading_momenta, precision, factor_step, loading_step
):
    k, cells = factors.shape[1:]
    species = loadings.shape[0]
    half = cells // 2
    sub = 640 if half % 640 == 0 else half
    n_site, n_sp = lax.axis_size("site"), lax.axis_size("sp")
    site, chips = mask_groups(n_site), mask_groups(n_sp)[1:]
    lt, lm = loadings.T, loading_momenta.T
    gain = jnp.broadcast_to(precision[:, None], (k, LANES))
    zero_rim = jnp.zeros((k, LANES), f32)

    def rims_from(first, last, full):
        left = from_behind(last, "site", 1)
        right = from_behind(first, "site", -1)
        if n_site > TGY:
            low, high = full[0, :, :TY], full[0, :, cells - TY :]
            lead = jnp.zeros((k, LANES - TY), f32)
            upper = jnp.concatenate([lead, from_behind(high, "site", TGY)], 1)
            lower = jnp.concatenate([from_behind(low, "site", -TGY), lead], 1)
        else:
            upper, lower = zero_rim, zero_rim
        return left, right, upper, lower

    def share(own, oth):
        terms = sum_terms(own + swap(oth, "sp", 1), "sp", chips)
        return terms[0], add(terms[1:])

    loadings_scratch = [pltpu.VMEM((6 * k, species), bf16), pltpu.VMEM((2 * k, species), bf16)]
    own, oth, load, held = call(
        functools.partial(first_kernel, k, half, sub),
        [VMEM, VMEM, HBM],
        [(k, half), (k, half), (k, species)],
        loadings_scratch
        + [pltpu.SemaphoreType.DMA((cells // sub,))],
        16,
        [(cells, species)],
    )(factors, lt, pltpu.with_memory_space_constraint(counts, pltpu.HBM))
    load_terms = sum_terms(load, "site", site)
    own, other = share(own, oth)

    first, last = call(functools.partial(rims_kernel, k), [VMEM], [(k, LANES)] * 2)(factors)
    a1, z_own, svec = call(
        functools.partial(ahead_kernel, k, half), [VMEM] * 7 + [SMEM], [(k, half), (k, half), (k, LANES)]
    )(factors, factor_momenta, *rims_from(first, last, factors), gain, factor_step)
    half_own, moved_own = call(
        functools.partial(move_kernel, half), [VMEM] * 5, [(k, half)] * 2
    )(own, other, a1, z_own, svec)
    moved_oth = swap(moved_own, "sp", 1)
    new_factors, first, last = call(
        functools.partial(join_kernel, k), [VMEM] * 2, [(1, k, cells), (k, LANES), (k, LANES)]
    )(moved_own, moved_oth)

    own, oth, load, newl, halfl = call(
        functools.partial(second_kernel, k, half, sub, len(load_terms)),
        [VMEM] * (len(load_terms) + 4) + [SMEM, VMEM],
        [(k, half), (k, half), (k + 8, species), (k, species), (k, species)],
        loadings_scratch,
        20,
    )(*load_terms, moved_own, moved_oth, lt, lm, loading_step, held)
    load_terms = sum_terms(load, "site", site)
    own, other = share(own, oth)

    a2, prior_energy = call(
        functools.partial(behind_kernel, k, half), [VMEM] * 8, [(k, half), (k, LANES)]
    )(new_factors, half_own, *rims_from(first, last, new_factors), gain, svec)
    end_own, b_part = call(
        functools.partial(end_kernel, k, half), [VMEM] * 5, [(k, half), (8, LANES)]
    )(own, other, a2, svec, prior_energy)
    end_oth = swap(end_own, "sp", 1)
    (new_momenta,) = call(functools.partial(pair_kernel, half), [VMEM] * 2, [(1, k, cells)])(end_own, end_oth)

    endl, s_part = call(
        functools.partial(loading_end_kernel, k, len(load_terms)),
        [VMEM] * (len(load_terms) + 2) + [SMEM],
        [(k, species), (8, LANES)],
    )(*load_terms, newl, halfl, loading_step)
    total = add(sum_terms(s_part, "sp", chips) + sum_terms(b_part, "site", site))
    total = total + swap(total, "sp", 1)
    entries = n_site * cells * n_sp * species
    energy = jnp.reshape(jnp.sum(total) / entries, (1,))
    return new_factors, new_momenta, newl.T, endl.T, energy


def solution(mesh):
    placed = (
        P("site", None, "sp"),
        P("site", None, None),
        P("sp", None),
        P("site", None, None),
        P("sp", None),
        P(),
        P(),
        P(),
    )

    return jax.shard_map(
        local,
        mesh=mesh,
        in_specs=placed,
        out_specs=(P("site", None, None), P("site", None, None), P("sp", None), P("sp", None), P()),
        check_vma=False,
    )
```

profile of v0, /device:TPU:0, one launch (start us, length us, event | category | flops | bytes accessed | tf_op | source)
XLA Modules:
  0.0 84.4 jit_solution(4659030203634608785)
XLA Ops:
  2.4 9.6 %shard_map.119 = (f32[16,2560]{1,0:T(8,128)S(1)}, f32[16,2560]{1,0:T(8,128)S(1)}, f32[16,512]{1,0:T(8,128)S(1)}, s32[5120,512]{1,0:T(8,128)S(1)}) custom-call(f32[1,16,5120]{2,1,0:T(8,128)S(1)} %copy-done, f32[16,512]{1,0:T(8,128)S(1)} %bitcast.5, s32[1,5120,512]{2,1,0:T(8,128)} %cnt_ref.1), custom_call_target="tpu_custom_call" | custom-call | tf_op jit(solution)/shard_map/pallas_call | solution.py:316
  13.6 2.9 %collective-permute-start.1 = (f32[16,2560]{1,0:T(8,128)S(1)}, f32[16,2560]{1,0:T(8,128)S(1)}, u32[]{:S(2)}, u32[]{:S(2)}) collective-permute-start(f32[16,2560]{1,0:T(8,128)S(1)} %add.33.own_ref), channel_id=1, source_target_pairs={{0,2},{1,3},{2,0},{3,1},{4,6},{5,7},{6,4},{7,5},{8,10},{9,11},{10,... | collective-permute-start | bytes 491528 | tf_op jit(solution)/shard_map/ppermute | solution.py:27
  16.8 3.4 %collective-permute-start.2 = (f32[16,128]{1,0:T(8,128)S(1)}, f32[16,128]{1,0:T(8,128)S(1)}, u32[]{:S(2)}, u32[]{:S(2)}) collective-permute-start(f32[16,128]{1,0:T(8,128)S(1)} %get-tuple-element.32), channel_id=1, source_target_pairs={{0,4},{4,8},{8,12},{12,16},{16,20},{20,24},{24,28},{1,5},{5,9},{9,... | collective-permute-start | bytes 24584 | tf_op jit(solution)/shard_map/ppermute | solution.py:33
  20.2 1.5 %collective-permute-start.3 = (f32[16,128]{1,0:T(8,128)S(1)}, f32[16,128]{1,0:T(8,128)S(1)}, u32[]{:S(2)}, u32[]{:S(2)}) collective-permute-start(f32[16,128]{1,0:T(8,128)S(1)} %get-tuple-element.33), channel_id=1, source_target_pairs={{4,0},{8,4},{12,8},{16,12},{20,16},{24,20},{28,24},{5,1},{9,5},{13... | collective-permute-start | bytes 24584 | tf_op jit(solution)/shard_map/ppermute | solution.py:33
  22.3 3.4 %collective-permute-done.3.right_ref = f32[16,128]{1,0:T(8,128)S(1)} collective-permute-done((f32[16,128]{1,0:T(8,128)S(1)}, f32[16,128]{1,0:T(8,128)S(1)}, u32[]{:S(2)}, u32[]{:S(2)}) %collective-permute-start.3) | collective-permute-done | bytes 8224 | tf_op jit(solution)/shard_map/ppermute | solution.py:33
  26.5 2.5 %collective-permute-start.5 = (f32[16,512]{1,0:T(8,128)S(1)}, f32[16,512]{1,0:T(8,128)S(1)}, u32[]{:S(2)}, u32[]{:S(2)}) collective-permute-start(f32[16,512]{1,0:T(8,128)S(1)} %get-tuple-element.39), channel_id=1, source_target_pairs={{0,4},{4,0},{8,12},{12,8},{16,20},{20,16},{24,28},{28,24},{1,5},{5... | collective-permute-start | bytes 98312 | tf_op jit(solution)/shard_map/ppermute | solution.py:27
  29.0 2.0 %collective-permute-done.5 = f32[16,512]{1,0:T(8,128)S(1)} collective-permute-done((f32[16,512]{1,0:T(8,128)S(1)}, f32[16,512]{1,0:T(8,128)S(1)}, u32[]{:S(2)}, u32[]{:S(2)}) %collective-permute-start.5) | collective-permute-done | bytes 32800 | tf_op jit(solution)/shard_map/ppermute | solution.py:27
  30.9 3.1 %collective-permute-start.8 = (f32[16,512]{1,0:T(8,128)S(1)}, f32[16,512]{1,0:T(8,128)S(1)}, u32[]{:S(2)}, u32[]{:S(2)}) collective-permute-start(f32[16,512]{1,0:T(8,128)S(1)} %add.34.refs_0_), channel_id=1, source_target_pairs={{0,24},{4,28},{8,16},{12,20},{16,8},{20,12},{24,0},{28,4},{1,25},{... | collective-permute-start | bytes 98312 | tf_op jit(solution)/shard_map/ppermute | solution.py:27
  34.1 1.3 %collective-permute-start.6 = (f32[16,512]{1,0:T(8,128)S(1)}, f32[16,512]{1,0:T(8,128)S(1)}, u32[]{:S(2)}, u32[]{:S(2)}) collective-permute-start(f32[16,512]{1,0:T(8,128)S(1)} %add.34.refs_0_), channel_id=1, source_target_pairs={{0,8},{4,12},{8,0},{12,4},{16,24},{20,28},{24,16},{28,20},{1,9},{5... | collective-permute-start | bytes 98312 | tf_op jit(solution)/shard_map/ppermute | solution.py:27
  36.7 2.2 %collective-permute-done.7.refs_2_ = f32[16,512]{1,0:T(8,128)S(1)} collective-permute-done((f32[16,512]{1,0:T(8,128)S(1)}, f32[16,512]{1,0:T(8,128)S(1)}, u32[]{:S(2)}, u32[]{:S(2)}) %collective-permute-start.7) | collective-permute-done | bytes 32800 | tf_op jit(solution)/shard_map/ppermute | solution.py:27
  38.9 6.3 %shard_map.124 = (f32[16,2560]{1,0:T(8,128)S(1)}, f32[16,2560]{1,0:T(8,128)S(1)}, f32[24,512]{1,0:T(8,128)S(1)}, f32[16,512]{1,0:T(8,128)}, f32[16,512]{1,0:T(8,128)S(1)}) custom-call(f32[16,512]{1,0:T(8,128)S(1)} %add.34.refs_0_, f32[16,512]{1,0:T(8,128)S(1)} %collective-permute-done.6.refs_1_, f32[16,512]{1,0:T(8,128)S(1)} %collective-permute-done.7.refs_2_, ...), custom_call_target="tpu_custom_call" | custom-call | tf_op jit(solution)/shard_map/pallas_call | solution.py:340
  45.2 1.4 %collective-permute-done.9 = f32[16,2560]{1,0:T(8,128)S(1)} collective-permute-done((f32[16,2560]{1,0:T(8,128)S(1)}, f32[16,2560]{1,0:T(8,128)S(1)}, u32[]{:S(2)}, u32[]{:S(2)}) %collective-permute-start.9) | collective-permute-done | bytes 163872 | tf_op jit(solution)/shard_map/ppermute | solution.py:27
  48.2 3.1 %collective-permute-done.14 = f32[24,512]{1,0:T(8,128)S(1)} collective-permute-done((f32[24,512]{1,0:T(8,128)S(1)}, f32[24,512]{1,0:T(8,128)S(1)}, u32[]{:S(2)}, u32[]{:S(2)}) %collective-permute-start.14) | collective-permute-done | bytes 49184 | tf_op jit(solution)/shard_map/ppermute | solution.py:27
  51.4 1.6 %collective-permute-start.17 = (f32[24,512]{1,0:T(8,128)S(1)}, f32[24,512]{1,0:T(8,128)S(1)}, u32[]{:S(2)}, u32[]{:S(2)}) collective-permute-start(f32[24,512]{1,0:T(8,128)S(1)} %add.36.refs_0_), channel_id=1, source_target_pairs={{0,24},{4,28},{8,16},{12,20},{16,8},{20,12},{24,0},{28,4},{1,25},{... | collective-permute-start | bytes 147464 | tf_op jit(solution)/shard_map/ppermute | solution.py:27
  53.5 2.3 %collective-permute-start.15 = (f32[24,512]{1,0:T(8,128)S(1)}, f32[24,512]{1,0:T(8,128)S(1)}, u32[]{:S(2)}, u32[]{:S(2)}) collective-permute-start(f32[24,512]{1,0:T(8,128)S(1)} %add.36.refs_0_), channel_id=1, source_target_pairs={{0,8},{4,12},{8,0},{12,4},{16,24},{20,28},{24,16},{28,20},{1,9},{5... | collective-permute-start | bytes 147464 | tf_op jit(solution)/shard_map/ppermute | solution.py:27
  56.7 2.8 %collective-permute-start.11 = (f32[16,128]{1,0:T(8,128)S(1)}, f32[16,128]{1,0:T(8,128)S(1)}, u32[]{:S(2)}, u32[]{:S(2)}) collective-permute-start(f32[16,128]{1,0:T(8,128)S(1)} %get-tuple-element.44), channel_id=1, source_target_pairs={{0,4},{4,8},{8,12},{12,16},{16,20},{20,24},{24,28},{1,5},{5,9},{9,... | collective-permute-start | bytes 24584 | tf_op jit(solution)/shard_map/ppermute | solution.py:33
  59.5 1.3 %collective-permute-done.11.left_ref = f32[16,128]{1,0:T(8,128)S(1)} collective-permute-done((f32[16,128]{1,0:T(8,128)S(1)}, f32[16,128]{1,0:T(8,128)S(1)}, u32[]{:S(2)}, u32[]{:S(2)}) %collective-permute-start.11) | collective-permute-done | bytes 8224 | tf_op jit(solution)/shard_map/ppermute | solution.py:33
  60.9 1.3 %collective-permute-start.12 = (f32[16,128]{1,0:T(8,128)S(1)}, f32[16,128]{1,0:T(8,128)S(1)}, u32[]{:S(2)}, u32[]{:S(2)}) collective-permute-start(f32[16,128]{1,0:T(8,128)S(1)} %get-tuple-element.45), channel_id=1, source_target_pairs={{4,0},{8,4},{12,8},{16,12},{20,16},{24,20},{28,24},{5,1},{9,5},{13... | collective-permute-start | bytes 24584 | tf_op jit(solution)/shard_map/ppermute | solution.py:33
  62.2 4.5 %collective-permute-done.12.right_ref = f32[16,128]{1,0:T(8,128)S(1)} collective-permute-done((f32[16,128]{1,0:T(8,128)S(1)}, f32[16,128]{1,0:T(8,128)S(1)}, u32[]{:S(2)}, u32[]{:S(2)}) %collective-permute-start.12) | collective-permute-done | bytes 8224 | tf_op jit(solution)/shard_map/ppermute | solution.py:33
  68.2 3.0 %collective-permute-start.19 = (f32[8,128]{1,0:T(8,128)S(1)}, f32[8,128]{1,0:T(8,128)S(1)}, u32[]{:S(2)}, u32[]{:S(2)}) collective-permute-start(f32[8,128]{1,0:T(8,128)S(1)} %get-tuple-element.54), channel_id=1, source_target_pairs={{0,4},{4,0},{8,12},{12,8},{16,20},{20,16},{24,28},{28,24},{1,5},{5... | collective-permute-start | bytes 12296 | tf_op jit(solution)/shard_map/ppermute | solution.py:27
  72.6 1.5 %collective-permute-start.18 = (f32[8,128]{1,0:T(8,128)S(1)}, f32[8,128]{1,0:T(8,128)S(1)}, u32[]{:S(2)}, u32[]{:S(2)}) collective-permute-start(f32[8,128]{1,0:T(8,128)S(1)} %get-tuple-element.53), channel_id=1, source_target_pairs={{0,2},{1,3},{2,0},{3,1},{4,6},{5,7},{6,4},{7,5},{8,10},{9,11},{10,... | collective-permute-start | bytes 12296 | tf_op jit(solution)/shard_map/ppermute | solution.py:27
  74.1 1.3 %collective-permute-start.22 = (f32[8,128]{1,0:T(8,128)S(1)}, f32[8,128]{1,0:T(8,128)S(1)}, u32[]{:S(2)}, u32[]{:S(2)}) collective-permute-start(f32[8,128]{1,0:T(8,128)S(1)} %add.38), channel_id=1, source_target_pairs={{0,24},{4,28},{8,16},{12,20},{16,8},{20,12},{24,0},{28,4},{1,25},{... | collective-permute-start | bytes 12296 | tf_op jit(solution)/shard_map/ppermute | solution.py:27
  76.0 2.5 %collective-permute-start.20 = (f32[8,128]{1,0:T(8,128)S(1)}, f32[8,128]{1,0:T(8,128)S(1)}, u32[]{:S(2)}, u32[]{:S(2)}) collective-permute-start(f32[8,128]{1,0:T(8,128)S(1)} %add.38), channel_id=1, source_target_pairs={{0,8},{4,12},{8,0},{12,4},{16,24},{20,28},{24,16},{28,20},{1,9},{5... | collective-permute-start | bytes 12296 | tf_op jit(solution)/shard_map/ppermute | solution.py:27
  80.1 1.2 %collective-permute-done.23 = f32[8,128]{1,0:T(8,128)S(1)} collective-permute-done((f32[8,128]{1,0:T(8,128)S(1)}, f32[8,128]{1,0:T(8,128)S(1)}, u32[]{:S(2)}, u32[]{:S(2)}) %collective-permute-start.23) | collective-permute-done | bytes 4128 | tf_op jit(solution)/shard_map/ppermute | solution.py:27
  (59 shorter events, 14.5 us)
Async XLA Ops:
  12.0 1.6 %collective-permute-start = (f32[16,2560]{1,0:T(8,128)S(1)}, f32[16,2560]{1,0:T(8,128)S(1)}, u32[]{:S(2)}, u32[]{:S(2)}) collective-permute-start(f32[16,2560]{1,0:T(8,128)S(1)} %get-tuple-element.31), channel_id=1, source_target_pairs={{0,1},{1,0},{2,3},{3,2},{4,5},{5,4},{6,7},{7,6},{8,9},{9,8},{10,11... | collective-permute-start | bytes 491528 | tf_op jit(solution)/shard_map/ppermute | solution.py:27
  13.6 12.7 %collective-permute-start.1 = (f32[16,2560]{1,0:T(8,128)S(1)}, f32[16,2560]{1,0:T(8,128)S(1)}, u32[]{:S(2)}, u32[]{:S(2)}) collective-permute-start(f32[16,2560]{1,0:T(8,128)S(1)} %add.33.own_ref), channel_id=1, source_target_pairs={{0,2},{1,3},{2,0},{3,1},{4,6},{5,7},{6,4},{7,5},{8,10},{9,11},{10,... | collective-permute-start | bytes 491528 | tf_op jit(solution)/shard_map/ppermute | solution.py:27
  16.8 5.6 %collective-permute-start.2 = (f32[16,128]{1,0:T(8,128)S(1)}, f32[16,128]{1,0:T(8,128)S(1)}, u32[]{:S(2)}, u32[]{:S(2)}) collective-permute-start(f32[16,128]{1,0:T(8,128)S(1)} %get-tuple-element.32), channel_id=1, source_target_pairs={{0,4},{4,8},{8,12},{12,16},{16,20},{20,24},{24,28},{1,5},{5,9},{9,... | collective-permute-start | bytes 24584 | tf_op jit(solution)/shard_map/ppermute | solution.py:33
  20.2 5.5 %collective-permute-start.3 = (f32[16,128]{1,0:T(8,128)S(1)}, f32[16,128]{1,0:T(8,128)S(1)}, u32[]{:S(2)}, u32[]{:S(2)}) collective-permute-start(f32[16,128]{1,0:T(8,128)S(1)} %get-tuple-element.33), channel_id=1, source_target_pairs={{4,0},{8,4},{12,8},{16,12},{20,16},{24,20},{28,24},{5,1},{9,5},{13... | collective-permute-start | bytes 24584 | tf_op jit(solution)/shard_map/ppermute | solution.py:33
  26.4 12.5 %collective-permute-start.4 = (f32[16,2560]{1,0:T(8,128)S(1)}, f32[16,2560]{1,0:T(8,128)S(1)}, u32[]{:S(2)}, u32[]{:S(2)}) collective-permute-start(f32[16,2560]{1,0:T(8,128)S(1)} %get-tuple-element.37.own_ref.refs_4_), channel_id=1, source_target_pairs={{0,1},{1,0},{2,3},{3,2},{4,5},{5,4},{6,7},{7,6},{8,9},{9,8},{10,11... | collective-permute-start | bytes 491528 | tf_op jit(solution)/shard_map/ppermute | solution.py:27
  26.5 4.5 %collective-permute-start.5 = (f32[16,512]{1,0:T(8,128)S(1)}, f32[16,512]{1,0:T(8,128)S(1)}, u32[]{:S(2)}, u32[]{:S(2)}) collective-permute-start(f32[16,512]{1,0:T(8,128)S(1)} %get-tuple-element.39), channel_id=1, source_target_pairs={{0,4},{4,0},{8,12},{12,8},{16,20},{20,16},{24,28},{28,24},{1,5},{5... | collective-permute-start | bytes 98312 | tf_op jit(solution)/shard_map/ppermute | solution.py:27
  30.9 5.8 %collective-permute-start.8 = (f32[16,512]{1,0:T(8,128)S(1)}, f32[16,512]{1,0:T(8,128)S(1)}, u32[]{:S(2)}, u32[]{:S(2)}) collective-permute-start(f32[16,512]{1,0:T(8,128)S(1)} %add.34.refs_0_), channel_id=1, source_target_pairs={{0,24},{4,28},{8,16},{12,20},{16,8},{20,12},{24,0},{28,4},{1,25},{... | collective-permute-start | bytes 98312 | tf_op jit(solution)/shard_map/ppermute | solution.py:27
  34.1 4.8 %collective-permute-start.7 = (f32[16,512]{1,0:T(8,128)S(1)}, f32[16,512]{1,0:T(8,128)S(1)}, u32[]{:S(2)}, u32[]{:S(2)}) collective-permute-start(f32[16,512]{1,0:T(8,128)S(1)} %add.34.refs_0_), channel_id=1, source_target_pairs={{0,16},{4,20},{8,24},{12,28},{16,0},{20,4},{24,8},{28,12},{1,17},{... | collective-permute-start | bytes 98312 | tf_op jit(solution)/shard_map/ppermute | solution.py:27
  34.1 4.8 %collective-permute-start.6 = (f32[16,512]{1,0:T(8,128)S(1)}, f32[16,512]{1,0:T(8,128)S(1)}, u32[]{:S(2)}, u32[]{:S(2)}) collective-permute-start(f32[16,512]{1,0:T(8,128)S(1)} %add.34.refs_0_), channel_id=1, source_target_pairs={{0,8},{4,12},{8,0},{12,4},{16,24},{20,28},{24,16},{28,20},{1,9},{5... | collective-permute-start | bytes 98312 | tf_op jit(solution)/shard_map/ppermute | solution.py:27
  45.2 1.4 %collective-permute-start.9 = (f32[16,2560]{1,0:T(8,128)S(1)}, f32[16,2560]{1,0:T(8,128)S(1)}, u32[]{:S(2)}, u32[]{:S(2)}) collective-permute-start(f32[16,2560]{1,0:T(8,128)S(1)} %get-tuple-element.42), channel_id=1, source_target_pairs={{0,1},{1,0},{2,3},{3,2},{4,5},{5,4},{6,7},{7,6},{8,9},{9,8},{10,11... | collective-permute-start | bytes 491528 | tf_op jit(solution)/shard_map/ppermute | solution.py:27
  46.7 21.5 %collective-permute-start.10 = (f32[16,2560]{1,0:T(8,128)S(1)}, f32[16,2560]{1,0:T(8,128)S(1)}, u32[]{:S(2)}, u32[]{:S(2)}) collective-permute-start(f32[16,2560]{1,0:T(8,128)S(1)} %add.35.own_ref), channel_id=1, source_target_pairs={{0,2},{1,3},{2,0},{3,1},{4,6},{5,7},{6,4},{7,5},{8,10},{9,11},{10,... | collective-permute-start | bytes 491528 | tf_op jit(solution)/shard_map/ppermute | solution.py:27
  47.3 4.1 %collective-permute-start.14 = (f32[24,512]{1,0:T(8,128)S(1)}, f32[24,512]{1,0:T(8,128)S(1)}, u32[]{:S(2)}, u32[]{:S(2)}) collective-permute-start(f32[24,512]{1,0:T(8,128)S(1)} %get-tuple-element.50), channel_id=1, source_target_pairs={{0,4},{4,0},{8,12},{12,8},{16,20},{20,16},{24,28},{28,24},{1,5},{5... | collective-permute-start | bytes 147464 | tf_op jit(solution)/shard_map/ppermute | solution.py:27
  51.4 19.8 %collective-permute-start.17 = (f32[24,512]{1,0:T(8,128)S(1)}, f32[24,512]{1,0:T(8,128)S(1)}, u32[]{:S(2)}, u32[]{:S(2)}) collective-permute-start(f32[24,512]{1,0:T(8,128)S(1)} %add.36.refs_0_), channel_id=1, source_target_pairs={{0,24},{4,28},{8,16},{12,20},{16,8},{20,12},{24,0},{28,4},{1,25},{... | collective-permute-start | bytes 147464 | tf_op jit(solution)/shard_map/ppermute | solution.py:27
  53.0 18.2 %collective-permute-start.16 = (f32[24,512]{1,0:T(8,128)S(1)}, f32[24,512]{1,0:T(8,128)S(1)}, u32[]{:S(2)}, u32[]{:S(2)}) collective-permute-start(f32[24,512]{1,0:T(8,128)S(1)} %add.36.refs_0_), channel_id=1, source_target_pairs={{0,16},{4,20},{8,24},{12,28},{16,0},{20,4},{24,8},{28,12},{1,17},{... | collective-permute-start | bytes 147464 | tf_op jit(solution)/shard_map/ppermute | solution.py:27
  53.5 17.7 %collective-permute-start.15 = (f32[24,512]{1,0:T(8,128)S(1)}, f32[24,512]{1,0:T(8,128)S(1)}, u32[]{:S(2)}, u32[]{:S(2)}) collective-permute-start(f32[24,512]{1,0:T(8,128)S(1)} %add.36.refs_0_), channel_id=1, source_target_pairs={{0,8},{4,12},{8,0},{12,4},{16,24},{20,28},{24,16},{28,20},{1,9},{5... | collective-permute-start | bytes 147464 | tf_op jit(solution)/shard_map/ppermute | solution.py:27
  56.7 4.2 %collective-permute-start.11 = (f32[16,128]{1,0:T(8,128)S(1)}, f32[16,128]{1,0:T(8,128)S(1)}, u32[]{:S(2)}, u32[]{:S(2)}) collective-permute-start(f32[16,128]{1,0:T(8,128)S(1)} %get-tuple-element.44), channel_id=1, source_target_pairs={{0,4},{4,8},{8,12},{12,16},{16,20},{20,24},{24,28},{1,5},{5,9},{9,... | collective-permute-start | bytes 24584 | tf_op jit(solution)/shard_map/ppermute | solution.py:33
  60.9 5.8 %collective-permute-start.12 = (f32[16,128]{1,0:T(8,128)S(1)}, f32[16,128]{1,0:T(8,128)S(1)}, u32[]{:S(2)}, u32[]{:S(2)}) collective-permute-start(f32[16,128]{1,0:T(8,128)S(1)} %get-tuple-element.45), channel_id=1, source_target_pairs={{4,0},{8,4},{12,8},{16,12},{20,16},{24,20},{28,24},{5,1},{9,5},{13... | collective-permute-start | bytes 24584 | tf_op jit(solution)/shard_map/ppermute | solution.py:33
  68.2 5.9 %collective-permute-start.19 = (f32[8,128]{1,0:T(8,128)S(1)}, f32[8,128]{1,0:T(8,128)S(1)}, u32[]{:S(2)}, u32[]{:S(2)}) collective-permute-start(f32[8,128]{1,0:T(8,128)S(1)} %get-tuple-element.54), channel_id=1, source_target_pairs={{0,4},{4,0},{8,12},{12,8},{16,20},{20,16},{24,28},{28,24},{1,5},{5... | collective-permute-start | bytes 12296 | tf_op jit(solution)/shard_map/ppermute | solution.py:27
  72.6 5.9 %collective-permute-start.18 = (f32[8,128]{1,0:T(8,128)S(1)}, f32[8,128]{1,0:T(8,128)S(1)}, u32[]{:S(2)}, u32[]{:S(2)}) collective-permute-start(f32[8,128]{1,0:T(8,128)S(1)} %get-tuple-element.53), channel_id=1, source_target_pairs={{0,2},{1,3},{2,0},{3,1},{4,6},{5,7},{6,4},{7,5},{8,10},{9,11},{10,... | collective-permute-start | bytes 12296 | tf_op jit(solution)/shard_map/ppermute | solution.py:27
  74.1 5.4 %collective-permute-start.22 = (f32[8,128]{1,0:T(8,128)S(1)}, f32[8,128]{1,0:T(8,128)S(1)}, u32[]{:S(2)}, u32[]{:S(2)}) collective-permute-start(f32[8,128]{1,0:T(8,128)S(1)} %add.38), channel_id=1, source_target_pairs={{0,24},{4,28},{8,16},{12,20},{16,8},{20,12},{24,0},{28,4},{1,25},{... | collective-permute-start | bytes 12296 | tf_op jit(solution)/shard_map/ppermute | solution.py:27
  75.4 4.5 %collective-permute-start.21 = (f32[8,128]{1,0:T(8,128)S(1)}, f32[8,128]{1,0:T(8,128)S(1)}, u32[]{:S(2)}, u32[]{:S(2)}) collective-permute-start(f32[8,128]{1,0:T(8,128)S(1)} %add.38), channel_id=1, source_target_pairs={{0,16},{4,20},{8,24},{12,28},{16,0},{20,4},{24,8},{28,12},{1,17},{... | collective-permute-start | bytes 12296 | tf_op jit(solution)/shard_map/ppermute | solution.py:27
  76.0 4.1 %collective-permute-start.20 = (f32[8,128]{1,0:T(8,128)S(1)}, f32[8,128]{1,0:T(8,128)S(1)}, u32[]{:S(2)}, u32[]{:S(2)}) collective-permute-start(f32[8,128]{1,0:T(8,128)S(1)} %add.38), channel_id=1, source_target_pairs={{0,8},{4,12},{8,0},{12,4},{16,24},{20,28},{24,16},{28,20},{1,9},{5... | collective-permute-start | bytes 12296 | tf_op jit(solution)/shard_map/ppermute | solution.py:27
  78.5 4.0 %collective-permute-start.13 = (f32[16,2560]{1,0:T(8,128)S(1)}, f32[16,2560]{1,0:T(8,128)S(1)}, u32[]{:S(2)}, u32[]{:S(2)}) collective-permute-start(f32[16,2560]{1,0:T(8,128)S(1)} %get-tuple-element.48.own_ref), channel_id=1, source_target_pairs={{0,1},{1,0},{2,3},{3,2},{4,5},{5,4},{6,7},{7,6},{8,9},{9,8},{10,11... | collective-permute-start | bytes 491528 | tf_op jit(solution)/shard_map/ppermute | solution.py:27
  80.1 1.2 %collective-permute-start.23 = (f32[8,128]{1,0:T(8,128)S(1)}, f32[8,128]{1,0:T(8,128)S(1)}, u32[]{:S(2)}, u32[]{:S(2)}) collective-permute-start(f32[8,128]{1,0:T(8,128)S(1)} %add_add_fusion), channel_id=1, source_target_pairs={{0,1},{1,0},{2,3},{3,2},{4,5},{5,4},{6,7},{7,6},{8,9},{9,8},{10,11... | collective-permute-start | bytes 12296 | tf_op jit(solution)/shard_map/ppermute | solution.py:27
  (8 other events, 125.0 us)
where the time goes:
time: 84.8 us; the launch traced here: 84.4 us
  starting transfers between devices  34.3 us (40%)
  waiting for transfers between devices  22.5 us (27%)
  Pallas kernels  19.5 us (23%)
  between operations  3.89 us (5%)
  local copies, waits for them, and re-layouts  3.54 us (4%)
    ppermute x20, starting transfers between devices, swap(): lax.ppermute(block, axis, [(i, i ^ mask) for i in range(lax.axis_size(axi...  25.3 us
    ppermute x20, waiting for transfers between devices, swap(): lax.ppermute(block, axis, [(i, i ^ mask) for i in range(lax.axis_size(axi...  13.2 us
    pallas_call x1, Pallas kernels, local(): call(functools.partial(first_kernel, k, half, sub), [VMEM, VMEM, HBM], [(...  9.62 us
    ppermute x4, waiting for transfers between devices, from_behind(): return lax.ppermute(block, axis, route)  9.27 us
    ppermute x4, starting transfers between devices, from_behind(): return lax.ppermute(block, axis, route)  9.01 us
    pallas_call x1, Pallas kernels, local(): call(functools.partial(second_kernel, k, half, sub, len(load_terms)), [VM...  6.33 us
    unnamed x16, local copies, waits for them, and re-layouts  3.47 us
  transfers between devices with their start and end apart: 24, of which 13 were waited for; matrix products, arithmetic and copies ran while one was open for 1% of the time, Pallas kernels for 3%

commit v1 on v0

--- a/solution.py
+++ b/solution.py
@@ -31,6 +31,11 @@
     devices = range(lax.axis_size(axis))
     route = [(i - distance, i) for i in devices if i - distance in devices]
     return lax.ppermute(block, axis, route)
+
+
+def paired(block, axis, first):
+    n = lax.axis_size(axis)
+    return lax.ppermute(block, axis, [(i, (i + 1 if (i - first) % 2 == 0 else i - 1) % n) for i in range(n)])
 
 
 def mask_groups(n):
@@ -105,7 +110,9 @@
     lg_ref[...] = jnp.concatenate([h, m], 0)
 
 
-def first_kernel(k, half, sub, z_ref, lt_ref, cnt_ref, own_ref, oth_ref, load_ref, buf_ref, ly_ref, lg_ref, sem):
+def first_kernel(
+    k, half, sub, z_hbm, lt_hbm, cnt_ref, own_ref, oth_ref, load_ref, buf_ref, ly_ref, lg_ref, z_ref, lt_ref, sem, sems
+):
     c = core()
     steps = half // sub
 
@@ -114,9 +121,17 @@
         at = pl.multiple_of(lax.rem(rho + c, 2) * half + (i % steps) * sub, sub)
         return pltpu.make_async_copy(cnt_ref.at[0, pl.ds(at, sub)], buf_ref.at[pl.ds(i * sub, sub)], sem.at[i])
 
+    small = [
+        pltpu.make_async_copy(lt_hbm, lt_ref, sems.at[0]),
+        pltpu.make_async_copy(z_hbm, z_ref, sems.at[1]),
+    ]
+    for job in small:
+        job.start()
     for i in range(2 * steps):
         copy(i).start()
+    small[0].wait()
     fill_loadings(lt_ref[...], ly_ref, lg_ref)
+    small[1].wait()
     ly, lg = ly_ref[...], lg_ref[...]
     total = None
     for i in range(2 * steps):
@@ -132,7 +147,7 @@
 def second_kernel(k, half, sub, n_terms, *refs):
     terms = refs[:n_terms]
     zown_ref, zoth_ref, lt_ref, lm_ref, sl_ref, cnt_ref = refs[n_terms : n_terms + 6]
-    own_ref, oth_ref, load_ref, newl_ref, halfl_ref, ly_ref, lg_ref = refs[n_terms + 6 :]
+    own_ref, oth_ref, load_ref, out_ref, newl_ref, halfl_ref, ly_ref, lg_ref = refs[n_terms + 6 :]
     steps = half // sub
     step = sl_ref[0]
     grad = add([t[...] for t in terms]) - lt_ref[...]
@@ -140,6 +155,7 @@
     newl = lt_ref[...] + step * halfl
     halfl_ref[...] = halfl
     newl_ref[...] = newl
+    out_ref[...] = newl
     fill_loadings(newl, ly_ref, lg_ref)
     ly, lg = ly_ref[...], lg_ref[...]
     total = None
@@ -193,20 +209,33 @@
     return out
 
 
+def sides(near, far):
+    me, n = lax.axis_index("site"), lax.axis_size("site")
+    even = lax.rem(me, 2) == 0
+    left = jnp.where(me == 0, 0.0, jnp.where(even, far, near))
+    right = jnp.where(me == n - 1, 0.0, jnp.where(even, near, far))
+    return left, right
+
+
+def rims_of(vregs, k):
+    first, last = pack_rims(vregs, k)
+    even = lax.rem(lax.axis_index("site"), 2) == 0
+    return jnp.where(even, last, first), jnp.where(even, first, last)
+
+
 def vregs_of(array):
     return [array[:, j * LANES : (j + 1) * LANES] for j in range(array.shape[1] // LANES)]
 
 
-def rims_kernel(k, z_ref, first_ref, last_ref):
-    first_ref[...], last_ref[...] = pack_rims(vregs_of(z_ref[0]), k)
-
-
-def ahead_kernel(k, half, z_ref, mom_ref, left_ref, right_ref, upper_ref, lower_ref, gain_ref, sf_ref, a_ref, z_own_ref, s_ref):
+def rims_kernel(k, z_ref, near_ref, far_ref):
+    near_ref[...], far_ref[...] = rims_of(vregs_of(z_ref[0]), k)
+
+
+def ahead_kernel(k, half, z_ref, mom_ref, near_ref, far_ref, upper_ref, lower_ref, gain_ref, sf_ref, a_ref, z_own_ref, s_ref):
     c = core()
     step = sf_ref[0]
-    out = prior_of(
-        vregs_of(z_ref[0]), 0, 2 * half // LANES, left_ref[...], right_ref[...], upper_ref[...], lower_ref[...], k
-    )
+    left, right = sides(near_ref[...], far_ref[...])
+    out = prior_of(vregs_of(z_ref[0]), 0, 2 * half // LANES, left, right, upper_ref[...], lower_ref[...], k)
     n = half // LANES
     gain = gain_ref[...] * (0.5 * step)
     for j in range(n):
@@ -226,30 +255,28 @@
         moved_ref[:, at] = z_ref[:, at] + s_ref[...] * h
 
 
-def join_kernel(k, own_ref, oth_ref, full_ref, first_ref, last_ref):
+def in_order(own, oth):
+    first = core() == 0
+    own, oth = vregs_of(own), vregs_of(oth)
+    return [jnp.where(first, a, b) for a, b in zip(own, oth)] + [jnp.where(first, b, a) for a, b in zip(own, oth)]
+
+
+def join_kernel(k, own_ref, oth_ref, near_ref, far_ref):
+    near_ref[...], far_ref[...] = rims_of(in_order(own_ref[...], oth_ref[...]), k)
+
+
+def behind_kernel(k, half, own_ref, oth_ref, h_ref, near_ref, far_ref, upper_ref, lower_ref, gain_ref, s_ref, a_ref, e_ref):
     c = core()
-    own, oth = vregs_of(own_ref[...]), vregs_of(oth_ref[...])
-    low = [jnp.where(c == 0, a, b) for a, b in zip(own, oth)]
-    high = [jnp.where(c == 0, b, a) for a, b in zip(own, oth)]
-    vregs = low + high
-    for j, v in enumerate(vregs):
-        full_ref[0, :, j * LANES : (j + 1) * LANES] = v
-    first_ref[...], last_ref[...] = pack_rims(vregs, k)
-
-
-def behind_kernel(k, half, z_ref, h_ref, left_ref, right_ref, upper_ref, lower_ref, gain_ref, s_ref, a_ref, e_ref):
-    c = core()
-    out = prior_of(
-        vregs_of(z_ref[0]), 0, 2 * half // LANES, left_ref[...], right_ref[...], upper_ref[...], lower_ref[...], k
-    )
+    left, right = sides(near_ref[...], far_ref[...])
+    z = in_order(own_ref[...], oth_ref[...])
+    out = prior_of(z, 0, 2 * half // LANES, left, right, upper_ref[...], lower_ref[...], k)
     n = half // LANES
     gain = gain_ref[...]
     energy = jnp.zeros((k, LANES), f32)
     for j in range(n):
         at = pl.ds(j * LANES, LANES)
         own = gain * jnp.where(c == 0, out[j], out[n + j])
-        src = pl.ds(pl.multiple_of(c * half + j * LANES, LANES), LANES)
-        energy = energy + z_ref[0, :, src] * own
+        energy = energy + own_ref[:, at] * own
         a_ref[:, at] = h_ref[:, at] - (0.5 * s_ref[...]) * own
     e_ref[...] = energy
 
@@ -296,17 +323,16 @@
     gain = jnp.broadcast_to(precision[:, None], (k, LANES))
     zero_rim = jnp.zeros((k, LANES), f32)
 
-    def rims_from(first, last, full):
-        left = from_behind(last, "site", 1)
-        right = from_behind(first, "site", -1)
+    def rims_from(near, far, low, high):
+        near = paired(near, "site", 0)
+        far = paired(far, "site", 1)
         if n_site > TGY:
-            low, high = full[0, :, :TY], full[0, :, cells - TY :]
             lead = jnp.zeros((k, LANES - TY), f32)
             upper = jnp.concatenate([lead, from_behind(high, "site", TGY)], 1)
             lower = jnp.concatenate([from_behind(low, "site", -TGY), lead], 1)
         else:
             upper, lower = zero_rim, zero_rim
-        return left, right, upper, lower
+        return near, far, upper, lower
 
     def share(own, oth):
         terms = sum_terms(own + swap(oth, "sp", 1), "sp", chips)
@@ -315,41 +341,46 @@
     loadings_scratch = [pltpu.VMEM((6 * k, species), bf16), pltpu.VMEM((2 * k, species), bf16)]
     own, oth, load, held = call(
         functools.partial(first_kernel, k, half, sub),
-        [VMEM, VMEM, HBM],
+        [HBM, HBM, HBM],
         [(k, half), (k, half), (k, species)],
         loadings_scratch
-        + [pltpu.SemaphoreType.DMA((cells // sub,))],
+        + [
+            pltpu.VMEM((1, k, cells), f32),
+            pltpu.VMEM((k, species), f32),
+            pltpu.SemaphoreType.DMA((cells // sub,)),
+            pltpu.SemaphoreType.DMA((2,)),
+        ],
         16,
         [(cells, species)],
-    )(factors, lt, pltpu.with_memory_space_constraint(counts, pltpu.HBM))
+    )(*[pltpu.with_memory_space_constraint(x, pltpu.HBM) for x in (factors, lt, counts)])
     load_terms = sum_terms(load, "site", site)
     own, other = share(own, oth)
 
-    first, last = call(functools.partial(rims_kernel, k), [VMEM], [(k, LANES)] * 2)(factors)
+    near, far = call(functools.partial(rims_kernel, k), [VMEM], [(k, LANES)] * 2)(factors)
     a1, z_own, svec = call(
         functools.partial(ahead_kernel, k, half), [VMEM] * 7 + [SMEM], [(k, half), (k, half), (k, LANES)]
-    )(factors, factor_momenta, *rims_from(first, last, factors), gain, factor_step)
+    )(factors, factor_momenta, *rims_from(near, far, factors[0, :, :TY], factors[0, :, cells - TY :]), gain, factor_step)
     half_own, moved_own = call(
         functools.partial(move_kernel, half), [VMEM] * 5, [(k, half)] * 2
     )(own, other, a1, z_own, svec)
     moved_oth = swap(moved_own, "sp", 1)
-    new_factors, first, last = call(
-        functools.partial(join_kernel, k), [VMEM] * 2, [(1, k, cells), (k, LANES), (k, LANES)]
-    )(moved_own, moved_oth)
-
-    own, oth, load, newl, halfl = call(
+    near, far = call(functools.partial(join_kernel, k), [VMEM] * 2, [(k, LANES)] * 2)(moved_own, moved_oth)
+    (new_factors,) = call(functools.partial(pair_kernel, half), [VMEM] * 2, [(1, k, cells)])(moved_own, moved_oth)
+
+    own, oth, load, new_loadings, newl, halfl = call(
         functools.partial(second_kernel, k, half, sub, len(load_terms)),
         [VMEM] * (len(load_terms) + 4) + [SMEM, VMEM],
-        [(k, half), (k, half), (k + 8, species), (k, species), (k, species)],
+        [(k, half), (k, half), (k + 8, species)] + [(k, species)] * 3,
         loadings_scratch,
         20,
     )(*load_terms, moved_own, moved_oth, lt, lm, loading_step, held)
     load_terms = sum_terms(load, "site", site)
     own, other = share(own, oth)
 
+    edges = new_factors[0, :, :TY], new_factors[0, :, cells - TY :]
     a2, prior_energy = call(
-        functools.partial(behind_kernel, k, half), [VMEM] * 8, [(k, half), (k, LANES)]
-    )(new_factors, half_own, *rims_from(first, last, new_factors), gain, svec)
+        functools.partial(behind_kernel, k, half), [VMEM] * 9, [(k, half), (k, LANES)]
+    )(moved_own, moved_oth, half_own, *rims_from(near, far, *edges), gain, svec)
     end_own, b_part = call(
         functools.partial(end_kernel, k, half), [VMEM] * 5, [(k, half), (8, LANES)]
     )(own, other, a2, svec, prior_energy)
@@ -365,7 +396,7 @@
     total = total + swap(total, "sp", 1)
     entries = n_site * cells * n_sp * species
     energy = jnp.reshape(jnp.sum(total) / entries, (1,))
-    return new_factors, new_momenta, newl.T, endl.T, energy
+    return new_factors, new_momenta, new_loadings.T, endl.T, energy
 
 
 def solution(mesh):

time: 84.8 us -> 81.6 us (0.962)
  starting transfers between devices: 34.3 us -> 29.9 us
  local copies, waits for them, and re-layouts: 3.54 us -> 0.09 us
  Pallas kernels: 19.5 us -> 22.4 us
  waiting for transfers between devices: 22.5 us -> 24.5 us
    ppermute x20, starting transfers between devices: 25.3 us -> 21 us  [swap(): lax.ppermute(block, axis, [(i, i ^ mask) for i in range(lax.axis_size(axi...]
    unnamed x16 -> x10, local copies, waits for them, and re-layouts: 3.47 us -> 0.02 us
    ppermute x20, waiting for transfers between devices: 13.2 us -> 16 us  [swap(): lax.ppermute(block, axis, [(i, i ^ mask) for i in range(lax.axis_size(axi...]
    pallas_call x3, Pallas kernels: 11 us -> 12.9 us  [the longest x1 12.2 us: local(): call(functools.partial(first_kernel, k, half, sub), [HBM, HBM, HBM], [(k,...]
  transfers between devices with their start and end apart: 24 -> 24, of which waited for: 13 -> 13; matrix products, arithmetic and copies ran while one was open for 1% -> 1% of each run, Pallas kernels for 3% -> 4%
where the time goes in v1:
time: 81.6 us; the launch traced here: 81.5 us
  starting transfers between devices  29.9 us (37%)
  waiting for transfers between devices  24.5 us (30%)
  Pallas kernels  22.4 us (27%)
  between operations  3.91 us (5%)
    ppermute x20, starting transfers between devices, swap(): lax.ppermute(block, axis, [(i, i ^ mask) for i in range(lax.axis_size(axi...  21 us
    ppermute x20, waiting for transfers between devices, swap(): lax.ppermute(block, axis, [(i, i ^ mask) for i in range(lax.axis_size(axi...  16 us
    pallas_call x1, Pallas kernels, local(): call(functools.partial(first_kernel, k, half, sub), [HBM, HBM, HBM], [(k,...  12.2 us
    ppermute x4, starting transfers between devices, paired(): lax.ppermute(block, axis, [(i, (i + 1 if (i - first) % 2 == 0 else i - 1)...  8.84 us
    ppermute x4, waiting for transfers between devices, paired(): lax.ppermute(block, axis, [(i, (i + 1 if (i - first) % 2 == 0 else i - 1)...  8.49 us
    pallas_call x1, Pallas kernels, local(): call(functools.partial(second_kernel, k, half, sub, len(load_terms)), [VM...  6.51 us
  transfers between devices with their start and end apart: 24, of which 13 were waited for; matrix products, arithmetic and copies ran while one was open for 1% of the time, Pallas kernels for 4%

profile of v1, /device:TPU:0, one launch (start us, length us, event | category | flops | bytes accessed | tf_op | source)
XLA Modules:
  0.0 81.5 jit_solution(7710191804771849303)
XLA Ops:
  0.7 12.2 %shard_map.119 = (f32[16,2560]{1,0:T(8,128)S(1)}, f32[16,2560]{1,0:T(8,128)S(1)}, f32[16,512]{1,0:T(8,128)S(1)}, s32[5120,512]{1,0:T(8,128)S(1)}) custom-call(f32[1,16,5120]{2,1,0:T(8,128)} %z_ref.3, f32[16,512]{1,0:T(8,128)} %bitcast.5, s32[1,5120,512]{2,1,0:T(8,128)} %cnt_ref.1), custom_call_target="tpu_custom_call" | custom-call | tf_op jit(solution)/shard_map/pallas_call | solution.py:342
  14.5 2.9 %collective-permute-start.1 = (f32[16,2560]{1,0:T(8,128)S(1)}, f32[16,2560]{1,0:T(8,128)S(1)}, u32[]{:S(2)}, u32[]{:S(2)}) collective-permute-start(f32[16,2560]{1,0:T(8,128)S(1)} %add.33.own_ref), channel_id=1, source_target_pairs={{0,2},{1,3},{2,0},{3,1},{4,6},{5,7},{6,4},{7,5},{8,10},{9,11},{10,... | collective-permute-start | bytes 491528 | tf_op jit(solution)/shard_map/ppermute | solution.py:27
  17.6 1.6 %collective-permute-start.2 = (f32[16,128]{1,0:T(8,128)S(1)}, f32[16,128]{1,0:T(8,128)S(1)}, u32[]{:S(2)}, u32[]{:S(2)}) collective-permute-start(f32[16,128]{1,0:T(8,128)S(1)} %get-tuple-element.32), channel_id=1, source_target_pairs={{0,4},{4,0},{8,12},{12,8},{16,20},{20,16},{24,28},{28,24},{1,5},{5... | collective-permute-start | bytes 24584 | tf_op jit(solution)/shard_map/ppermute | solution.py:38
  19.2 3.5 %collective-permute-start.3 = (f32[16,128]{1,0:T(8,128)S(1)}, f32[16,128]{1,0:T(8,128)S(1)}, u32[]{:S(2)}, u32[]{:S(2)}) collective-permute-start(f32[16,128]{1,0:T(8,128)S(1)} %get-tuple-element.33), channel_id=1, source_target_pairs={{0,28},{4,8},{8,4},{12,16},{16,12},{20,24},{24,20},{28,0},{1,29},{... | collective-permute-start | bytes 24584 | tf_op jit(solution)/shard_map/ppermute | solution.py:38
  23.4 2.1 %collective-permute-done.3.far_ref = f32[16,128]{1,0:T(8,128)S(1)} collective-permute-done((f32[16,128]{1,0:T(8,128)S(1)}, f32[16,128]{1,0:T(8,128)S(1)}, u32[]{:S(2)}, u32[]{:S(2)}) %collective-permute-start.3) | collective-permute-done | bytes 8224 | tf_op jit(solution)/shard_map/ppermute | solution.py:38
  26.3 3.9 %collective-permute-done.5 = f32[16,512]{1,0:T(8,128)S(1)} collective-permute-done((f32[16,512]{1,0:T(8,128)S(1)}, f32[16,512]{1,0:T(8,128)S(1)}, u32[]{:S(2)}, u32[]{:S(2)}) %collective-permute-start.5) | collective-permute-done | bytes 32800 | tf_op jit(solution)/shard_map/ppermute | solution.py:27
  30.2 2.7 %collective-permute-start.7 = (f32[16,512]{1,0:T(8,128)S(1)}, f32[16,512]{1,0:T(8,128)S(1)}, u32[]{:S(2)}, u32[]{:S(2)}) collective-permute-start(f32[16,512]{1,0:T(8,128)S(1)} %add.34.refs_0_), channel_id=1, source_target_pairs={{0,16},{4,20},{8,24},{12,28},{16,0},{20,4},{24,8},{28,12},{1,17},{... | collective-permute-start | bytes 98312 | tf_op jit(solution)/shard_map/ppermute | solution.py:27
  33.0 1.6 %collective-permute-start.8 = (f32[16,512]{1,0:T(8,128)S(1)}, f32[16,512]{1,0:T(8,128)S(1)}, u32[]{:S(2)}, u32[]{:S(2)}) collective-permute-start(f32[16,512]{1,0:T(8,128)S(1)} %add.34.refs_0_), channel_id=1, source_target_pairs={{0,24},{4,28},{8,16},{12,20},{16,8},{20,12},{24,0},{28,4},{1,25},{... | collective-permute-start | bytes 98312 | tf_op jit(solution)/shard_map/ppermute | solution.py:27
  35.4 3.3 %collective-permute-done.8.refs_3_ = f32[16,512]{1,0:T(8,128)S(1)} collective-permute-done((f32[16,512]{1,0:T(8,128)S(1)}, f32[16,512]{1,0:T(8,128)S(1)}, u32[]{:S(2)}, u32[]{:S(2)}) %collective-permute-start.8) | collective-permute-done | bytes 32800 | tf_op jit(solution)/shard_map/ppermute | solution.py:27
  38.7 6.5 %shard_map.124 = (f32[16,2560]{1,0:T(8,128)S(1)}, f32[16,2560]{1,0:T(8,128)S(1)}, f32[24,512]{1,0:T(8,128)S(1)}, f32[16,512]{1,0:T(8,128)}, f32[16,512]{1,0:T(8,128)S(1)}, /*index=5*/f32[16,512]{1,0:T(8,128)S(1)}) custom-call(f32[16,512]{1,0:T(8,128)S(1)} %add.34.refs_0_, f32[16,512]{1,0:T(8,128)S(1)} %collective-permute-done.6.refs_1_, ...), custom_call_target="tpu_custom_call" | custom-call | tf_op jit(solution)/shard_map/pallas_call | solution.py:370
  45.2 1.4 %collective-permute-done.9 = f32[16,2560]{1,0:T(8,128)S(1)} collective-permute-done((f32[16,2560]{1,0:T(8,128)S(1)}, f32[16,2560]{1,0:T(8,128)S(1)}, u32[]{:S(2)}, u32[]{:S(2)}) %collective-permute-start.9) | collective-permute-done | bytes 163872 | tf_op jit(solution)/shard_map/ppermute | solution.py:27
  47.2 1.9 %collective-permute-start.14 = (f32[24,512]{1,0:T(8,128)S(1)}, f32[24,512]{1,0:T(8,128)S(1)}, u32[]{:S(2)}, u32[]{:S(2)}) collective-permute-start(f32[24,512]{1,0:T(8,128)S(1)} %get-tuple-element.49), channel_id=1, source_target_pairs={{0,4},{4,0},{8,12},{12,8},{16,20},{20,16},{24,28},{28,24},{1,5},{5... | collective-permute-start | bytes 147464 | tf_op jit(solution)/shard_map/ppermute | solution.py:27
  49.2 2.2 %collective-permute-done.14 = f32[24,512]{1,0:T(8,128)S(1)} collective-permute-done((f32[24,512]{1,0:T(8,128)S(1)}, f32[24,512]{1,0:T(8,128)S(1)}, u32[]{:S(2)}, u32[]{:S(2)}) %collective-permute-start.14) | collective-permute-done | bytes 49184 | tf_op jit(solution)/shard_map/ppermute | solution.py:27
  51.4 2.2 %collective-permute-start.16 = (f32[24,512]{1,0:T(8,128)S(1)}, f32[24,512]{1,0:T(8,128)S(1)}, u32[]{:S(2)}, u32[]{:S(2)}) collective-permute-start(f32[24,512]{1,0:T(8,128)S(1)} %add.36.refs_0_), channel_id=1, source_target_pairs={{0,16},{4,20},{8,24},{12,28},{16,0},{20,4},{24,8},{28,12},{1,17},{... | collective-permute-start | bytes 147464 | tf_op jit(solution)/shard_map/ppermute | solution.py:27
  53.6 2.2 %collective-permute-start.17 = (f32[24,512]{1,0:T(8,128)S(1)}, f32[24,512]{1,0:T(8,128)S(1)}, u32[]{:S(2)}, u32[]{:S(2)}) collective-permute-start(f32[24,512]{1,0:T(8,128)S(1)} %add.36.refs_0_), channel_id=1, source_target_pairs={{0,24},{4,28},{8,16},{12,20},{16,8},{20,12},{24,0},{28,4},{1,25},{... | collective-permute-start | bytes 147464 | tf_op jit(solution)/shard_map/ppermute | solution.py:27
  56.0 2.0 %collective-permute-start.11 = (f32[16,128]{1,0:T(8,128)S(1)}, f32[16,128]{1,0:T(8,128)S(1)}, u32[]{:S(2)}, u32[]{:S(2)}) collective-permute-start(f32[16,128]{1,0:T(8,128)S(1)} %get-tuple-element.43), channel_id=1, source_target_pairs={{0,4},{4,0},{8,12},{12,8},{16,20},{20,16},{24,28},{28,24},{1,5},{5... | collective-permute-start | bytes 24584 | tf_op jit(solution)/shard_map/ppermute | solution.py:38
  58.0 1.7 %collective-permute-done.11.near_ref = f32[16,128]{1,0:T(8,128)S(1)} collective-permute-done((f32[16,128]{1,0:T(8,128)S(1)}, f32[16,128]{1,0:T(8,128)S(1)}, u32[]{:S(2)}, u32[]{:S(2)}) %collective-permute-start.11) | collective-permute-done | bytes 8224 | tf_op jit(solution)/shard_map/ppermute | solution.py:38
  59.8 1.7 %collective-permute-start.12 = (f32[16,128]{1,0:T(8,128)S(1)}, f32[16,128]{1,0:T(8,128)S(1)}, u32[]{:S(2)}, u32[]{:S(2)}) collective-permute-start(f32[16,128]{1,0:T(8,128)S(1)} %get-tuple-element.44), channel_id=1, source_target_pairs={{0,28},{4,8},{8,4},{12,16},{16,12},{20,24},{24,20},{28,0},{1,29},{... | collective-permute-start | bytes 24584 | tf_op jit(solution)/shard_map/ppermute | solution.py:38
  61.5 4.6 %collective-permute-done.12.far_ref = f32[16,128]{1,0:T(8,128)S(1)} collective-permute-done((f32[16,128]{1,0:T(8,128)S(1)}, f32[16,128]{1,0:T(8,128)S(1)}, u32[]{:S(2)}, u32[]{:S(2)}) %collective-permute-start.12) | collective-permute-done | bytes 8224 | tf_op jit(solution)/shard_map/ppermute | solution.py:38
  67.5 1.5 %collective-permute-start.18 = (f32[8,128]{1,0:T(8,128)S(1)}, f32[8,128]{1,0:T(8,128)S(1)}, u32[]{:S(2)}, u32[]{:S(2)}) collective-permute-start(f32[8,128]{1,0:T(8,128)S(1)} %get-tuple-element.53), channel_id=1, source_target_pairs={{0,2},{1,3},{2,0},{3,1},{4,6},{5,7},{6,4},{7,5},{8,10},{9,11},{10,... | collective-permute-start | bytes 12296 | tf_op jit(solution)/shard_map/ppermute | solution.py:27
  69.0 1.3 %collective-permute-done.19 = f32[8,128]{1,0:T(8,128)S(1)} collective-permute-done((f32[8,128]{1,0:T(8,128)S(1)}, f32[8,128]{1,0:T(8,128)S(1)}, u32[]{:S(2)}, u32[]{:S(2)}) %collective-permute-start.19) | collective-permute-done | bytes 4128 | tf_op jit(solution)/shard_map/ppermute | solution.py:27
  70.3 1.4 %collective-permute-start.21 = (f32[8,128]{1,0:T(8,128)S(1)}, f32[8,128]{1,0:T(8,128)S(1)}, u32[]{:S(2)}, u32[]{:S(2)}) collective-permute-start(f32[8,128]{1,0:T(8,128)S(1)} %add.38), channel_id=1, source_target_pairs={{0,16},{4,20},{8,24},{12,28},{16,0},{20,4},{24,8},{28,12},{1,17},{... | collective-permute-start | bytes 12296 | tf_op jit(solution)/shard_map/ppermute | solution.py:27
  71.7 3.0 %collective-permute-start.22 = (f32[8,128]{1,0:T(8,128)S(1)}, f32[8,128]{1,0:T(8,128)S(1)}, u32[]{:S(2)}, u32[]{:S(2)}) collective-permute-start(f32[8,128]{1,0:T(8,128)S(1)} %add.38), channel_id=1, source_target_pairs={{0,24},{4,28},{8,16},{12,20},{16,8},{20,12},{24,0},{28,4},{1,25},{... | collective-permute-start | bytes 12296 | tf_op jit(solution)/shard_map/ppermute | solution.py:27
  74.9 2.3 %collective-permute-done.22 = f32[8,128]{1,0:T(8,128)S(1)} collective-permute-done((f32[8,128]{1,0:T(8,128)S(1)}, f32[8,128]{1,0:T(8,128)S(1)}, u32[]{:S(2)}, u32[]{:S(2)}) %collective-permute-start.22) | collective-permute-done | bytes 4128 | tf_op jit(solution)/shard_map/ppermute | solution.py:27
  (54 shorter events, 7.8 us)
Async XLA Ops:
  12.8 1.6 %collective-permute-start = (f32[16,2560]{1,0:T(8,128)S(1)}, f32[16,2560]{1,0:T(8,128)S(1)}, u32[]{:S(2)}, u32[]{:S(2)}) collective-permute-start(f32[16,2560]{1,0:T(8,128)S(1)} %get-tuple-element.31), channel_id=1, source_target_pairs={{0,1},{1,0},{2,3},{3,2},{4,5},{5,4},{6,7},{7,6},{8,9},{9,8},{10,11... | collective-permute-start | bytes 491528 | tf_op jit(solution)/shard_map/ppermute | solution.py:27
  14.5 11.6 %collective-permute-start.1 = (f32[16,2560]{1,0:T(8,128)S(1)}, f32[16,2560]{1,0:T(8,128)S(1)}, u32[]{:S(2)}, u32[]{:S(2)}) collective-permute-start(f32[16,2560]{1,0:T(8,128)S(1)} %add.33.own_ref), channel_id=1, source_target_pairs={{0,2},{1,3},{2,0},{3,1},{4,6},{5,7},{6,4},{7,5},{8,10},{9,11},{10,... | collective-permute-start | bytes 491528 | tf_op jit(solution)/shard_map/ppermute | solution.py:27
  17.6 5.8 %collective-permute-start.2 = (f32[16,128]{1,0:T(8,128)S(1)}, f32[16,128]{1,0:T(8,128)S(1)}, u32[]{:S(2)}, u32[]{:S(2)}) collective-permute-start(f32[16,128]{1,0:T(8,128)S(1)} %get-tuple-element.32), channel_id=1, source_target_pairs={{0,4},{4,0},{8,12},{12,8},{16,20},{20,16},{24,28},{28,24},{1,5},{5... | collective-permute-start | bytes 24584 | tf_op jit(solution)/shard_map/ppermute | solution.py:38
  19.2 6.3 %collective-permute-start.3 = (f32[16,128]{1,0:T(8,128)S(1)}, f32[16,128]{1,0:T(8,128)S(1)}, u32[]{:S(2)}, u32[]{:S(2)}) collective-permute-start(f32[16,128]{1,0:T(8,128)S(1)} %get-tuple-element.33), channel_id=1, source_target_pairs={{0,28},{4,8},{8,4},{12,16},{16,12},{20,24},{24,20},{28,0},{1,29},{... | collective-permute-start | bytes 24584 | tf_op jit(solution)/shard_map/ppermute | solution.py:38
  26.2 12.5 %collective-permute-start.4 = (f32[16,2560]{1,0:T(8,128)S(1)}, f32[16,2560]{1,0:T(8,128)S(1)}, u32[]{:S(2)}, u32[]{:S(2)}) collective-permute-start(f32[16,2560]{1,0:T(8,128)S(1)} %get-tuple-element.37.own_ref.refs_4_), channel_id=1, source_target_pairs={{0,1},{1,0},{2,3},{3,2},{4,5},{5,4},{6,7},{7,6},{8,9},{9,8},{10,11... | collective-permute-start | bytes 491528 | tf_op jit(solution)/shard_map/ppermute | solution.py:27
  26.2 4.0 %collective-permute-start.5 = (f32[16,512]{1,0:T(8,128)S(1)}, f32[16,512]{1,0:T(8,128)S(1)}, u32[]{:S(2)}, u32[]{:S(2)}) collective-permute-start(f32[16,512]{1,0:T(8,128)S(1)} %get-tuple-element.38), channel_id=1, source_target_pairs={{0,4},{4,0},{8,12},{12,8},{16,20},{20,16},{24,28},{28,24},{1,5},{5... | collective-permute-start | bytes 98312 | tf_op jit(solution)/shard_map/ppermute | solution.py:27
  30.2 5.0 %collective-permute-start.6 = (f32[16,512]{1,0:T(8,128)S(1)}, f32[16,512]{1,0:T(8,128)S(1)}, u32[]{:S(2)}, u32[]{:S(2)}) collective-permute-start(f32[16,512]{1,0:T(8,128)S(1)} %add.34.refs_0_), channel_id=1, source_target_pairs={{0,8},{4,12},{8,0},{12,4},{16,24},{20,28},{24,16},{28,20},{1,9},{5... | collective-permute-start | bytes 98312 | tf_op jit(solution)/shard_map/ppermute | solution.py:27
  30.2 5.2 %collective-permute-start.7 = (f32[16,512]{1,0:T(8,128)S(1)}, f32[16,512]{1,0:T(8,128)S(1)}, u32[]{:S(2)}, u32[]{:S(2)}) collective-permute-start(f32[16,512]{1,0:T(8,128)S(1)} %add.34.refs_0_), channel_id=1, source_target_pairs={{0,16},{4,20},{8,24},{12,28},{16,0},{20,4},{24,8},{28,12},{1,17},{... | collective-permute-start | bytes 98312 | tf_op jit(solution)/shard_map/ppermute | solution.py:27
  33.0 5.7 %collective-permute-start.8 = (f32[16,512]{1,0:T(8,128)S(1)}, f32[16,512]{1,0:T(8,128)S(1)}, u32[]{:S(2)}, u32[]{:S(2)}) collective-permute-start(f32[16,512]{1,0:T(8,128)S(1)} %add.34.refs_0_), channel_id=1, source_target_pairs={{0,24},{4,28},{8,16},{12,20},{16,8},{20,12},{24,0},{28,4},{1,25},{... | collective-permute-start | bytes 98312 | tf_op jit(solution)/shard_map/ppermute | solution.py:27
  45.2 1.4 %collective-permute-start.9 = (f32[16,2560]{1,0:T(8,128)S(1)}, f32[16,2560]{1,0:T(8,128)S(1)}, u32[]{:S(2)}, u32[]{:S(2)}) collective-permute-start(f32[16,2560]{1,0:T(8,128)S(1)} %get-tuple-element.41), channel_id=1, source_target_pairs={{0,1},{1,0},{2,3},{3,2},{4,5},{5,4},{6,7},{7,6},{8,9},{9,8},{10,11... | collective-permute-start | bytes 491528 | tf_op jit(solution)/shard_map/ppermute | solution.py:27
  46.6 20.0 %collective-permute-start.10 = (f32[16,2560]{1,0:T(8,128)S(1)}, f32[16,2560]{1,0:T(8,128)S(1)}, u32[]{:S(2)}, u32[]{:S(2)}) collective-permute-start(f32[16,2560]{1,0:T(8,128)S(1)} %add.35.own_ref), channel_id=1, source_target_pairs={{0,2},{1,3},{2,0},{3,1},{4,6},{5,7},{6,4},{7,5},{8,10},{9,11},{10,... | collective-permute-start | bytes 491528 | tf_op jit(solution)/shard_map/ppermute | solution.py:27
  47.2 4.1 %collective-permute-start.14 = (f32[24,512]{1,0:T(8,128)S(1)}, f32[24,512]{1,0:T(8,128)S(1)}, u32[]{:S(2)}, u32[]{:S(2)}) collective-permute-start(f32[24,512]{1,0:T(8,128)S(1)} %get-tuple-element.49), channel_id=1, source_target_pairs={{0,4},{4,0},{8,12},{12,8},{16,20},{20,16},{24,28},{28,24},{1,5},{5... | collective-permute-start | bytes 147464 | tf_op jit(solution)/shard_map/ppermute | solution.py:27
  51.3 15.5 %collective-permute-start.15 = (f32[24,512]{1,0:T(8,128)S(1)}, f32[24,512]{1,0:T(8,128)S(1)}, u32[]{:S(2)}, u32[]{:S(2)}) collective-permute-start(f32[24,512]{1,0:T(8,128)S(1)} %add.36.refs_0_), channel_id=1, source_target_pairs={{0,8},{4,12},{8,0},{12,4},{16,24},{20,28},{24,16},{28,20},{1,9},{5... | collective-permute-start | bytes 147464 | tf_op jit(solution)/shard_map/ppermute | solution.py:27
  51.4 15.5 %collective-permute-start.16 = (f32[24,512]{1,0:T(8,128)S(1)}, f32[24,512]{1,0:T(8,128)S(1)}, u32[]{:S(2)}, u32[]{:S(2)}) collective-permute-start(f32[24,512]{1,0:T(8,128)S(1)} %add.36.refs_0_), channel_id=1, source_target_pairs={{0,16},{4,20},{8,24},{12,28},{16,0},{20,4},{24,8},{28,12},{1,17},{... | collective-permute-start | bytes 147464 | tf_op jit(solution)/shard_map/ppermute | solution.py:27
  53.6 13.3 %collective-permute-start.17 = (f32[24,512]{1,0:T(8,128)S(1)}, f32[24,512]{1,0:T(8,128)S(1)}, u32[]{:S(2)}, u32[]{:S(2)}) collective-permute-start(f32[24,512]{1,0:T(8,128)S(1)} %add.36.refs_0_), channel_id=1, source_target_pairs={{0,24},{4,28},{8,16},{12,20},{16,8},{20,12},{24,0},{28,4},{1,25},{... | collective-permute-start | bytes 147464 | tf_op jit(solution)/shard_map/ppermute | solution.py:27
  56.0 3.7 %collective-permute-start.11 = (f32[16,128]{1,0:T(8,128)S(1)}, f32[16,128]{1,0:T(8,128)S(1)}, u32[]{:S(2)}, u32[]{:S(2)}) collective-permute-start(f32[16,128]{1,0:T(8,128)S(1)} %get-tuple-element.43), channel_id=1, source_target_pairs={{0,4},{4,0},{8,12},{12,8},{16,20},{20,16},{24,28},{28,24},{1,5},{5... | collective-permute-start | bytes 24584 | tf_op jit(solution)/shard_map/ppermute | solution.py:38
  59.8 6.3 %collective-permute-start.12 = (f32[16,128]{1,0:T(8,128)S(1)}, f32[16,128]{1,0:T(8,128)S(1)}, u32[]{:S(2)}, u32[]{:S(2)}) collective-permute-start(f32[16,128]{1,0:T(8,128)S(1)} %get-tuple-element.44), channel_id=1, source_target_pairs={{0,28},{4,8},{8,4},{12,16},{16,12},{20,24},{24,20},{28,0},{1,29},{... | collective-permute-start | bytes 24584 | tf_op jit(solution)/shard_map/ppermute | solution.py:38
  66.7 3.7 %collective-permute-start.19 = (f32[8,128]{1,0:T(8,128)S(1)}, f32[8,128]{1,0:T(8,128)S(1)}, u32[]{:S(2)}, u32[]{:S(2)}) collective-permute-start(f32[8,128]{1,0:T(8,128)S(1)} %get-tuple-element.54), channel_id=1, source_target_pairs={{0,4},{4,0},{8,12},{12,8},{16,20},{20,16},{24,28},{28,24},{1,5},{5... | collective-permute-start | bytes 12296 | tf_op jit(solution)/shard_map/ppermute | solution.py:27
  67.5 7.2 %collective-permute-start.18 = (f32[8,128]{1,0:T(8,128)S(1)}, f32[8,128]{1,0:T(8,128)S(1)}, u32[]{:S(2)}, u32[]{:S(2)}) collective-permute-start(f32[8,128]{1,0:T(8,128)S(1)} %get-tuple-element.53), channel_id=1, source_target_pairs={{0,2},{1,3},{2,0},{3,1},{4,6},{5,7},{6,4},{7,5},{8,10},{9,11},{10,... | collective-permute-start | bytes 12296 | tf_op jit(solution)/shard_map/ppermute | solution.py:27
  70.3 4.4 %collective-permute-start.20 = (f32[8,128]{1,0:T(8,128)S(1)}, f32[8,128]{1,0:T(8,128)S(1)}, u32[]{:S(2)}, u32[]{:S(2)}) collective-permute-start(f32[8,128]{1,0:T(8,128)S(1)} %add.38), channel_id=1, source_target_pairs={{0,8},{4,12},{8,0},{12,4},{16,24},{20,28},{24,16},{28,20},{1,9},{5... | collective-permute-start | bytes 12296 | tf_op jit(solution)/shard_map/ppermute | solution.py:27
  70.3 4.5 %collective-permute-start.21 = (f32[8,128]{1,0:T(8,128)S(1)}, f32[8,128]{1,0:T(8,128)S(1)}, u32[]{:S(2)}, u32[]{:S(2)}) collective-permute-start(f32[8,128]{1,0:T(8,128)S(1)} %add.38), channel_id=1, source_target_pairs={{0,16},{4,20},{8,24},{12,28},{16,0},{20,4},{24,8},{28,12},{1,17},{... | collective-permute-start | bytes 12296 | tf_op jit(solution)/shard_map/ppermute | solution.py:27
  71.7 5.4 %collective-permute-start.22 = (f32[8,128]{1,0:T(8,128)S(1)}, f32[8,128]{1,0:T(8,128)S(1)}, u32[]{:S(2)}, u32[]{:S(2)}) collective-permute-start(f32[8,128]{1,0:T(8,128)S(1)} %add.38), channel_id=1, source_target_pairs={{0,24},{4,28},{8,16},{12,20},{16,8},{20,12},{24,0},{28,4},{1,25},{... | collective-permute-start | bytes 12296 | tf_op jit(solution)/shard_map/ppermute | solution.py:27
  74.7 4.8 %collective-permute-start.13 = (f32[16,2560]{1,0:T(8,128)S(1)}, f32[16,2560]{1,0:T(8,128)S(1)}, u32[]{:S(2)}, u32[]{:S(2)}) collective-permute-start(f32[16,2560]{1,0:T(8,128)S(1)} %get-tuple-element.47.own_ref), channel_id=1, source_target_pairs={{0,1},{1,0},{2,3},{3,2},{4,5},{5,4},{6,7},{7,6},{8,9},{9,8},{10,11... | collective-permute-start | bytes 491528 | tf_op jit(solution)/shard_map/ppermute | solution.py:27
  77.1 1.2 %collective-permute-start.23 = (f32[8,128]{1,0:T(8,128)S(1)}, f32[8,128]{1,0:T(8,128)S(1)}, u32[]{:S(2)}, u32[]{:S(2)}) collective-permute-start(f32[8,128]{1,0:T(8,128)S(1)} %add_add_fusion), channel_id=1, source_target_pairs={{0,1},{1,0},{2,3},{3,2},{4,5},{5,4},{6,7},{7,6},{8,9},{9,8},{10,11... | collective-permute-start | bytes 12296 | tf_op jit(solution)/shard_map/ppermute | solution.py:27
  (5 other events, 142.6 us)

commit v2 on v1

--- a/solution.py
+++ b/solution.py
@@ -35,7 +35,8 @@
 
 def paired(block, axis, first):
     n = lax.axis_size(axis)
-    return lax.ppermute(block, axis, [(i, (i + 1 if (i - first) % 2 == 0 else i - 1) % n) for i in range(n)])
+    route = [(i, i + 1 if (i - first) % 2 == 0 else i - 1) for i in range(n)]
+    return lax.ppermute(block, axis, [(i, j) for i, j in route if 0 <= j < n])
 
 
 def mask_groups(n):
@@ -59,13 +60,12 @@
     return terms
 
 
-def call(kernel, in_specs, outs, scratch=(), limit=4, held=()):
+def call(kernel, in_specs, outs, scratch=(), limit=4, packed=()):
     return pl.pallas_call(
         kernel,
         in_specs=in_specs,
-        out_specs=[VMEM] * (len(outs) + len(held)),
-        out_shape=[jax.ShapeDtypeStruct(s, f32) for s in outs]
-        + [jax.ShapeDtypeStruct(s, jnp.int32) for s in held],
+        out_specs=[VMEM] * len(outs),
+        out_shape=[jax.ShapeDtypeStruct(s, bf16 if i in packed else f32) for i, s in enumerate(outs)],
         scratch_shapes=list(scratch),
         compiler_params=pltpu.CompilerParams(vmem_limit_bytes=limit << 20),
     )
@@ -86,40 +86,53 @@
     return lax.dot_general(a, b, (((ca,), (cb,)), ((), ())), preferred_element_type=f32)
 
 
-def evaluate_block(zb, counts, ly, lg, k):
+def residuals(zb, c, ly):
     h, m, l = split3(zb)
     y = dotg(jnp.concatenate([h, h, h, m, m, l], 0), ly, 0, 0)
     i = jnp.exp2(y)
-    c = counts.astype(f32)
     r = c - i
     rh = r.astype(bf16)
-    rl = (r - rh.astype(f32)).astype(bf16)
+    return y, i, rh, (r - rh.astype(f32)).astype(bf16), h, m
+
+
+def factor_terms(rh, rl, lg, k):
     a = dotg(lg, rh, 1, 1)
-    b = dotg(lg[:k], rl, 1, 1)
-    fac = a[:k] + a[k:] + b
-    a = dotg(jnp.concatenate([h, m], 0), rh, 1, 0)
-    b = dotg(h, rl, 1, 0)
-    load = a[:k] + a[k:] + b
-    return fac, load, c, y, i
+    return a[:k] + a[k:] + dotg(lg[k:], rl, 1, 1)
+
+
+def loading_terms(h, m, rh, rl, k):
+    a = dotg(jnp.concatenate([m, h], 0), rh, 1, 0)
+    return a[:k] + a[k:] + dotg(h, rl, 1, 0)
 
 
 def fill_loadings(lt, ly_ref, lg_ref):
     h, m, l = split3(lt * f32(LOG2E))
     ly_ref[...] = jnp.concatenate([h, m, l, h, m, h], 0)
     h, m, _ = split3(lt)
-    lg_ref[...] = jnp.concatenate([h, m], 0)
+    lg_ref[...] = jnp.concatenate([m, h], 0)
+
+
+def rows_to_8(x):
+    return jnp.sum(x.reshape(x.shape[0] // 8, 8, x.shape[1]), 0)
+
+
+DEPTH = 3
 
 
 def first_kernel(
-    k, half, sub, z_hbm, lt_hbm, cnt_ref, own_ref, oth_ref, load_ref, buf_ref, ly_ref, lg_ref, z_ref, lt_ref, sem, sems
+    k, half, sub, z_hbm, lt_hbm, cnt_ref, load_ref, lg_ref, held_ref, rh_ref, rl_ref, ly_ref, z_ref, lt_ref, buf_ref, sem, sems
 ):
     c = core()
     steps = half // sub
+    slots = DEPTH + 1
+
+    def place(i):
+        return pl.multiple_of(lax.rem((1 - i // steps) + c, 2) * half + (i % steps) * sub, sub)
 
     def copy(i):
-        rho = 1 - i // steps
-        at = pl.multiple_of(lax.rem(rho + c, 2) * half + (i % steps) * sub, sub)
-        return pltpu.make_async_copy(cnt_ref.at[0, pl.ds(at, sub)], buf_ref.at[pl.ds(i * sub, sub)], sem.at[i])
+        return pltpu.make_async_copy(
+            cnt_ref.at[0, pl.ds(place(i), sub)], buf_ref.at[pl.ds((i % slots) * sub, sub)], sem.at[i]
+        )
 
     small = [
         pltpu.make_async_copy(lt_hbm, lt_ref, sems.at[0]),
@@ -127,50 +140,70 @@
     ]
     for job in small:
         job.start()
-    for i in range(2 * steps):
+    for i in range(min(DEPTH, 2 * steps)):
         copy(i).start()
     small[0].wait()
     fill_loadings(lt_ref[...], ly_ref, lg_ref)
     small[1].wait()
-    ly, lg = ly_ref[...], lg_ref[...]
-    total = None
+    ly = ly_ref[...]
+    loads = []
     for i in range(2 * steps):
-        rho = 1 - i // steps
-        at = pl.multiple_of(lax.rem(rho + c, 2) * half + (i % steps) * sub, sub)
         copy(i).wait()
-        fac, load, _, _, _ = evaluate_block(z_ref[0, :, pl.ds(at, sub)], buf_ref[pl.ds(i * sub, sub), :], ly, lg, k)
-        (oth_ref if rho else own_ref)[:, pl.ds((i % steps) * sub, sub)] = fac
-        total = load if total is None else total + load
-    load_ref[...] = total
-
-
-def second_kernel(k, half, sub, n_terms, *refs):
+        if i + DEPTH < 2 * steps:
+            copy(i + DEPTH).start()
+        cf = buf_ref[pl.ds((i % slots) * sub, sub), :].astype(f32)
+        rows = pl.ds(i * sub, sub)
+        held_ref[rows, :] = cf
+        _, _, rh, rl, h, m = residuals(z_ref[0, :, pl.ds(place(i), sub)], cf, ly)
+        rh_ref[rows, :] = rh
+        rl_ref[rows, :] = rl
+        loads.append(loading_terms(h, m, rh, rl, k))
+    load_ref[...] = add(loads)
+
+
+def factor_kernel(k, half, sub, start, lg_ref, rh_ref, rl_ref, fac_ref):
+    lg = lg_ref[...]
+    for i in range(half // sub):
+        rows = pl.ds(start + i * sub, sub)
+        fac_ref[:, i * sub : (i + 1) * sub] = factor_terms(rh_ref[rows, :], rl_ref[rows, :], lg, k)
+
+
+def move_loadings_kernel(n_terms, *refs):
     terms = refs[:n_terms]
-    zown_ref, zoth_ref, lt_ref, lm_ref, sl_ref, cnt_ref = refs[n_terms : n_terms + 6]
-    own_ref, oth_ref, load_ref, out_ref, newl_ref, halfl_ref, ly_ref, lg_ref = refs[n_terms + 6 :]
-    steps = half // sub
+    lt_ref, lm_ref, sl_ref, out_ref, newl_ref, halfl_ref, ly_ref, lg_ref = refs[n_terms:]
     step = sl_ref[0]
-    grad = add([t[...] for t in terms]) - lt_ref[...]
-    halfl = lm_ref[...] + 0.5 * step * grad
+    halfl = lm_ref[...] + 0.5 * step * (add([t[...] for t in terms]) - lt_ref[...])
     newl = lt_ref[...] + step * halfl
     halfl_ref[...] = halfl
     newl_ref[...] = newl
     out_ref[...] = newl
     fill_loadings(newl, ly_ref, lg_ref)
+
+
+def second_kernel(k, half, sub, start, z_ref, ly_ref, lg_ref, cnt_ref, fac_ref, lik_ref, rh_ref, rl_ref):
     ly, lg = ly_ref[...], lg_ref[...]
-    total = None
-    lik = None
-    for i in range(2 * steps):
-        rho = 1 - i // steps
-        z_ref = zoth_ref if rho else zown_ref
-        here = pl.ds((i % steps) * sub, sub)
-        fac, load, cf, y, inten = evaluate_block(z_ref[:, here], cnt_ref[pl.ds(i * sub, sub), :], ly, lg, k)
-        (oth_ref if rho else own_ref)[:, here] = fac
-        total = load if total is None else total + load
-        term = jnp.sum((inten - (cf * f32(LN2)) * y).reshape(sub // 8, 8, y.shape[1]), 0)
-        lik = term if lik is None else lik + term
-    load_ref[:k, :] = total
-    load_ref[k:, :] = lik
+    likes, sums = [], []
+    for i in range(half // sub):
+        rows = pl.ds(i * sub, sub)
+        cf = cnt_ref[pl.ds(start + i * sub, sub), :]
+        y, inten, rh, rl, _, _ = residuals(z_ref[:, rows], cf, ly)
+        rh_ref[rows, :] = rh
+        rl_ref[rows, :] = rl
+        fac_ref[:, rows] = factor_terms(rh, rl, lg, k)
+        likes.append(rows_to_8(cf * y))
+        sums.append(rows_to_8(inten))
+    lik_ref[...] = add(sums) - f32(LN2) * add(likes)
+
+
+def loading_kernel(k, half, sub, zo_ref, rho_ref, rlo_ref, zw_ref, rhw_ref, rlw_ref, liko_ref, likw_ref, load_ref):
+    loads = []
+    for z_ref, rh_ref, rl_ref in ((zo_ref, rho_ref, rlo_ref), (zw_ref, rhw_ref, rlw_ref)):
+        for i in range(half // sub):
+            rows = pl.ds(i * sub, sub)
+            h, m, _ = split3(z_ref[:, rows])
+            loads.append(loading_terms(h, m, rh_ref[rows, :], rl_ref[rows, :], k))
+    load_ref[:k, :] = add(loads)
+    load_ref[k:, :] = liko_ref[...] + likw_ref[...]
 
 
 def lane(shape):
@@ -338,22 +371,27 @@
         terms = sum_terms(own + swap(oth, "sp", 1), "sp", chips)
         return terms[0], add(terms[1:])
 
-    loadings_scratch = [pltpu.VMEM((6 * k, species), bf16), pltpu.VMEM((2 * k, species), bf16)]
-    own, oth, load, held = call(
+    rates, grads = (6 * k, species), (2 * k, species)
+    load, lg, held, rh, rl = call(
         functools.partial(first_kernel, k, half, sub),
         [HBM, HBM, HBM],
-        [(k, half), (k, half), (k, species)],
-        loadings_scratch
-        + [
+        [(k, species), grads, (cells, species), (cells, species), (cells, species)],
+        [
+            pltpu.VMEM(rates, bf16),
             pltpu.VMEM((1, k, cells), f32),
             pltpu.VMEM((k, species), f32),
+            pltpu.VMEM(((DEPTH + 1) * sub, species), jnp.int32),
             pltpu.SemaphoreType.DMA((cells // sub,)),
             pltpu.SemaphoreType.DMA((2,)),
         ],
-        16,
-        [(cells, species)],
+        12,
+        (1, 3, 4),
     )(*[pltpu.with_memory_space_constraint(x, pltpu.HBM) for x in (factors, lt, counts)])
     load_terms = sum_terms(load, "site", site)
+    oth, own = [
+        call(functools.partial(factor_kernel, k, half, sub, start), [VMEM] * 3, [(k, half)])(lg, rh, rl)[0]
+        for start in (0, half)
+    ]
     own, other = share(own, oth)
 
     near, far = call(functools.partial(rims_kernel, k), [VMEM], [(k, LANES)] * 2)(factors)
@@ -367,13 +405,25 @@
     near, far = call(functools.partial(join_kernel, k), [VMEM] * 2, [(k, LANES)] * 2)(moved_own, moved_oth)
     (new_factors,) = call(functools.partial(pair_kernel, half), [VMEM] * 2, [(1, k, cells)])(moved_own, moved_oth)
 
-    own, oth, load, new_loadings, newl, halfl = call(
-        functools.partial(second_kernel, k, half, sub, len(load_terms)),
-        [VMEM] * (len(load_terms) + 4) + [SMEM, VMEM],
-        [(k, half), (k, half), (k + 8, species)] + [(k, species)] * 3,
-        loadings_scratch,
-        20,
-    )(*load_terms, moved_own, moved_oth, lt, lm, loading_step, held)
+    new_loadings, newl, halfl, ly, lg = call(
+        functools.partial(move_loadings_kernel, len(load_terms)),
+        [VMEM] * (len(load_terms) + 2) + [SMEM],
+        [(k, species)] * 3 + [rates, grads],
+        packed=(3, 4),
+    )(*load_terms, lt, lm, loading_step)
+    (oth, lik_oth, *parts_oth), (own, lik_own, *parts_own) = [
+        call(
+            functools.partial(second_kernel, k, half, sub, start),
+            [VMEM] * 4,
+            [(k, half), (8, species), (half, species), (half, species)],
+            limit=8,
+            packed=(2, 3),
+        )(z, ly, lg, held)
+        for start, z in ((0, moved_oth), (half, moved_own))
+    ]
+    (load,) = call(functools.partial(loading_kernel, k, half, sub), [VMEM] * 8, [(k + 8, species)])(
+        moved_oth, *parts_oth, moved_own, *parts_own, lik_oth, lik_own
+    )
     load_terms = sum_terms(load, "site", site)
     own, other = share(own, oth)
 

time: 81.6 us -> 77.8 us (0.953)
  waiting for transfers between devices: 24.5 us -> 19.3 us
  starting transfers between devices: 29.9 us -> 33.5 us
  Pallas kernels: 22.4 us -> 20.1 us
    ppermute x20, starting transfers between devices: 21 us -> 30.3 us  [swap(): lax.ppermute(block, axis, [(i, i ^ mask) for i in range(lax.axis_size(axi...]
    pallas_call x1, Pallas kernels: 12.2 us -> 6.09 us  [local(): call(functools.partial(first_kernel, k, half, sub), [HBM, HBM, HBM], [(k,...]
    ppermute x4, starting transfers between devices: 8.84 us -> 3.21 us  [paired(): return lax.ppermute(block, axis, [(i, j) for i, j in route if 0 <= j < n])]
    ppermute x4, waiting for transfers between devices: 8.49 us -> 4.22 us  [paired(): return lax.ppermute(block, axis, [(i, j) for i, j in route if 0 <= j < n])]
    pallas_call x1 -> x6, Pallas kernels: 6.51 us -> 10.3 us  [the longest x2 5.07 us: local(): call(functools.partial(second_kernel, k, half, sub, start), [VMEM] * 4, [...]
    ppermute x20, waiting for transfers between devices: 16 us -> 15.1 us  [swap(): lax.ppermute(block, axis, [(i, i ^ mask) for i in range(lax.axis_size(axi...]
  transfers between devices with their start and end apart: 24 -> 24, of which waited for: 13 -> 10; matrix products, arithmetic and copies ran while one was open for 1% -> 1% of each run, Pallas kernels for 4% -> 12%
where the time goes in v2:
time: 77.8 us; the launch traced here: 77.6 us
  starting transfers between devices  33.5 us (43%)
  Pallas kernels  20.1 us (26%)
  waiting for transfers between devices  19.3 us (25%)
  between operations  3.88 us (5%)
    ppermute x20, starting transfers between devices, swap(): lax.ppermute(block, axis, [(i, i ^ mask) for i in range(lax.axis_size(axi...  30.3 us
    ppermute x20, waiting for transfers between devices, swap(): lax.ppermute(block, axis, [(i, i ^ mask) for i in range(lax.axis_size(axi...  15.1 us
    pallas_call x1, Pallas kernels, local(): call(functools.partial(first_kernel, k, half, sub), [HBM, HBM, HBM], [(k,...  6.09 us
    pallas_call x2, Pallas kernels, local(): call(functools.partial(second_kernel, k, half, sub, start), [VMEM] * 4, [...  5.07 us
    ppermute x4, waiting for transfers between devices, paired(): return lax.ppermute(block, axis, [(i, j) for i, j in route if 0 <= j < n])  4.22 us
    ppermute x4, starting transfers between devices, paired(): return lax.ppermute(block, axis, [(i, j) for i, j in route if 0 <= j < n])  3.21 us
    pallas_call x2, Pallas kernels, local(): call(functools.partial(factor_kernel, k, half, sub, start), [VMEM] * 3, [...  2.99 us
    pallas_call x1, Pallas kernels, local(): call(functools.partial(loading_kernel, k, half, sub), [VMEM] * 8, [(k + 8...  1.57 us
  transfers between devices with their start and end apart: 24, of which 10 were waited for; matrix products, arithmetic and copies ran while one was open for 1% of the time, Pallas kernels for 12%

profile of v2, /device:TPU:0, one launch (start us, length us, event | category | flops | bytes accessed | tf_op | source)
XLA Modules:
  0.0 77.6 jit_solution(8599838294775211889)
XLA Ops:
  0.6 6.1 %shard_map.119 = (f32[16,512]{1,0:T(8,128)S(1)}, bf16[32,512]{1,0:T(8,128)(2,1)S(1)}, f32[5120,512]{1,0:T(8,128)S(1)}, bf16[5120,512]{1,0:T(8,128)(2,1)S(1)}, bf16[5120,512]{1,0:T(8,128)(2,1)S(1)}) custom-call(f32[1,16,5120]{2,1,0:T(8,128)} %z_ref.3, f32[16,512]{1,0:T(8,128)} %bitcast.5, s32[1,5120,512]{2,1,0:T(8,128)} %cnt_ref.1), custom_call_target="tpu_custom_call" | custom-call | tf_op jit(solution)/shard_map/pallas_call | solution.py:375
  6.7 1.5 %shard_map.121 = f32[16,2560]{1,0:T(8,128)S(1)} custom-call(bf16[32,512]{1,0:T(8,128)(2,1)S(1)} %get-tuple-element.38.lg_ref, bf16[5120,512]{1,0:T(8,128)(2,1)S(1)} %get-tuple-element.39.rh_ref, bf16[5120,512]{1,0:T(8,128)(2,1)S(1)} %get-tuple-element.40.rl_ref), custom_call_target="tpu_custom_call" | custom-call | tf_op jit(solution)/shard_map/pallas_call | solution.py:392
  8.8 1.5 %shard_map.120 = f32[16,2560]{1,0:T(8,128)S(1)} custom-call(bf16[32,512]{1,0:T(8,128)(2,1)S(1)} %get-tuple-element.38.lg_ref, bf16[5120,512]{1,0:T(8,128)(2,1)S(1)} %get-tuple-element.39.rh_ref, bf16[5120,512]{1,0:T(8,128)(2,1)S(1)} %get-tuple-element.40.rl_ref), custom_call_target="tpu_custom_call" | custom-call | tf_op jit(solution)/shard_map/pallas_call | solution.py:392
  10.4 2.6 %collective-permute-start.1 = (f32[16,2560]{1,0:T(8,128)S(1)}, f32[16,2560]{1,0:T(8,128)S(1)}, u32[]{:S(2)}, u32[]{:S(2)}) collective-permute-start(f32[16,2560]{1,0:T(8,128)S(1)} %add.33.own_ref), channel_id=1, source_target_pairs={{0,2},{1,3},{2,0},{3,1},{4,6},{5,7},{6,4},{7,5},{8,10},{9,11},{10,... | collective-permute-start | bytes 491528 | tf_op jit(solution)/shard_map/ppermute | solution.py:27
  13.2 1.6 %collective-permute-start.2 = (f32[16,128]{1,0:T(8,128)S(1)}, f32[16,128]{1,0:T(8,128)S(1)}, u32[]{:S(2)}, u32[]{:S(2)}) collective-permute-start(f32[16,128]{1,0:T(8,128)S(1)} %get-tuple-element.41), channel_id=1, source_target_pairs={{0,4},{4,0},{8,12},{12,8},{16,20},{20,16},{24,28},{28,24},{1,5},{5... | collective-permute-start | bytes 24584 | tf_op jit(solution)/shard_map/ppermute | solution.py:39
  14.7 0.8 %collective-permute-start.3 = (f32[16,128]{1,0:T(8,128)S(1)}, f32[16,128]{1,0:T(8,128)S(1)}, u32[]{:S(2)}, u32[]{:S(2)}) collective-permute-start(f32[16,128]{1,0:T(8,128)S(1)} %get-tuple-element.42), channel_id=1, source_target_pairs={{4,8},{8,4},{12,16},{16,12},{20,24},{24,20},{5,9},{9,5},{13,17},{1... | collective-permute-start | bytes 24584 | tf_op jit(solution)/shard_map/ppermute | solution.py:39
  17.9 4.6 %collective-permute-start.5 = (f32[16,512]{1,0:T(8,128)S(1)}, f32[16,512]{1,0:T(8,128)S(1)}, u32[]{:S(2)}, u32[]{:S(2)}) collective-permute-start(f32[16,512]{1,0:T(8,128)S(1)} %get-tuple-element.47), channel_id=1, source_target_pairs={{0,4},{4,0},{8,12},{12,8},{16,20},{20,16},{24,28},{28,24},{1,5},{5... | collective-permute-start | bytes 98312 | tf_op jit(solution)/shard_map/ppermute | solution.py:27
  22.5 2.0 %collective-permute-done.5 = f32[16,512]{1,0:T(8,128)S(1)} collective-permute-done((f32[16,512]{1,0:T(8,128)S(1)}, f32[16,512]{1,0:T(8,128)S(1)}, u32[]{:S(2)}, u32[]{:S(2)}) %collective-permute-start.5) | collective-permute-done | bytes 32800 | tf_op jit(solution)/shard_map/ppermute | solution.py:27
  24.5 3.0 %collective-permute-start.6 = (f32[16,512]{1,0:T(8,128)S(1)}, f32[16,512]{1,0:T(8,128)S(1)}, u32[]{:S(2)}, u32[]{:S(2)}) collective-permute-start(f32[16,512]{1,0:T(8,128)S(1)} %add.34.refs_0_), channel_id=1, source_target_pairs={{0,8},{4,12},{8,0},{12,4},{16,24},{20,28},{24,16},{28,20},{1,9},{5... | collective-permute-start | bytes 98312 | tf_op jit(solution)/shard_map/ppermute | solution.py:27
  27.5 2.6 %collective-permute-start.7 = (f32[16,512]{1,0:T(8,128)S(1)}, f32[16,512]{1,0:T(8,128)S(1)}, u32[]{:S(2)}, u32[]{:S(2)}) collective-permute-start(f32[16,512]{1,0:T(8,128)S(1)} %add.34.refs_0_), channel_id=1, source_target_pairs={{0,16},{4,20},{8,24},{12,28},{16,0},{20,4},{24,8},{28,12},{1,17},{... | collective-permute-start | bytes 98312 | tf_op jit(solution)/shard_map/ppermute | solution.py:27
  30.7 1.8 %collective-permute-done.7.refs_2_ = f32[16,512]{1,0:T(8,128)S(1)} collective-permute-done((f32[16,512]{1,0:T(8,128)S(1)}, f32[16,512]{1,0:T(8,128)S(1)}, u32[]{:S(2)}, u32[]{:S(2)}) %collective-permute-start.7) | collective-permute-done | bytes 32800 | tf_op jit(solution)/shard_map/ppermute | solution.py:27
  32.5 3.2 %collective-permute-done.8.refs_3_ = f32[16,512]{1,0:T(8,128)S(1)} collective-permute-done((f32[16,512]{1,0:T(8,128)S(1)}, f32[16,512]{1,0:T(8,128)S(1)}, u32[]{:S(2)}, u32[]{:S(2)}) %collective-permute-start.8) | collective-permute-done | bytes 32800 | tf_op jit(solution)/shard_map/ppermute | solution.py:27
  36.4 2.5 %shard_map.128 = (f32[16,2560]{1,0:T(8,128)S(1)}, f32[8,512]{1,0:T(8,128)S(1)}, bf16[2560,512]{1,0:T(8,128)(2,1)S(1)}, bf16[2560,512]{1,0:T(8,128)(2,1)S(1)}) custom-call(f32[16,2560]{1,0:T(8,128)S(1)} %collective-permute-done.4.oth_ref.z_ref.zo_ref, bf16[96,512]{1,0:T(8,128)(2,1)S(1)} %get-tuple-element.48.ly_ref, ...), custom_call_target="tpu_custom_call" | custom-call | tf_op jit(solution)/shard_map/pallas_call | solution.py:415
  38.9 2.5 %shard_map.127 = (f32[16,2560]{1,0:T(8,128)S(1)}, f32[8,512]{1,0:T(8,128)S(1)}, bf16[2560,512]{1,0:T(8,128)(2,1)S(1)}, bf16[2560,512]{1,0:T(8,128)(2,1)S(1)}) custom-call(f32[16,2560]{1,0:T(8,128)S(1)} %get-tuple-element.46.own_ref.z_ref.zw_ref, bf16[96,512]{1,0:T(8,128)(2,1)S(1)} %get-tuple-element.48.ly_ref, bf16[32,512]{1,0:T(8,128)(2,1)S(1)} %get-tuple-element.49.lg_ref, ...), custom_call_target="tpu_custom_call" | custom-call | tf_op jit(solution)/shard_map/pallas_call | solution.py:415
  42.2 1.6 %shard_map.133 = f32[24,512]{1,0:T(8,128)S(1)} custom-call(f32[16,2560]{1,0:T(8,128)S(1)} %collective-permute-done.4.oth_ref.z_ref.zo_ref, bf16[2560,512]{1,0:T(8,128)(2,1)S(1)} %get-tuple-element.60.rho_ref, bf16[2560,512]{1,0:T(8,128)(2,1)S(1)} %get-tuple-element.61.rlo_ref, f32[16,2560]{1,0:T(8,128)S(1)} %get-tuple-element.46.own_ref.z_ref.zw_ref, ...), custom_call_target="tpu_custom_call" | custom-call | tf_op jit(solution)/shard_map/pallas_call | solution.py:424
  43.8 4.0 %collective-permute-done.14 = f32[24,512]{1,0:T(8,128)S(1)} collective-permute-done((f32[24,512]{1,0:T(8,128)S(1)}, f32[24,512]{1,0:T(8,128)S(1)}, u32[]{:S(2)}, u32[]{:S(2)}) %collective-permute-start.14) | collective-permute-done | bytes 49184 | tf_op jit(solution)/shard_map/ppermute | solution.py:27
  47.9 0.9 %collective-permute-start.16 = (f32[24,512]{1,0:T(8,128)S(1)}, f32[24,512]{1,0:T(8,128)S(1)}, u32[]{:S(2)}, u32[]{:S(2)}) collective-permute-start(f32[24,512]{1,0:T(8,128)S(1)} %add.36.refs_0_), channel_id=1, source_target_pairs={{0,16},{4,20},{8,24},{12,28},{16,0},{20,4},{24,8},{28,12},{1,17},{... | collective-permute-start | bytes 147464 | tf_op jit(solution)/shard_map/ppermute | solution.py:27
  48.8 3.5 %collective-permute-start.17 = (f32[24,512]{1,0:T(8,128)S(1)}, f32[24,512]{1,0:T(8,128)S(1)}, u32[]{:S(2)}, u32[]{:S(2)}) collective-permute-start(f32[24,512]{1,0:T(8,128)S(1)} %add.36.refs_0_), channel_id=1, source_target_pairs={{0,24},{4,28},{8,16},{12,20},{16,8},{20,12},{24,0},{28,4},{1,25},{... | collective-permute-start | bytes 147464 | tf_op jit(solution)/shard_map/ppermute | solution.py:27
  52.7 3.6 %collective-permute-done.11.near_ref = f32[16,128]{1,0:T(8,128)S(1)} collective-permute-done((f32[16,128]{1,0:T(8,128)S(1)}, f32[16,128]{1,0:T(8,128)S(1)}, u32[]{:S(2)}, u32[]{:S(2)}) %collective-permute-start.11) | collective-permute-done | bytes 8224 | tf_op jit(solution)/shard_map/ppermute | solution.py:39
  57.5 5.9 %collective-permute-start.19 = (f32[8,128]{1,0:T(8,128)S(1)}, f32[8,128]{1,0:T(8,128)S(1)}, u32[]{:S(2)}, u32[]{:S(2)}) collective-permute-start(f32[8,128]{1,0:T(8,128)S(1)} %get-tuple-element.70), channel_id=1, source_target_pairs={{0,4},{4,0},{8,12},{12,8},{16,20},{20,16},{24,28},{28,24},{1,5},{5... | collective-permute-start | bytes 12296 | tf_op jit(solution)/shard_map/ppermute | solution.py:27
  64.1 1.5 %collective-permute-start.18 = (f32[8,128]{1,0:T(8,128)S(1)}, f32[8,128]{1,0:T(8,128)S(1)}, u32[]{:S(2)}, u32[]{:S(2)}) collective-permute-start(f32[8,128]{1,0:T(8,128)S(1)} %get-tuple-element.69), channel_id=1, source_target_pairs={{0,2},{1,3},{2,0},{3,1},{4,6},{5,7},{6,4},{7,5},{8,10},{9,11},{10,... | collective-permute-start | bytes 12296 | tf_op jit(solution)/shard_map/ppermute | solution.py:27
  66.1 1.7 %collective-permute-start.21 = (f32[8,128]{1,0:T(8,128)S(1)}, f32[8,128]{1,0:T(8,128)S(1)}, u32[]{:S(2)}, u32[]{:S(2)}) collective-permute-start(f32[8,128]{1,0:T(8,128)S(1)} %add.38), channel_id=1, source_target_pairs={{0,16},{4,20},{8,24},{12,28},{16,0},{20,4},{24,8},{28,12},{1,17},{... | collective-permute-start | bytes 12296 | tf_op jit(solution)/shard_map/ppermute | solution.py:27
  67.9 2.1 %collective-permute-start.22 = (f32[8,128]{1,0:T(8,128)S(1)}, f32[8,128]{1,0:T(8,128)S(1)}, u32[]{:S(2)}, u32[]{:S(2)}) collective-permute-start(f32[8,128]{1,0:T(8,128)S(1)} %add.38), channel_id=1, source_target_pairs={{0,24},{4,28},{8,16},{12,20},{16,8},{20,12},{24,0},{28,4},{1,25},{... | collective-permute-start | bytes 12296 | tf_op jit(solution)/shard_map/ppermute | solution.py:27
  70.6 2.6 %collective-permute-done.22 = f32[8,128]{1,0:T(8,128)S(1)} collective-permute-done((f32[8,128]{1,0:T(8,128)S(1)}, f32[8,128]{1,0:T(8,128)S(1)}, u32[]{:S(2)}, u32[]{:S(2)}) %collective-permute-start.22) | collective-permute-done | bytes 4128 | tf_op jit(solution)/shard_map/ppermute | solution.py:27
  (59 shorter events, 10.1 us)
Async XLA Ops:
  8.3 2.1 %collective-permute-start = (f32[16,2560]{1,0:T(8,128)S(1)}, f32[16,2560]{1,0:T(8,128)S(1)}, u32[]{:S(2)}, u32[]{:S(2)}) collective-permute-start(f32[16,2560]{1,0:T(8,128)S(1)} %shard_map.121), channel_id=1, source_target_pairs={{0,1},{1,0},{2,3},{3,2},{4,5},{5,4},{6,7},{7,6},{8,9},{9,8},{10,11... | collective-permute-start | bytes 491528 | tf_op jit(solution)/shard_map/ppermute | solution.py:27
  10.4 7.4 %collective-permute-start.1 = (f32[16,2560]{1,0:T(8,128)S(1)}, f32[16,2560]{1,0:T(8,128)S(1)}, u32[]{:S(2)}, u32[]{:S(2)}) collective-permute-start(f32[16,2560]{1,0:T(8,128)S(1)} %add.33.own_ref), channel_id=1, source_target_pairs={{0,2},{1,3},{2,0},{3,1},{4,6},{5,7},{6,4},{7,5},{8,10},{9,11},{10,... | collective-permute-start | bytes 491528 | tf_op jit(solution)/shard_map/ppermute | solution.py:27
  13.2 3.7 %collective-permute-start.2 = (f32[16,128]{1,0:T(8,128)S(1)}, f32[16,128]{1,0:T(8,128)S(1)}, u32[]{:S(2)}, u32[]{:S(2)}) collective-permute-start(f32[16,128]{1,0:T(8,128)S(1)} %get-tuple-element.41), channel_id=1, source_target_pairs={{0,4},{4,0},{8,12},{12,8},{16,20},{20,16},{24,28},{28,24},{1,5},{5... | collective-permute-start | bytes 24584 | tf_op jit(solution)/shard_map/ppermute | solution.py:39
  14.7 2.2 %collective-permute-start.3 = (f32[16,128]{1,0:T(8,128)S(1)}, f32[16,128]{1,0:T(8,128)S(1)}, u32[]{:S(2)}, u32[]{:S(2)}) collective-permute-start(f32[16,128]{1,0:T(8,128)S(1)} %get-tuple-element.42), channel_id=1, source_target_pairs={{4,8},{8,4},{12,16},{16,12},{20,24},{24,20},{5,9},{9,5},{13,17},{1... | collective-permute-start | bytes 24584 | tf_op jit(solution)/shard_map/ppermute | solution.py:39
  17.8 18.6 %collective-permute-start.4 = (f32[16,2560]{1,0:T(8,128)S(1)}, f32[16,2560]{1,0:T(8,128)S(1)}, u32[]{:S(2)}, u32[]{:S(2)}) collective-permute-start(f32[16,2560]{1,0:T(8,128)S(1)} %get-tuple-element.46.own_ref.z_ref.zw_ref), channel_id=1, source_target_pairs={{0,1},{1,0},{2,3},{3,2},{4,5},{5,4},{6,7},{7,6},{8,9},{9,8},{10,11... | collective-permute-start | bytes 491528 | tf_op jit(solution)/shard_map/ppermute | solution.py:27
  17.9 6.6 %collective-permute-start.5 = (f32[16,512]{1,0:T(8,128)S(1)}, f32[16,512]{1,0:T(8,128)S(1)}, u32[]{:S(2)}, u32[]{:S(2)}) collective-permute-start(f32[16,512]{1,0:T(8,128)S(1)} %get-tuple-element.47), channel_id=1, source_target_pairs={{0,4},{4,0},{8,12},{12,8},{16,20},{20,16},{24,28},{28,24},{1,5},{5... | collective-permute-start | bytes 98312 | tf_op jit(solution)/shard_map/ppermute | solution.py:27
  24.5 6.2 %collective-permute-start.6 = (f32[16,512]{1,0:T(8,128)S(1)}, f32[16,512]{1,0:T(8,128)S(1)}, u32[]{:S(2)}, u32[]{:S(2)}) collective-permute-start(f32[16,512]{1,0:T(8,128)S(1)} %add.34.refs_0_), channel_id=1, source_target_pairs={{0,8},{4,12},{8,0},{12,4},{16,24},{20,28},{24,16},{28,20},{1,9},{5... | collective-permute-start | bytes 98312 | tf_op jit(solution)/shard_map/ppermute | solution.py:27
  27.5 5.0 %collective-permute-start.7 = (f32[16,512]{1,0:T(8,128)S(1)}, f32[16,512]{1,0:T(8,128)S(1)}, u32[]{:S(2)}, u32[]{:S(2)}) collective-permute-start(f32[16,512]{1,0:T(8,128)S(1)} %add.34.refs_0_), channel_id=1, source_target_pairs={{0,16},{4,20},{8,24},{12,28},{16,0},{20,4},{24,8},{28,12},{1,17},{... | collective-permute-start | bytes 98312 | tf_op jit(solution)/shard_map/ppermute | solution.py:27
  30.1 5.7 %collective-permute-start.8 = (f32[16,512]{1,0:T(8,128)S(1)}, f32[16,512]{1,0:T(8,128)S(1)}, u32[]{:S(2)}, u32[]{:S(2)}) collective-permute-start(f32[16,512]{1,0:T(8,128)S(1)} %add.34.refs_0_), channel_id=1, source_target_pairs={{0,24},{4,28},{8,16},{12,20},{16,8},{20,12},{24,0},{28,4},{1,25},{... | collective-permute-start | bytes 98312 | tf_op jit(solution)/shard_map/ppermute | solution.py:27
  38.9 2.6 %collective-permute-start.9 = (f32[16,2560]{1,0:T(8,128)S(1)}, f32[16,2560]{1,0:T(8,128)S(1)}, u32[]{:S(2)}, u32[]{:S(2)}) collective-permute-start(f32[16,2560]{1,0:T(8,128)S(1)} %get-tuple-element.52), channel_id=1, source_target_pairs={{0,1},{1,0},{2,3},{3,2},{4,5},{5,4},{6,7},{7,6},{8,9},{9,8},{10,11... | collective-permute-start | bytes 491528 | tf_op jit(solution)/shard_map/ppermute | solution.py:27
  41.5 15.9 %collective-permute-start.10 = (f32[16,2560]{1,0:T(8,128)S(1)}, f32[16,2560]{1,0:T(8,128)S(1)}, u32[]{:S(2)}, u32[]{:S(2)}) collective-permute-start(f32[16,2560]{1,0:T(8,128)S(1)} %add.35.own_ref), channel_id=1, source_target_pairs={{0,2},{1,3},{2,0},{3,1},{4,6},{5,7},{6,4},{7,5},{8,10},{9,11},{10,... | collective-permute-start | bytes 491528 | tf_op jit(solution)/shard_map/ppermute | solution.py:27
  43.7 4.1 %collective-permute-start.14 = (f32[24,512]{1,0:T(8,128)S(1)}, f32[24,512]{1,0:T(8,128)S(1)}, u32[]{:S(2)}, u32[]{:S(2)}) collective-permute-start(f32[24,512]{1,0:T(8,128)S(1)} %shard_map.133), channel_id=1, source_target_pairs={{0,4},{4,0},{8,12},{12,8},{16,20},{20,16},{24,28},{28,24},{1,5},{5... | collective-permute-start | bytes 147464 | tf_op jit(solution)/shard_map/ppermute | solution.py:27
  47.8 15.6 %collective-permute-start.15 = (f32[24,512]{1,0:T(8,128)S(1)}, f32[24,512]{1,0:T(8,128)S(1)}, u32[]{:S(2)}, u32[]{:S(2)}) collective-permute-start(f32[24,512]{1,0:T(8,128)S(1)} %add.36.refs_0_), channel_id=1, source_target_pairs={{0,8},{4,12},{8,0},{12,4},{16,24},{20,28},{24,16},{28,20},{1,9},{5... | collective-permute-start | bytes 147464 | tf_op jit(solution)/shard_map/ppermute | solution.py:27
  47.9 15.5 %collective-permute-start.16 = (f32[24,512]{1,0:T(8,128)S(1)}, f32[24,512]{1,0:T(8,128)S(1)}, u32[]{:S(2)}, u32[]{:S(2)}) collective-permute-start(f32[24,512]{1,0:T(8,128)S(1)} %add.36.refs_0_), channel_id=1, source_target_pairs={{0,16},{4,20},{8,24},{12,28},{16,0},{20,4},{24,8},{28,12},{1,17},{... | collective-permute-start | bytes 147464 | tf_op jit(solution)/shard_map/ppermute | solution.py:27
  48.8 14.6 %collective-permute-start.17 = (f32[24,512]{1,0:T(8,128)S(1)}, f32[24,512]{1,0:T(8,128)S(1)}, u32[]{:S(2)}, u32[]{:S(2)}) collective-permute-start(f32[24,512]{1,0:T(8,128)S(1)} %add.36.refs_0_), channel_id=1, source_target_pairs={{0,24},{4,28},{8,16},{12,20},{16,8},{20,12},{24,0},{28,4},{1,25},{... | collective-permute-start | bytes 147464 | tf_op jit(solution)/shard_map/ppermute | solution.py:27
  52.5 3.7 %collective-permute-start.11 = (f32[16,128]{1,0:T(8,128)S(1)}, f32[16,128]{1,0:T(8,128)S(1)}, u32[]{:S(2)}, u32[]{:S(2)}) collective-permute-start(f32[16,128]{1,0:T(8,128)S(1)} %get-tuple-element.54), channel_id=1, source_target_pairs={{0,4},{4,0},{8,12},{12,8},{16,20},{20,16},{24,28},{28,24},{1,5},{5... | collective-permute-start | bytes 24584 | tf_op jit(solution)/shard_map/ppermute | solution.py:39
  56.2 0.7 collective-permute-start.12
  57.5 8.1 %collective-permute-start.19 = (f32[8,128]{1,0:T(8,128)S(1)}, f32[8,128]{1,0:T(8,128)S(1)}, u32[]{:S(2)}, u32[]{:S(2)}) collective-permute-start(f32[8,128]{1,0:T(8,128)S(1)} %get-tuple-element.70), channel_id=1, source_target_pairs={{0,4},{4,0},{8,12},{12,8},{16,20},{20,16},{24,28},{28,24},{1,5},{5... | collective-permute-start | bytes 12296 | tf_op jit(solution)/shard_map/ppermute | solution.py:27
  64.1 5.9 %collective-permute-start.18 = (f32[8,128]{1,0:T(8,128)S(1)}, f32[8,128]{1,0:T(8,128)S(1)}, u32[]{:S(2)}, u32[]{:S(2)}) collective-permute-start(f32[8,128]{1,0:T(8,128)S(1)} %get-tuple-element.69), channel_id=1, source_target_pairs={{0,2},{1,3},{2,0},{3,1},{4,6},{5,7},{6,4},{7,5},{8,10},{9,11},{10,... | collective-permute-start | bytes 12296 | tf_op jit(solution)/shard_map/ppermute | solution.py:27
  65.6 4.4 %collective-permute-start.20 = (f32[8,128]{1,0:T(8,128)S(1)}, f32[8,128]{1,0:T(8,128)S(1)}, u32[]{:S(2)}, u32[]{:S(2)}) collective-permute-start(f32[8,128]{1,0:T(8,128)S(1)} %add.38), channel_id=1, source_target_pairs={{0,8},{4,12},{8,0},{12,4},{16,24},{20,28},{24,16},{28,20},{1,9},{5... | collective-permute-start | bytes 12296 | tf_op jit(solution)/shard_map/ppermute | solution.py:27
  66.1 4.5 %collective-permute-start.21 = (f32[8,128]{1,0:T(8,128)S(1)}, f32[8,128]{1,0:T(8,128)S(1)}, u32[]{:S(2)}, u32[]{:S(2)}) collective-permute-start(f32[8,128]{1,0:T(8,128)S(1)} %add.38), channel_id=1, source_target_pairs={{0,16},{4,20},{8,24},{12,28},{16,0},{20,4},{24,8},{28,12},{1,17},{... | collective-permute-start | bytes 12296 | tf_op jit(solution)/shard_map/ppermute | solution.py:27
  67.9 5.4 %collective-permute-start.22 = (f32[8,128]{1,0:T(8,128)S(1)}, f32[8,128]{1,0:T(8,128)S(1)}, u32[]{:S(2)}, u32[]{:S(2)}) collective-permute-start(f32[8,128]{1,0:T(8,128)S(1)} %add.38), channel_id=1, source_target_pairs={{0,24},{4,28},{8,16},{12,20},{16,8},{20,12},{24,0},{28,4},{1,25},{... | collective-permute-start | bytes 12296 | tf_op jit(solution)/shard_map/ppermute | solution.py:27
  69.9 5.7 %collective-permute-start.13 = (f32[16,2560]{1,0:T(8,128)S(1)}, f32[16,2560]{1,0:T(8,128)S(1)}, u32[]{:S(2)}, u32[]{:S(2)}) collective-permute-start(f32[16,2560]{1,0:T(8,128)S(1)} %get-tuple-element.58.own_ref), channel_id=1, source_target_pairs={{0,1},{1,0},{2,3},{3,2},{4,5},{5,4},{6,7},{7,6},{8,9},{9,8},{10,11... | collective-permute-start | bytes 491528 | tf_op jit(solution)/shard_map/ppermute | solution.py:27
  73.3 1.2 %collective-permute-start.23 = (f32[8,128]{1,0:T(8,128)S(1)}, f32[8,128]{1,0:T(8,128)S(1)}, u32[]{:S(2)}, u32[]{:S(2)}) collective-permute-start(f32[8,128]{1,0:T(8,128)S(1)} %add_add_fusion), channel_id=1, source_target_pairs={{0,1},{1,0},{2,3},{3,2},{4,5},{5,4},{6,7},{7,6},{8,9},{9,8},{10,11... | collective-permute-start | bytes 12296 | tf_op jit(solution)/shard_map/ppermute | solution.py:27
  (5 other events, 77.2 us)

commit v3 on v2

--- a/solution.py
+++ b/solution.py
@@ -120,7 +120,8 @@
 
 
 def first_kernel(
-    k, half, sub, z_hbm, lt_hbm, cnt_ref, load_ref, lg_ref, held_ref, rh_ref, rl_ref, ly_ref, z_ref, lt_ref, buf_ref, sem, sems
+    k, half, sub, z_hbm, lt_hbm, cnt_ref, load_ref, oth_ref, lg_ref, held_ref, rh_ref, rl_ref,
+    ly_ref, z_ref, lt_ref, buf_ref, sem, sems
 ):
     c = core()
     steps = half // sub
@@ -145,7 +146,8 @@
     small[0].wait()
     fill_loadings(lt_ref[...], ly_ref, lg_ref)
     small[1].wait()
-    ly = ly_ref[...]
+    load_ref[:, -2 * LANES : -LANES], load_ref[:, -LANES:] = pack_rims(vregs_of(z_ref[0]), k)
+    ly, lg = ly_ref[...], lg_ref[...]
     loads = []
     for i in range(2 * steps):
         copy(i).wait()
@@ -155,16 +157,20 @@
         rows = pl.ds(i * sub, sub)
         held_ref[rows, :] = cf
         _, _, rh, rl, h, m = residuals(z_ref[0, :, pl.ds(place(i), sub)], cf, ly)
-        rh_ref[rows, :] = rh
-        rl_ref[rows, :] = rl
         loads.append(loading_terms(h, m, rh, rl, k))
-    load_ref[...] = add(loads)
-
-
-def factor_kernel(k, half, sub, start, lg_ref, rh_ref, rl_ref, fac_ref):
+        if i < steps:
+            oth_ref[:, i * sub : (i + 1) * sub] = factor_terms(rh, rl, lg, k)
+        else:
+            rows = pl.ds((i - steps) * sub, sub)
+            rh_ref[rows, :] = rh
+            rl_ref[rows, :] = rl
+    load_ref[:, : -2 * LANES] = add(loads)
+
+
+def factor_kernel(k, half, sub, lg_ref, rh_ref, rl_ref, fac_ref):
     lg = lg_ref[...]
     for i in range(half // sub):
-        rows = pl.ds(start + i * sub, sub)
+        rows = pl.ds(i * sub, sub)
         fac_ref[:, i * sub : (i + 1) * sub] = factor_terms(rh_ref[rows, :], rl_ref[rows, :], lg, k)
 
 
@@ -172,7 +178,7 @@
     terms = refs[:n_terms]
     lt_ref, lm_ref, sl_ref, out_ref, newl_ref, halfl_ref, ly_ref, lg_ref = refs[n_terms:]
     step = sl_ref[0]
-    halfl = lm_ref[...] + 0.5 * step * (add([t[...] for t in terms]) - lt_ref[...])
+    halfl = lm_ref[...] + 0.5 * step * (add([t[:, : lt_ref.shape[1]] for t in terms]) - lt_ref[...])
     newl = lt_ref[...] + step * halfl
     halfl_ref[...] = halfl
     newl_ref[...] = newl
@@ -202,8 +208,11 @@
             rows = pl.ds(i * sub, sub)
             h, m, _ = split3(z_ref[:, rows])
             loads.append(loading_terms(h, m, rh_ref[rows, :], rl_ref[rows, :], k))
-    load_ref[:k, :] = add(loads)
-    load_ref[k:, :] = liko_ref[...] + likw_ref[...]
+    load_ref[:k, : -2 * LANES] = add(loads)
+    load_ref[k:, : -2 * LANES] = liko_ref[...] + likw_ref[...]
+    load_ref[k:, -2 * LANES :] = jnp.zeros((load_ref.shape[0] - k, 2 * LANES), f32)
+    rims = pack_rims(in_order(zw_ref[...], zo_ref[...]), k)
+    load_ref[:k, -2 * LANES : -LANES], load_ref[:k, -LANES:] = rims
 
 
 def lane(shape):
@@ -242,9 +251,19 @@
     return out
 
 
-def sides(near, far):
+def sides(ride, refs, k):
     me, n = lax.axis_index("site"), lax.axis_size("site")
     even = lax.rem(me, 2) == 0
+    if ride:
+        pair, one, three = refs
+        near = jnp.where(even, pair[:k, -2 * LANES : -LANES], pair[:k, -LANES:])
+        row = me // 2
+        close = (lax.rem(row, 2) == 1) == even
+        first = jnp.where(close, one[:k, -2 * LANES : -LANES], three[:k, -2 * LANES : -LANES])
+        last = jnp.where(close, one[:k, -LANES:], three[:k, -LANES:])
+        far = jnp.where(even, last, first)
+    else:
+        near, far = refs[0][...], refs[1][...]
     left = jnp.where(me == 0, 0.0, jnp.where(even, far, near))
     right = jnp.where(me == n - 1, 0.0, jnp.where(even, near, far))
     return left, right
@@ -264,10 +283,21 @@
     near_ref[...], far_ref[...] = rims_of(vregs_of(z_ref[0]), k)
 
 
-def ahead_kernel(k, half, z_ref, mom_ref, near_ref, far_ref, upper_ref, lower_ref, gain_ref, sf_ref, a_ref, z_own_ref, s_ref):
+def stage_kernel(own_ref, got_ref, out_ref):
+    own, got = own_ref[...], got_ref[...]
+    out_ref[:, : -2 * LANES] = own[:, : -2 * LANES] + got[:, : -2 * LANES]
+    even = lax.rem(lax.axis_index("site"), 2) == 0
+    out_ref[:, -2 * LANES : -LANES] = jnp.where(even, own[:, -2 * LANES : -LANES], got[:, -2 * LANES : -LANES])
+    out_ref[:, -LANES:] = jnp.where(even, got[:, -LANES:], own[:, -LANES:])
+
+
+def ahead_kernel(
+    ride, k, half, z_ref, mom_ref, upper_ref, lower_ref, gain_ref, sf_ref, *refs
+):
+    *halo, a_ref, z_own_ref, s_ref = refs
     c = core()
     step = sf_ref[0]
-    left, right = sides(near_ref[...], far_ref[...])
+    left, right = sides(ride, halo, k)
     out = prior_of(vregs_of(z_ref[0]), 0, 2 * half // LANES, left, right, upper_ref[...], lower_ref[...], k)
     n = half // LANES
     gain = gain_ref[...] * (0.5 * step)
@@ -298,9 +328,10 @@
     near_ref[...], far_ref[...] = rims_of(in_order(own_ref[...], oth_ref[...]), k)
 
 
-def behind_kernel(k, half, own_ref, oth_ref, h_ref, near_ref, far_ref, upper_ref, lower_ref, gain_ref, s_ref, a_ref, e_ref):
+def behind_kernel(ride, k, half, own_ref, oth_ref, h_ref, upper_ref, lower_ref, gain_ref, s_ref, *refs):
+    *halo, a_ref, e_ref = refs
     c = core()
-    left, right = sides(near_ref[...], far_ref[...])
+    left, right = sides(ride, halo, k)
     z = in_order(own_ref[...], oth_ref[...])
     out = prior_of(z, 0, 2 * half // LANES, left, right, upper_ref[...], lower_ref[...], k)
     n = half // LANES
@@ -334,8 +365,8 @@
 def loading_end_kernel(k, n_terms, *refs):
     terms = refs[:n_terms]
     newl_ref, halfl_ref, sl_ref, end_ref, s_ref = refs[n_terms:]
-    total = add([t[...] for t in terms])
     newl = newl_ref[...]
+    total = add([t[:, : newl.shape[1]] for t in terms])
     end = halfl_ref[...] + (0.5 * sl_ref[0]) * (total[:k] - newl)
     end_ref[...] = end
     squares = 0.5 * (end * end + newl * newl)
@@ -356,26 +387,38 @@
     gain = jnp.broadcast_to(precision[:, None], (k, LANES))
     zero_rim = jnp.zeros((k, LANES), f32)
 
-    def rims_from(near, far, low, high):
-        near = paired(near, "site", 0)
-        far = paired(far, "site", 1)
-        if n_site > TGY:
-            lead = jnp.zeros((k, LANES - TY), f32)
-            upper = jnp.concatenate([lead, from_behind(high, "site", TGY)], 1)
-            lower = jnp.concatenate([from_behind(low, "site", -TGY), lead], 1)
-        else:
-            upper, lower = zero_rim, zero_rim
-        return near, far, upper, lower
+    ride = site == [[1], [2, 4, 6]]
+
+    def exchange(load):
+        if not ride:
+            return sum_terms(load, "site", site), ()
+        got = swap(load, "site", 1)
+        (total,) = call(stage_kernel, [VMEM] * 2, [load.shape])(load, got)
+        terms = [total] + [swap(total, "site", m) for m in site[1]]
+        return terms, (got, terms[1], terms[3])
+
+    def upright(low, high):
+        if n_site <= TGY:
+            return zero_rim, zero_rim
+        lead = jnp.zeros((k, LANES - TY), f32)
+        upper = jnp.concatenate([lead, from_behind(high, "site", TGY)], 1)
+        return upper, jnp.concatenate([from_behind(low, "site", -TGY), lead], 1)
+
+    def sideways(kernel, halo, *arrays):
+        if ride:
+            return halo
+        near, far = call(functools.partial(kernel, k), [VMEM] * len(arrays), [(k, LANES)] * 2)(*arrays)
+        return paired(near, "site", 0), paired(far, "site", 1)
 
     def share(own, oth):
         terms = sum_terms(own + swap(oth, "sp", 1), "sp", chips)
         return terms[0], add(terms[1:])
 
     rates, grads = (6 * k, species), (2 * k, species)
-    load, lg, held, rh, rl = call(
+    load, oth, lg, held, rh, rl = call(
         functools.partial(first_kernel, k, half, sub),
         [HBM, HBM, HBM],
-        [(k, species), grads, (cells, species), (cells, species), (cells, species)],
+        [(k, species + 2 * LANES), (k, half), grads, (cells, species), (half, species), (half, species)],
         [
             pltpu.VMEM(rates, bf16),
             pltpu.VMEM((1, k, cells), f32),
@@ -385,24 +428,23 @@
             pltpu.SemaphoreType.DMA((2,)),
         ],
         12,
-        (1, 3, 4),
+        (2, 4, 5),
     )(*[pltpu.with_memory_space_constraint(x, pltpu.HBM) for x in (factors, lt, counts)])
-    load_terms = sum_terms(load, "site", site)
-    oth, own = [
-        call(functools.partial(factor_kernel, k, half, sub, start), [VMEM] * 3, [(k, half)])(lg, rh, rl)[0]
-        for start in (0, half)
-    ]
+    load_terms, halo = exchange(load)
+    (own,) = call(functools.partial(factor_kernel, k, half, sub), [VMEM] * 3, [(k, half)])(lg, rh, rl)
     own, other = share(own, oth)
 
-    near, far = call(functools.partial(rims_kernel, k), [VMEM], [(k, LANES)] * 2)(factors)
+    halo = sideways(rims_kernel, halo, factors)
+    edges = upright(factors[0, :, :TY], factors[0, :, cells - TY :])
     a1, z_own, svec = call(
-        functools.partial(ahead_kernel, k, half), [VMEM] * 7 + [SMEM], [(k, half), (k, half), (k, LANES)]
-    )(factors, factor_momenta, *rims_from(near, far, factors[0, :, :TY], factors[0, :, cells - TY :]), gain, factor_step)
+        functools.partial(ahead_kernel, ride, k, half),
+        [VMEM] * 5 + [SMEM] + [VMEM] * len(halo),
+        [(k, half), (k, half), (k, LANES)],
+    )(factors, factor_momenta, *edges, gain, factor_step, *halo)
     half_own, moved_own = call(
         functools.partial(move_kernel, half), [VMEM] * 5, [(k, half)] * 2
     )(own, other, a1, z_own, svec)
     moved_oth = swap(moved_own, "sp", 1)
-    near, far = call(functools.partial(join_kernel, k), [VMEM] * 2, [(k, LANES)] * 2)(moved_own, moved_oth)
     (new_factors,) = call(functools.partial(pair_kernel, half), [VMEM] * 2, [(1, k, cells)])(moved_own, moved_oth)
 
     new_loadings, newl, halfl, ly, lg = call(
@@ -411,7 +453,7 @@
         [(k, species)] * 3 + [rates, grads],
         packed=(3, 4),
     )(*load_terms, lt, lm, loading_step)
-    (oth, lik_oth, *parts_oth), (own, lik_own, *parts_own) = [
+    (own, lik_own, *parts_own), (oth, lik_oth, *parts_oth) = [
         call(
             functools.partial(second_kernel, k, half, sub, start),
             [VMEM] * 4,
@@ -419,18 +461,19 @@
             limit=8,
             packed=(2, 3),
         )(z, ly, lg, held)
-        for start, z in ((0, moved_oth), (half, moved_own))
+        for start, z in ((half, moved_own), (0, moved_oth))
     ]
-    (load,) = call(functools.partial(loading_kernel, k, half, sub), [VMEM] * 8, [(k + 8, species)])(
+    (load,) = call(functools.partial(loading_kernel, k, half, sub), [VMEM] * 8, [(k + 8, species + 2 * LANES)])(
         moved_oth, *parts_oth, moved_own, *parts_own, lik_oth, lik_own
     )
-    load_terms = sum_terms(load, "site", site)
+    load_terms, halo = exchange(load)
     own, other = share(own, oth)
 
-    edges = new_factors[0, :, :TY], new_factors[0, :, cells - TY :]
+    halo = sideways(join_kernel, halo, moved_own, moved_oth)
+    edges = upright(new_factors[0, :, :TY], new_factors[0, :, cells - TY :])
     a2, prior_energy = call(
-        functools.partial(behind_kernel, k, half), [VMEM] * 9, [(k, half), (k, LANES)]
-    )(moved_own, moved_oth, half_own, *rims_from(near, far, *edges), gain, svec)
+        functools.partial(behind_kernel, ride, k, half), [VMEM] * (7 + len(halo)), [(k, half), (k, LANES)]
+    )(moved_own, moved_oth, half_own, *edges, gain, svec, *halo)
     end_own, b_part = call(
         functools.partial(end_kernel, k, half), [VMEM] * 5, [(k, half), (8, LANES)]
     )(own, other, a2, svec, prior_energy)

time: 77.8 us -> 68.3 us (0.88)
  starting transfers between devices: 33.5 us -> 22.9 us
  waiting for transfers between devices: 19.3 us -> 20.5 us
    ppermute x20, starting transfers between devices: 30.3 us -> 22.9 us  [swap(): lax.ppermute(block, axis, [(i, i ^ mask) for i in range(lax.axis_size(axi...]
    ppermute x20, waiting for transfers between devices: 15.1 us -> 20.5 us  [swap(): lax.ppermute(block, axis, [(i, i ^ mask) for i in range(lax.axis_size(axi...]
    ppermute x4 -> x0, waiting for transfers between devices: 4.22 us -> none  [paired(): return lax.ppermute(block, axis, [(i, j) for i, j in route if 0 <= j < n])]
    ppermute x4 -> x0, starting transfers between devices: 3.21 us -> none  [paired(): return lax.ppermute(block, axis, [(i, j) for i, j in route if 0 <= j < n])]
    pallas_call x1, Pallas kernels: 6.09 us -> 8.05 us  [local(): call(functools.partial(first_kernel, k, half, sub), [HBM, HBM, HBM], [(k,...]
    pallas_call x6 -> x5, Pallas kernels: 4.48 us -> 2.54 us  [the longest x1 1.49 us: local(): call(functools.partial(factor_kernel, k, half, sub), [VMEM] * 3, [(k, hal...]
  transfers between devices with their start and end apart: 24 -> 20, of which waited for: 10 -> 10; matrix products, arithmetic and copies ran while one was open for 1% -> 1% of each run, Pallas kernels for 12% -> 13%
where the time goes in v3:
time: 68.3 us; the launch traced here: 68.2 us
  starting transfers between devices  22.9 us (34%)
  waiting for transfers between devices  20.5 us (30%)
  Pallas kernels  20.1 us (29%)
  between operations  3.86 us (6%)
  other arithmetic  0.69 us (1%)
    ppermute x20, starting transfers between devices, swap(): lax.ppermute(block, axis, [(i, i ^ mask) for i in range(lax.axis_size(axi...  22.9 us
    ppermute x20, waiting for transfers between devices, swap(): lax.ppermute(block, axis, [(i, i ^ mask) for i in range(lax.axis_size(axi...  20.5 us
    pallas_call x1, Pallas kernels, local(): call(functools.partial(first_kernel, k, half, sub), [HBM, HBM, HBM], [(k,...  8.05 us
    pallas_call x2, Pallas kernels, local(): call(functools.partial(second_kernel, k, half, sub, start), [VMEM] * 4, [...  5.05 us
    pallas_call x1, Pallas kernels, local(): call(functools.partial(loading_kernel, k, half, sub), [VMEM] * 8, [(k + 8...  1.57 us
    pallas_call x2, Pallas kernels, local(): call(functools.partial(pair_kernel, half), [VMEM] * 2, [(1, k, cells)])  1.52 us
    pallas_call x1, Pallas kernels, local(): call(functools.partial(factor_kernel, k, half, sub), [VMEM] * 3, [(k, hal...  1.49 us
  transfers between devices with their start and end apart: 20, of which 10 were waited for; matrix products, arithmetic and copies ran while one was open for 1% of the time, Pallas kernels for 13%

profile of v3, /device:TPU:0, one launch (start us, length us, event | category | flops | bytes accessed | tf_op | source)
XLA Modules:
  0.0 68.2 jit_solution(12684086823371284719)
XLA Ops:
  0.6 8.0 %shard_map.119 = (f32[16,768]{1,0:T(8,128)S(1)}, f32[16,2560]{1,0:T(8,128)S(1)}, bf16[32,512]{1,0:T(8,128)(2,1)S(1)}, f32[5120,512]{1,0:T(8,128)S(1)}, bf16[2560...) custom-call(f32[1,16,5120]{2,1,0:T(8,128)} %z_ref.1, f32[16,512]{1,0:T(8,128)} %bitcast.5, s32[1,5120,512]{2,1,0:T(8,128)} %cnt_ref.1), custom_call_target="tpu_custom_call" | custom-call | tf_op jit(solution)/shard_map/pallas_call | solution.py:418
  9.3 1.5 %shard_map.120 = f32[16,2560]{1,0:T(8,128)S(1)} custom-call(bf16[32,512]{1,0:T(8,128)(2,1)S(1)} %get-tuple-element.35.lg_ref, bf16[2560,512]{1,0:T(8,128)(2,1)S(1)} %get-tuple-element.36.rh_ref, bf16[2560,512]{1,0:T(8,128)(2,1)S(1)} %get-tuple-element.37.rl_ref), custom_call_target="tpu_custom_call" | custom-call | tf_op jit(solution)/shard_map/pallas_call | solution.py:434
  10.8 2.6 %collective-permute-start.1 = (f32[16,2560]{1,0:T(8,128)S(1)}, f32[16,2560]{1,0:T(8,128)S(1)}, u32[]{:S(2)}, u32[]{:S(2)}) collective-permute-start(f32[16,2560]{1,0:T(8,128)S(1)} %add.27.own_ref), channel_id=1, source_target_pairs={{0,2},{1,3},{2,0},{3,1},{4,6},{5,7},{6,4},{7,5},{8,10},{9,11},{10,... | collective-permute-start | bytes 491528 | tf_op jit(solution)/shard_map/ppermute | solution.py:27
  13.4 1.5 %collective-permute-start.2 = (f32[16,768]{1,0:T(8,128)S(1)}, f32[16,768]{1,0:T(8,128)S(1)}, u32[]{:S(2)}, u32[]{:S(2)}) collective-permute-start(f32[16,768]{1,0:T(8,128)S(1)} %get-tuple-element.39.own_ref), channel_id=1, source_target_pairs={{0,4},{4,0},{8,12},{12,8},{16,20},{20,16},{24,28},{28,24},{1,5},{5... | collective-permute-start | bytes 147464 | tf_op jit(solution)/shard_map/ppermute | solution.py:27
  14.9 2.6 %collective-permute-done.2.got_ref.refs_0_ = f32[16,768]{1,0:T(8,128)S(1)} collective-permute-done((f32[16,768]{1,0:T(8,128)S(1)}, f32[16,768]{1,0:T(8,128)S(1)}, u32[]{:S(2)}, u32[]{:S(2)}) %collective-permute-start.2) | collective-permute-done | bytes 49184 | tf_op jit(solution)/shard_map/ppermute | solution.py:27
  17.5 1.6 %collective-permute-start.3 = (f32[16,768]{1,0:T(8,128)S(1)}, f32[16,768]{1,0:T(8,128)S(1)}, u32[]{:S(2)}, u32[]{:S(2)}) collective-permute-start(f32[16,768]{1,0:T(8,128)S(1)} %shard_map.121.refs_0_), channel_id=1, source_target_pairs={{0,8},{4,12},{8,0},{12,4},{16,24},{20,28},{24,16},{28,20},{1,9},{5... | collective-permute-start | bytes 147464 | tf_op jit(solution)/shard_map/ppermute | solution.py:27
  19.2 2.5 %collective-permute-start.4 = (f32[16,768]{1,0:T(8,128)S(1)}, f32[16,768]{1,0:T(8,128)S(1)}, u32[]{:S(2)}, u32[]{:S(2)}) collective-permute-start(f32[16,768]{1,0:T(8,128)S(1)} %shard_map.121.refs_0_), channel_id=1, source_target_pairs={{0,24},{4,28},{8,16},{12,20},{16,8},{20,12},{24,0},{28,4},{1,25},{... | collective-permute-start | bytes 147464 | tf_op jit(solution)/shard_map/ppermute | solution.py:27
  22.3 2.8 %collective-permute-done.4.refs_2_.refs_3_ = f32[16,768]{1,0:T(8,128)S(1)} collective-permute-done((f32[16,768]{1,0:T(8,128)S(1)}, f32[16,768]{1,0:T(8,128)S(1)}, u32[]{:S(2)}, u32[]{:S(2)}) %collective-permute-start.4) | collective-permute-done | bytes 49184 | tf_op jit(solution)/shard_map/ppermute | solution.py:27
  27.3 4.4 %collective-permute-done.6.refs_2_ = f32[16,768]{1,0:T(8,128)S(1)} collective-permute-done((f32[16,768]{1,0:T(8,128)S(1)}, f32[16,768]{1,0:T(8,128)S(1)}, u32[]{:S(2)}, u32[]{:S(2)}) %collective-permute-start.6) | collective-permute-done | bytes 49184 | tf_op jit(solution)/shard_map/ppermute | solution.py:27
  32.3 2.5 %shard_map.127 = (f32[16,2560]{1,0:T(8,128)S(1)}, f32[8,512]{1,0:T(8,128)S(1)}, bf16[2560,512]{1,0:T(8,128)(2,1)S(1)}, bf16[2560,512]{1,0:T(8,128)(2,1)S(1)}) custom-call(f32[16,2560]{1,0:T(8,128)S(1)} %collective-permute-done.5.oth_ref.z_ref.zo_ref, bf16[96,512]{1,0:T(8,128)(2,1)S(1)} %get-tuple-element.44.ly_ref, ...), custom_call_target="tpu_custom_call" | custom-call | tf_op jit(solution)/shard_map/pallas_call | solution.py:457
  35.0 2.5 %shard_map.126 = (f32[16,2560]{1,0:T(8,128)S(1)}, f32[8,512]{1,0:T(8,128)S(1)}, bf16[2560,512]{1,0:T(8,128)(2,1)S(1)}, bf16[2560,512]{1,0:T(8,128)(2,1)S(1)}) custom-call(f32[16,2560]{1,0:T(8,128)S(1)} %get-tuple-element.43.own_ref.z_ref.zw_ref, bf16[96,512]{1,0:T(8,128)(2,1)S(1)} %get-tuple-element.44.ly_ref, bf16[32,512]{1,0:T(8,128)(2,1)S(1)} %get-tuple-element.45.lg_ref, ...), custom_call_target="tpu_custom_call" | custom-call | tf_op jit(solution)/shard_map/pallas_call | solution.py:457
  38.2 1.6 %shard_map.128.own_ref = f32[24,768]{1,0:T(8,128)S(1)} custom-call(f32[16,2560]{1,0:T(8,128)S(1)} %collective-permute-done.5.oth_ref.z_ref.zo_ref, bf16[2560,512]{1,0:T(8,128)(2,1)S(1)} %get-tuple-element.50.rho_ref, bf16[2560,512]{1,0:T(8,128)(2,1)S(1)} %get-tuple-element.51.rlo_ref, f32[16,2560]{1,0:T(8,128)S(1)} %get-tuple-element.43.own_ref.z_ref.zw_ref, ...), custom_call_target="tpu_custom_call" | custom-call | tf_op jit(solution)/shard_map/pallas_call | solution.py:466
  39.7 1.5 %collective-permute-start.9 = (f32[24,768]{1,0:T(8,128)S(1)}, f32[24,768]{1,0:T(8,128)S(1)}, u32[]{:S(2)}, u32[]{:S(2)}) collective-permute-start(f32[24,768]{1,0:T(8,128)S(1)} %shard_map.128.own_ref), channel_id=1, source_target_pairs={{0,4},{4,0},{8,12},{12,8},{16,20},{20,16},{24,28},{28,24},{1,5},{5... | collective-permute-start | bytes 221192 | tf_op jit(solution)/shard_map/ppermute | solution.py:27
  41.3 2.8 %collective-permute-done.9.got_ref.refs_0_ = f32[24,768]{1,0:T(8,128)S(1)} collective-permute-done((f32[24,768]{1,0:T(8,128)S(1)}, f32[24,768]{1,0:T(8,128)S(1)}, u32[]{:S(2)}, u32[]{:S(2)}) %collective-permute-start.9) | collective-permute-done | bytes 73760 | tf_op jit(solution)/shard_map/ppermute | solution.py:27
  44.2 1.9 %collective-permute-start.11 = (f32[24,768]{1,0:T(8,128)S(1)}, f32[24,768]{1,0:T(8,128)S(1)}, u32[]{:S(2)}, u32[]{:S(2)}) collective-permute-start(f32[24,768]{1,0:T(8,128)S(1)} %shard_map.129.refs_0_), channel_id=1, source_target_pairs={{0,24},{4,28},{8,16},{12,20},{16,8},{20,12},{24,0},{28,4},{1,25},{... | collective-permute-start | bytes 221192 | tf_op jit(solution)/shard_map/ppermute | solution.py:27
  46.1 1.6 %collective-permute-start.13 = (f32[24,768]{1,0:T(8,128)S(1)}, f32[24,768]{1,0:T(8,128)S(1)}, u32[]{:S(2)}, u32[]{:S(2)}) collective-permute-start(f32[24,768]{1,0:T(8,128)S(1)} %shard_map.129.refs_0_), channel_id=1, source_target_pairs={{0,16},{4,20},{8,24},{12,28},{16,0},{20,4},{24,8},{28,12},{1,17},{... | collective-permute-start | bytes 221192 | tf_op jit(solution)/shard_map/ppermute | solution.py:27
  47.7 1.8 %collective-permute-done.10.refs_1_ = f32[24,768]{1,0:T(8,128)S(1)} collective-permute-done((f32[24,768]{1,0:T(8,128)S(1)}, f32[24,768]{1,0:T(8,128)S(1)}, u32[]{:S(2)}, u32[]{:S(2)}) %collective-permute-start.10) | collective-permute-done | bytes 73760 | tf_op jit(solution)/shard_map/ppermute | solution.py:27
  49.5 1.4 %collective-permute-done.11.refs_2_.refs_3_ = f32[24,768]{1,0:T(8,128)S(1)} collective-permute-done((f32[24,768]{1,0:T(8,128)S(1)}, f32[24,768]{1,0:T(8,128)S(1)}, u32[]{:S(2)}, u32[]{:S(2)}) %collective-permute-start.11) | collective-permute-done | bytes 73760 | tf_op jit(solution)/shard_map/ppermute | solution.py:27
  51.4 1.6 %collective-permute-start.15 = (f32[8,128]{1,0:T(8,128)S(1)}, f32[8,128]{1,0:T(8,128)S(1)}, u32[]{:S(2)}, u32[]{:S(2)}) collective-permute-start(f32[8,128]{1,0:T(8,128)S(1)} %get-tuple-element.64), channel_id=1, source_target_pairs={{0,4},{4,0},{8,12},{12,8},{16,20},{20,16},{24,28},{28,24},{1,5},{5... | collective-permute-start | bytes 12296 | tf_op jit(solution)/shard_map/ppermute | solution.py:27
  54.5 1.5 %collective-permute-start.14 = (f32[8,128]{1,0:T(8,128)S(1)}, f32[8,128]{1,0:T(8,128)S(1)}, u32[]{:S(2)}, u32[]{:S(2)}) collective-permute-start(f32[8,128]{1,0:T(8,128)S(1)} %get-tuple-element.63), channel_id=1, source_target_pairs={{0,2},{1,3},{2,0},{3,1},{4,6},{5,7},{6,4},{7,5},{8,10},{9,11},{10,... | collective-permute-start | bytes 12296 | tf_op jit(solution)/shard_map/ppermute | solution.py:27
  56.0 1.9 %collective-permute-start.16 = (f32[8,128]{1,0:T(8,128)S(1)}, f32[8,128]{1,0:T(8,128)S(1)}, u32[]{:S(2)}, u32[]{:S(2)}) collective-permute-start(f32[8,128]{1,0:T(8,128)S(1)} %add.30), channel_id=1, source_target_pairs={{0,8},{4,12},{8,0},{12,4},{16,24},{20,28},{24,16},{28,20},{1,9},{5... | collective-permute-start | bytes 12296 | tf_op jit(solution)/shard_map/ppermute | solution.py:27
  58.4 1.9 %collective-permute-start.18 = (f32[8,128]{1,0:T(8,128)S(1)}, f32[8,128]{1,0:T(8,128)S(1)}, u32[]{:S(2)}, u32[]{:S(2)}) collective-permute-start(f32[8,128]{1,0:T(8,128)S(1)} %add.30), channel_id=1, source_target_pairs={{0,24},{4,28},{8,16},{12,20},{16,8},{20,12},{24,0},{28,4},{1,25},{... | collective-permute-start | bytes 12296 | tf_op jit(solution)/shard_map/ppermute | solution.py:27
  60.4 2.0 %collective-permute-done.17 = f32[8,128]{1,0:T(8,128)S(1)} collective-permute-done((f32[8,128]{1,0:T(8,128)S(1)}, f32[8,128]{1,0:T(8,128)S(1)}, u32[]{:S(2)}, u32[]{:S(2)}) %collective-permute-start.17) | collective-permute-done | bytes 4128 | tf_op jit(solution)/shard_map/ppermute | solution.py:27
  62.4 1.4 %collective-permute-done.18 = f32[8,128]{1,0:T(8,128)S(1)} collective-permute-done((f32[8,128]{1,0:T(8,128)S(1)}, f32[8,128]{1,0:T(8,128)S(1)}, u32[]{:S(2)}, u32[]{:S(2)}) %collective-permute-start.18) | collective-permute-done | bytes 4128 | tf_op jit(solution)/shard_map/ppermute | solution.py:27
  (48 shorter events, 8.8 us)
Async XLA Ops:
  8.7 2.1 %collective-permute-start = (f32[16,2560]{1,0:T(8,128)S(1)}, f32[16,2560]{1,0:T(8,128)S(1)}, u32[]{:S(2)}, u32[]{:S(2)}) collective-permute-start(f32[16,2560]{1,0:T(8,128)S(1)} %get-tuple-element.38), channel_id=1, source_target_pairs={{0,1},{1,0},{2,3},{3,2},{4,5},{5,4},{6,7},{7,6},{8,9},{9,8},{10,11... | collective-permute-start | bytes 491528 | tf_op jit(solution)/shard_map/ppermute | solution.py:27
  9.2 15.9 %copy-start = (f32[1,16,5120]{2,1,0:T(8,128)S(1)}, f32[1,16,5120]{2,1,0:T(8,128)}, u32[]{:S(2)}) copy-start(f32[1,16,5120]{2,1,0:T(8,128)} %z_ref.1) | copy-start | bytes 983044
  9.2 15.9 %copy-start.1 = (f32[1,16,5120]{2,1,0:T(8,128)S(1)}, f32[1,16,5120]{2,1,0:T(8,128)}, u32[]{:S(2)}) copy-start(f32[1,16,5120]{2,1,0:T(8,128)} %mom_ref.1) | copy-start | bytes 983044
  9.3 22.4 %copy-start.2 = (f32[512,16]{0,1:T(8,128)S(1)}, f32[512,16]{0,1:T(8,128)}, u32[]{:S(2)}) copy-start(f32[512,16]{0,1:T(8,128)} %param.10) | copy-start | bytes 98308
  9.3 22.4 %copy-start.3 = (f32[512,16]{0,1:T(8,128)S(1)}, f32[512,16]{0,1:T(8,128)}, u32[]{:S(2)}) copy-start(f32[512,16]{0,1:T(8,128)} %param.12) | copy-start | bytes 98308
  10.8 14.8 %collective-permute-start.1 = (f32[16,2560]{1,0:T(8,128)S(1)}, f32[16,2560]{1,0:T(8,128)S(1)}, u32[]{:S(2)}, u32[]{:S(2)}) collective-permute-start(f32[16,2560]{1,0:T(8,128)S(1)} %add.27.own_ref), channel_id=1, source_target_pairs={{0,2},{1,3},{2,0},{3,1},{4,6},{5,7},{6,4},{7,5},{8,10},{9,11},{10,... | collective-permute-start | bytes 491528 | tf_op jit(solution)/shard_map/ppermute | solution.py:27
  13.4 4.1 %collective-permute-start.2 = (f32[16,768]{1,0:T(8,128)S(1)}, f32[16,768]{1,0:T(8,128)S(1)}, u32[]{:S(2)}, u32[]{:S(2)}) collective-permute-start(f32[16,768]{1,0:T(8,128)S(1)} %get-tuple-element.39.own_ref), channel_id=1, source_target_pairs={{0,4},{4,0},{8,12},{12,8},{16,20},{20,16},{24,28},{28,24},{1,5},{5... | collective-permute-start | bytes 147464 | tf_op jit(solution)/shard_map/ppermute | solution.py:27
  17.5 4.7 %collective-permute-start.3 = (f32[16,768]{1,0:T(8,128)S(1)}, f32[16,768]{1,0:T(8,128)S(1)}, u32[]{:S(2)}, u32[]{:S(2)}) collective-permute-start(f32[16,768]{1,0:T(8,128)S(1)} %shard_map.121.refs_0_), channel_id=1, source_target_pairs={{0,8},{4,12},{8,0},{12,4},{16,24},{20,28},{24,16},{28,20},{1,9},{5... | collective-permute-start | bytes 147464 | tf_op jit(solution)/shard_map/ppermute | solution.py:27
  19.2 5.9 %collective-permute-start.4 = (f32[16,768]{1,0:T(8,128)S(1)}, f32[16,768]{1,0:T(8,128)S(1)}, u32[]{:S(2)}, u32[]{:S(2)}) collective-permute-start(f32[16,768]{1,0:T(8,128)S(1)} %shard_map.121.refs_0_), channel_id=1, source_target_pairs={{0,24},{4,28},{8,16},{12,20},{16,8},{20,12},{24,0},{28,4},{1,25},{... | collective-permute-start | bytes 147464 | tf_op jit(solution)/shard_map/ppermute | solution.py:27
  25.7 6.6 %collective-permute-start.5 = (f32[16,2560]{1,0:T(8,128)S(1)}, f32[16,2560]{1,0:T(8,128)S(1)}, u32[]{:S(2)}, u32[]{:S(2)}) collective-permute-start(f32[16,2560]{1,0:T(8,128)S(1)} %get-tuple-element.43.own_ref.z_ref.zw_ref), channel_id=1, source_target_pairs={{0,1},{1,0},{2,3},{3,2},{4,5},{5,4},{6,7},{7,6},{8,9},{9,8},{10,11... | collective-permute-start | bytes 491528 | tf_op jit(solution)/shard_map/ppermute | solution.py:27
  25.8 5.9 %collective-permute-start.6 = (f32[16,768]{1,0:T(8,128)S(1)}, f32[16,768]{1,0:T(8,128)S(1)}, u32[]{:S(2)}, u32[]{:S(2)}) collective-permute-start(f32[16,768]{1,0:T(8,128)S(1)} %shard_map.121.refs_0_), channel_id=1, source_target_pairs={{0,16},{4,20},{8,24},{12,28},{16,0},{20,4},{24,8},{28,12},{1,17},{... | collective-permute-start | bytes 147464 | tf_op jit(solution)/shard_map/ppermute | solution.py:27
  34.9 2.6 %collective-permute-start.7 = (f32[16,2560]{1,0:T(8,128)S(1)}, f32[16,2560]{1,0:T(8,128)S(1)}, u32[]{:S(2)}, u32[]{:S(2)}) collective-permute-start(f32[16,2560]{1,0:T(8,128)S(1)} %get-tuple-element.48), channel_id=1, source_target_pairs={{0,1},{1,0},{2,3},{3,2},{4,5},{5,4},{6,7},{7,6},{8,9},{9,8},{10,11... | collective-permute-start | bytes 491528 | tf_op jit(solution)/shard_map/ppermute | solution.py:27
  37.6 13.8 %collective-permute-start.8 = (f32[16,2560]{1,0:T(8,128)S(1)}, f32[16,2560]{1,0:T(8,128)S(1)}, u32[]{:S(2)}, u32[]{:S(2)}) collective-permute-start(f32[16,2560]{1,0:T(8,128)S(1)} %add.28.own_ref), channel_id=1, source_target_pairs={{0,2},{1,3},{2,0},{3,1},{4,6},{5,7},{6,4},{7,5},{8,10},{9,11},{10,... | collective-permute-start | bytes 491528 | tf_op jit(solution)/shard_map/ppermute | solution.py:27
  39.7 4.4 %collective-permute-start.9 = (f32[24,768]{1,0:T(8,128)S(1)}, f32[24,768]{1,0:T(8,128)S(1)}, u32[]{:S(2)}, u32[]{:S(2)}) collective-permute-start(f32[24,768]{1,0:T(8,128)S(1)} %shard_map.128.own_ref), channel_id=1, source_target_pairs={{0,4},{4,0},{8,12},{12,8},{16,20},{20,16},{24,28},{28,24},{1,5},{5... | collective-permute-start | bytes 221192 | tf_op jit(solution)/shard_map/ppermute | solution.py:27
  44.1 5.4 %collective-permute-start.10 = (f32[24,768]{1,0:T(8,128)S(1)}, f32[24,768]{1,0:T(8,128)S(1)}, u32[]{:S(2)}, u32[]{:S(2)}) collective-permute-start(f32[24,768]{1,0:T(8,128)S(1)} %shard_map.129.refs_0_), channel_id=1, source_target_pairs={{0,8},{4,12},{8,0},{12,4},{16,24},{20,28},{24,16},{28,20},{1,9},{5... | collective-permute-start | bytes 221192 | tf_op jit(solution)/shard_map/ppermute | solution.py:27
  44.2 6.6 %collective-permute-start.11 = (f32[24,768]{1,0:T(8,128)S(1)}, f32[24,768]{1,0:T(8,128)S(1)}, u32[]{:S(2)}, u32[]{:S(2)}) collective-permute-start(f32[24,768]{1,0:T(8,128)S(1)} %shard_map.129.refs_0_), channel_id=1, source_target_pairs={{0,24},{4,28},{8,16},{12,20},{16,8},{20,12},{24,0},{28,4},{1,25},{... | collective-permute-start | bytes 221192 | tf_op jit(solution)/shard_map/ppermute | solution.py:27
  46.1 7.7 %collective-permute-start.13 = (f32[24,768]{1,0:T(8,128)S(1)}, f32[24,768]{1,0:T(8,128)S(1)}, u32[]{:S(2)}, u32[]{:S(2)}) collective-permute-start(f32[24,768]{1,0:T(8,128)S(1)} %shard_map.129.refs_0_), channel_id=1, source_target_pairs={{0,16},{4,20},{8,24},{12,28},{16,0},{20,4},{24,8},{28,12},{1,17},{... | collective-permute-start | bytes 221192 | tf_op jit(solution)/shard_map/ppermute | solution.py:27
  51.4 4.5 %collective-permute-start.15 = (f32[8,128]{1,0:T(8,128)S(1)}, f32[8,128]{1,0:T(8,128)S(1)}, u32[]{:S(2)}, u32[]{:S(2)}) collective-permute-start(f32[8,128]{1,0:T(8,128)S(1)} %get-tuple-element.64), channel_id=1, source_target_pairs={{0,4},{4,0},{8,12},{12,8},{16,20},{20,16},{24,28},{28,24},{1,5},{5... | collective-permute-start | bytes 12296 | tf_op jit(solution)/shard_map/ppermute | solution.py:27
  54.5 5.9 %collective-permute-start.14 = (f32[8,128]{1,0:T(8,128)S(1)}, f32[8,128]{1,0:T(8,128)S(1)}, u32[]{:S(2)}, u32[]{:S(2)}) collective-permute-start(f32[8,128]{1,0:T(8,128)S(1)} %get-tuple-element.63), channel_id=1, source_target_pairs={{0,2},{1,3},{2,0},{3,1},{4,6},{5,7},{6,4},{7,5},{8,10},{9,11},{10,... | collective-permute-start | bytes 12296 | tf_op jit(solution)/shard_map/ppermute | solution.py:27
  56.0 4.4 %collective-permute-start.16 = (f32[8,128]{1,0:T(8,128)S(1)}, f32[8,128]{1,0:T(8,128)S(1)}, u32[]{:S(2)}, u32[]{:S(2)}) collective-permute-start(f32[8,128]{1,0:T(8,128)S(1)} %add.30), channel_id=1, source_target_pairs={{0,8},{4,12},{8,0},{12,4},{16,24},{20,28},{24,16},{28,20},{1,9},{5... | collective-permute-start | bytes 12296 | tf_op jit(solution)/shard_map/ppermute | solution.py:27
  57.9 4.5 %collective-permute-start.17 = (f32[8,128]{1,0:T(8,128)S(1)}, f32[8,128]{1,0:T(8,128)S(1)}, u32[]{:S(2)}, u32[]{:S(2)}) collective-permute-start(f32[8,128]{1,0:T(8,128)S(1)} %add.30), channel_id=1, source_target_pairs={{0,16},{4,20},{8,24},{12,28},{16,0},{20,4},{24,8},{28,12},{1,17},{... | collective-permute-start | bytes 12296 | tf_op jit(solution)/shard_map/ppermute | solution.py:27
  58.4 5.4 %collective-permute-start.18 = (f32[8,128]{1,0:T(8,128)S(1)}, f32[8,128]{1,0:T(8,128)S(1)}, u32[]{:S(2)}, u32[]{:S(2)}) collective-permute-start(f32[8,128]{1,0:T(8,128)S(1)} %add.30), channel_id=1, source_target_pairs={{0,24},{4,28},{8,16},{12,20},{16,8},{20,12},{24,0},{28,4},{1,25},{... | collective-permute-start | bytes 12296 | tf_op jit(solution)/shard_map/ppermute | solution.py:27
  60.3 5.9 %collective-permute-start.12 = (f32[16,2560]{1,0:T(8,128)S(1)}, f32[16,2560]{1,0:T(8,128)S(1)}, u32[]{:S(2)}, u32[]{:S(2)}) collective-permute-start(f32[16,2560]{1,0:T(8,128)S(1)} %get-tuple-element.58.own_ref), channel_id=1, source_target_pairs={{0,1},{1,0},{2,3},{3,2},{4,5},{5,4},{6,7},{7,6},{8,9},{9,8},{10,11... | collective-permute-start | bytes 491528 | tf_op jit(solution)/shard_map/ppermute | solution.py:27
  63.8 1.2 %collective-permute-start.19 = (f32[8,128]{1,0:T(8,128)S(1)}, f32[8,128]{1,0:T(8,128)S(1)}, u32[]{:S(2)}, u32[]{:S(2)}) collective-permute-start(f32[8,128]{1,0:T(8,128)S(1)} %add_add_fusion), channel_id=1, source_target_pairs={{0,1},{1,0},{2,3},{3,2},{4,5},{5,4},{6,7},{7,6},{8,9},{9,8},{10,11... | collective-permute-start | bytes 12296 | tf_op jit(solution)/shard_map/ppermute | solution.py:27
  (1 other events, 15.8 us)

commit v4 on v3

--- a/solution.py
+++ b/solution.py
@@ -46,6 +46,10 @@
         groups.append([stride * g for g in range(1, radix)])
         stride *= radix
     return groups
+
+
+def rides(n_site):
+    return n_site == 8 == TGY
 
 
 def add(terms):
@@ -120,7 +124,7 @@
 
 
 def first_kernel(
-    k, half, sub, z_hbm, lt_hbm, cnt_ref, load_ref, oth_ref, lg_ref, held_ref, rh_ref, rl_ref,
+    k, half, sub, z_hbm, lt_hbm, cnt_ref, load_ref, lg_ref, held_ref, rho_ref, rlo_ref, rhw_ref, rlw_ref,
     ly_ref, z_ref, lt_ref, buf_ref, sem, sems
 ):
     c = core()
@@ -147,7 +151,7 @@
     fill_loadings(lt_ref[...], ly_ref, lg_ref)
     small[1].wait()
     load_ref[:, -2 * LANES : -LANES], load_ref[:, -LANES:] = pack_rims(vregs_of(z_ref[0]), k)
-    ly, lg = ly_ref[...], lg_ref[...]
+    ly = ly_ref[...]
     loads = []
     for i in range(2 * steps):
         copy(i).wait()
@@ -158,12 +162,10 @@
         held_ref[rows, :] = cf
         _, _, rh, rl, h, m = residuals(z_ref[0, :, pl.ds(place(i), sub)], cf, ly)
         loads.append(loading_terms(h, m, rh, rl, k))
-        if i < steps:
-            oth_ref[:, i * sub : (i + 1) * sub] = factor_terms(rh, rl, lg, k)
-        else:
-            rows = pl.ds((i - steps) * sub, sub)
-            rh_ref[rows, :] = rh
-            rl_ref[rows, :] = rl
+        rh_ref, rl_ref = (rho_ref, rlo_ref) if i < steps else (rhw_ref, rlw_ref)
+        rows = pl.ds((i % steps) * sub, sub)
+        rh_ref[rows, :] = rh
+        rl_ref[rows, :] = rl
     load_ref[:, : -2 * LANES] = add(loads)
 
 
@@ -176,13 +178,12 @@
 
 def move_loadings_kernel(n_terms, *refs):
     terms = refs[:n_terms]
-    lt_ref, lm_ref, sl_ref, out_ref, newl_ref, halfl_ref, ly_ref, lg_ref = refs[n_terms:]
+    lt_ref, lm_ref, sl_ref, newl_ref, halfl_ref, ly_ref, lg_ref = refs[n_terms:]
     step = sl_ref[0]
     halfl = lm_ref[...] + 0.5 * step * (add([t[:, : lt_ref.shape[1]] for t in terms]) - lt_ref[...])
     newl = lt_ref[...] + step * halfl
     halfl_ref[...] = halfl
     newl_ref[...] = newl
-    out_ref[...] = newl
     fill_loadings(newl, ly_ref, lg_ref)
 
 
@@ -229,25 +230,33 @@
     return first, last
 
 
-def prior_of(vregs, lo, hi, left, right, upper, lower, k):
+def prior_of(vregs, upper, lower, k):
     q = lax.rem(lane((k, LANES)), TY)
+    wide = lane((k, LANES))
     n = len(vregs)
-    wide = lane((k, LANES))
     out = []
-    zero = jnp.zeros((k, LANES), f32)
-    for j in range(lo, hi):
-        v = vregs[j]
-        back = pltpu.roll(v, 1, 1)
-        ahead = pltpu.roll(v, LANES - 1, 1)
-        lrim = pltpu.roll(left, (LANES - j) % LANES, 1) if j else left
-        rrim = pltpu.roll(right, (TY - 1 - j) % LANES, 1)
-        beside = jnp.where(q == 0, lrim, back) + jnp.where(q == TY - 1, rrim, ahead)
+    for j, v in enumerate(vregs):
+        back = jnp.where(q == 0, 0.0, pltpu.roll(v, 1, 1))
+        ahead = jnp.where(q == TY - 1, 0.0, pltpu.roll(v, LANES - 1, 1))
         prev = vregs[j - 1] if j else upper
         nxt = vregs[j + 1] if j + 1 < n else lower
-        shift_down = pltpu.roll(v, TY, 1)
-        above = jnp.where(wide < TY, pltpu.roll(prev, TY, 1), shift_down)
+        above = jnp.where(wide < TY, pltpu.roll(prev, TY, 1), pltpu.roll(v, TY, 1))
         below = jnp.where(wide >= LANES - TY, pltpu.roll(nxt, LANES - TY, 1), pltpu.roll(v, LANES - TY, 1))
-        out.append((kappa_sq + 4.0) * v - (above + below + beside))
+        out.append((kappa_sq + 4.0) * v - (above + below + (back + ahead)))
+    return out
+
+
+def beside_of(left, right, half, k):
+    q = lax.rem(lane((k, LANES)), TY)
+    n = half // LANES
+    low = core() == 0
+    left = jnp.where(low, left, pltpu.roll(left, (LANES - n) % LANES, 1))
+    right = jnp.where(low, right, pltpu.roll(right, (LANES - n) % LANES, 1))
+    out = []
+    for j in range(n):
+        lrim = pltpu.roll(left, LANES - j, 1) if j else left
+        rrim = pltpu.roll(right, (TY - 1 - j) % LANES, 1)
+        out.append(jnp.where(q == 0, lrim, 0.0) + jnp.where(q == TY - 1, rrim, 0.0))
     return out
 
 
@@ -259,9 +268,7 @@
         near = jnp.where(even, pair[:k, -2 * LANES : -LANES], pair[:k, -LANES:])
         row = me // 2
         close = (lax.rem(row, 2) == 1) == even
-        first = jnp.where(close, one[:k, -2 * LANES : -LANES], three[:k, -2 * LANES : -LANES])
-        last = jnp.where(close, one[:k, -LANES:], three[:k, -LANES:])
-        far = jnp.where(even, last, first)
+        far = jnp.where(close, one[:k, -LANES:], three[:k, -LANES:])
     else:
         near, far = refs[0][...], refs[1][...]
     left = jnp.where(me == 0, 0.0, jnp.where(even, far, near))
@@ -283,22 +290,22 @@
     near_ref[...], far_ref[...] = rims_of(vregs_of(z_ref[0]), k)
 
 
-def stage_kernel(own_ref, got_ref, out_ref):
-    own, got = own_ref[...], got_ref[...]
-    out_ref[:, : -2 * LANES] = own[:, : -2 * LANES] + got[:, : -2 * LANES]
-    even = lax.rem(lax.axis_index("site"), 2) == 0
-    out_ref[:, -2 * LANES : -LANES] = jnp.where(even, own[:, -2 * LANES : -LANES], got[:, -2 * LANES : -LANES])
-    out_ref[:, -LANES:] = jnp.where(even, got[:, -LANES:], own[:, -LANES:])
-
-
-def ahead_kernel(
-    ride, k, half, z_ref, mom_ref, upper_ref, lower_ref, gain_ref, sf_ref, *refs
-):
-    *halo, a_ref, z_own_ref, s_ref = refs
+def stage_kernel(near, own_ref, got_ref, *refs):
+    *sums, out_ref = refs
+    a, b = sums if sums else (own_ref, got_ref)
+    width = own_ref.shape[1] - 2 * LANES
+    out_ref[:, :width] = a[:, :width] + b[:, :width]
+    site = lax.axis_index("site")
+    even = lax.rem(site, 2) == 0
+    first = jnp.where(even, own_ref[:, -2 * LANES : -LANES], got_ref[:, -2 * LANES : -LANES])
+    last = jnp.where(even, got_ref[:, -LANES:], own_ref[:, -LANES:])
+    out_ref[:, width:] = jnp.where((lax.rem(site // 2, 2) == 0) == near, last, first)
+
+
+def ahead_kernel(k, half, z_ref, mom_ref, upper_ref, lower_ref, gain_ref, sf_ref, a_ref, z_own_ref, s_ref):
     c = core()
     step = sf_ref[0]
-    left, right = sides(ride, halo, k)
-    out = prior_of(vregs_of(z_ref[0]), 0, 2 * half // LANES, left, right, upper_ref[...], lower_ref[...], k)
+    out = prior_of(vregs_of(z_ref[0]), upper_ref[...], lower_ref[...], k)
     n = half // LANES
     gain = gain_ref[...] * (0.5 * step)
     for j in range(n):
@@ -310,12 +317,15 @@
     s_ref[...] = jnp.full(s_ref.shape, step, f32)
 
 
-def move_kernel(half, own_ref, other_ref, a_ref, z_ref, s_ref, half_ref, moved_ref):
+def move_kernel(ride, k, half, own_ref, other_ref, a_ref, z_ref, s_ref, gain_ref, *refs):
+    *halo, half_ref, moved_ref = refs
+    beside = beside_of(*sides(ride, halo, k), half, k)
+    step, gain = s_ref[...], gain_ref[...]
     for j in range(half // LANES):
         at = pl.ds(j * LANES, LANES)
-        h = a_ref[:, at] + (0.5 * s_ref[...]) * (own_ref[:, at] + other_ref[:, at])
+        h = a_ref[:, at] + (0.5 * step) * ((own_ref[:, at] + other_ref[:, at]) + gain * beside[j])
         half_ref[:, at] = h
-        moved_ref[:, at] = z_ref[:, at] + s_ref[...] * h
+        moved_ref[:, at] = z_ref[:, at] + step * h
 
 
 def in_order(own, oth):
@@ -328,12 +338,9 @@
     near_ref[...], far_ref[...] = rims_of(in_order(own_ref[...], oth_ref[...]), k)
 
 
-def behind_kernel(ride, k, half, own_ref, oth_ref, h_ref, upper_ref, lower_ref, gain_ref, s_ref, *refs):
-    *halo, a_ref, e_ref = refs
+def behind_kernel(k, half, own_ref, oth_ref, h_ref, upper_ref, lower_ref, gain_ref, s_ref, a_ref, e_ref):
     c = core()
-    left, right = sides(ride, halo, k)
-    z = in_order(own_ref[...], oth_ref[...])
-    out = prior_of(z, 0, 2 * half // LANES, left, right, upper_ref[...], lower_ref[...], k)
+    out = prior_of(in_order(own_ref[...], oth_ref[...]), upper_ref[...], lower_ref[...], k)
     n = half // LANES
     gain = gain_ref[...]
     energy = jnp.zeros((k, LANES), f32)
@@ -345,21 +352,30 @@
     e_ref[...] = energy
 
 
-def end_kernel(k, half, own_ref, other_ref, a_ref, s_ref, pe_ref, end_ref, b_ref):
+def end_kernel(ride, k, half, own_ref, other_ref, a_ref, z_ref, s_ref, gain_ref, pe_ref, *refs):
+    *halo, end_ref, b_ref = refs
+    beside = beside_of(*sides(ride, halo, k), half, k)
+    step, gain = s_ref[...], gain_ref[...]
     energy = pe_ref[...]
     for j in range(half // LANES):
         at = pl.ds(j * LANES, LANES)
-        e = a_ref[:, at] + (0.5 * s_ref[...]) * (own_ref[:, at] + other_ref[:, at])
+        rim = gain * beside[j]
+        e = a_ref[:, at] + (0.5 * step) * ((own_ref[:, at] + other_ref[:, at]) + rim)
         end_ref[:, at] = e
-        energy = energy + e * e
+        energy = energy + (e * e - z_ref[:, at] * rim)
     b_ref[...] = 0.5 * sum(energy[g * 8 : (g + 1) * 8] for g in range(k // 8))
 
 
-def pair_kernel(half, own_ref, oth_ref, full_ref):
+def pair_kernel(half, own_ref, oth_ref, loadings_ref, full_ref, out_ref):
     c = core()
     own, oth = own_ref[...], oth_ref[...]
     full_ref[0, :, :half] = jnp.where(c == 0, own, oth)
     full_ref[0, :, half:] = jnp.where(c == 0, oth, own)
+    out_ref[...] = loadings_ref[...]
+
+
+def energy_kernel(entries, own_ref, got_ref, out_ref):
+    out_ref[0] = jnp.sum(own_ref[...] + got_ref[...]) / entries
 
 
 def loading_end_kernel(k, n_terms, *refs):
@@ -387,15 +403,23 @@
     gain = jnp.broadcast_to(precision[:, None], (k, LANES))
     zero_rim = jnp.zeros((k, LANES), f32)
 
-    ride = site == [[1], [2, 4, 6]]
+    ride = rides(n_site)
 
     def exchange(load):
         if not ride:
             return sum_terms(load, "site", site), ()
+        shape = (load.shape[0], species + LANES)
+
+        def stage(near, *args):
+            kernel = functools.partial(stage_kernel, near)
+            return call(kernel, [VMEM] * len(args), [shape])(*args)[0]
+
         got = swap(load, "site", 1)
-        (total,) = call(stage_kernel, [VMEM] * 2, [load.shape])(load, got)
-        terms = [total] + [swap(total, "site", m) for m in site[1]]
-        return terms, (got, terms[1], terms[3])
+        two = stage(True, load, got)
+        got_two = swap(two, "site", 2)
+        four = stage(False, load, got, two, got_two)
+        got_four = swap(four, "site", 6)
+        return [four, got_four], (got, got_two, got_four)
 
     def upright(low, high):
         if n_site <= TGY:
@@ -415,10 +439,10 @@
         return terms[0], add(terms[1:])
 
     rates, grads = (6 * k, species), (2 * k, species)
-    load, oth, lg, held, rh, rl = call(
+    load, lg, held, rho, rlo, rhw, rlw = call(
         functools.partial(first_kernel, k, half, sub),
         [HBM, HBM, HBM],
-        [(k, species + 2 * LANES), (k, half), grads, (cells, species), (half, species), (half, species)],
+        [(k, species + 2 * LANES), grads, (cells, species)] + [(half, species)] * 4,
         [
             pltpu.VMEM(rates, bf16),
             pltpu.VMEM((1, k, cells), f32),
@@ -428,31 +452,34 @@
             pltpu.SemaphoreType.DMA((2,)),
         ],
         12,
-        (2, 4, 5),
+        (1, 3, 4, 5, 6),
     )(*[pltpu.with_memory_space_constraint(x, pltpu.HBM) for x in (factors, lt, counts)])
     load_terms, halo = exchange(load)
-    (own,) = call(functools.partial(factor_kernel, k, half, sub), [VMEM] * 3, [(k, half)])(lg, rh, rl)
+    (oth,), (own,) = [
+        call(functools.partial(factor_kernel, k, half, sub), [VMEM] * 3, [(k, half)])(lg, rh, rl)
+        for rh, rl in ((rho, rlo), (rhw, rlw))
+    ]
     own, other = share(own, oth)
 
     halo = sideways(rims_kernel, halo, factors)
     edges = upright(factors[0, :, :TY], factors[0, :, cells - TY :])
     a1, z_own, svec = call(
-        functools.partial(ahead_kernel, ride, k, half),
-        [VMEM] * 5 + [SMEM] + [VMEM] * len(halo),
-        [(k, half), (k, half), (k, LANES)],
-    )(factors, factor_momenta, *edges, gain, factor_step, *halo)
+        functools.partial(ahead_kernel, k, half), [VMEM] * 5 + [SMEM], [(k, half), (k, half), (k, LANES)]
+    )(factors, factor_momenta, *edges, gain, factor_step)
     half_own, moved_own = call(
-        functools.partial(move_kernel, half), [VMEM] * 5, [(k, half)] * 2
-    )(own, other, a1, z_own, svec)
+        functools.partial(move_kernel, ride, k, half), [VMEM] * (6 + len(halo)), [(k, half)] * 2
+    )(own, other, a1, z_own, svec, gain, *halo)
     moved_oth = swap(moved_own, "sp", 1)
-    (new_factors,) = call(functools.partial(pair_kernel, half), [VMEM] * 2, [(1, k, cells)])(moved_own, moved_oth)
-
-    new_loadings, newl, halfl, ly, lg = call(
+
+    newl, halfl, ly, lg = call(
         functools.partial(move_loadings_kernel, len(load_terms)),
         [VMEM] * (len(load_terms) + 2) + [SMEM],
-        [(k, species)] * 3 + [rates, grads],
-        packed=(3, 4),
+        [(k, species)] * 2 + [rates, grads],
+        packed=(2, 3),
     )(*load_terms, lt, lm, loading_step)
+    new_factors, new_loadings = call(
+        functools.partial(pair_kernel, half), [VMEM] * 3, [(1, k, cells), (k, species)]
+    )(moved_own, moved_oth, newl)
     (own, lik_own, *parts_own), (oth, lik_oth, *parts_oth) = [
         call(
             functools.partial(second_kernel, k, half, sub, start),
@@ -472,24 +499,30 @@
     halo = sideways(join_kernel, halo, moved_own, moved_oth)
     edges = upright(new_factors[0, :, :TY], new_factors[0, :, cells - TY :])
     a2, prior_energy = call(
-        functools.partial(behind_kernel, ride, k, half), [VMEM] * (7 + len(halo)), [(k, half), (k, LANES)]
-    )(moved_own, moved_oth, half_own, *edges, gain, svec, *halo)
+        functools.partial(behind_kernel, k, half), [VMEM] * 7, [(k, half), (k, LANES)]
+    )(moved_own, moved_oth, half_own, *edges, gain, svec)
     end_own, b_part = call(
-        functools.partial(end_kernel, k, half), [VMEM] * 5, [(k, half), (8, LANES)]
-    )(own, other, a2, svec, prior_energy)
+        functools.partial(end_kernel, ride, k, half), [VMEM] * (7 + len(halo)), [(k, half), (8, LANES)]
+    )(own, other, a2, moved_own, svec, gain, prior_energy, *halo)
     end_oth = swap(end_own, "sp", 1)
-    (new_momenta,) = call(functools.partial(pair_kernel, half), [VMEM] * 2, [(1, k, cells)])(end_own, end_oth)
-
     endl, s_part = call(
         functools.partial(loading_end_kernel, k, len(load_terms)),
         [VMEM] * (len(load_terms) + 2) + [SMEM],
         [(k, species), (8, LANES)],
     )(*load_terms, newl, halfl, loading_step)
+    new_momenta, end_loadings = call(
+        functools.partial(pair_kernel, half), [VMEM] * 3, [(1, k, cells), (k, species)]
+    )(end_own, end_oth, endl)
     total = add(sum_terms(s_part, "sp", chips) + sum_terms(b_part, "site", site))
-    total = total + swap(total, "sp", 1)
-    entries = n_site * cells * n_sp * species
-    energy = jnp.reshape(jnp.sum(total) / entries, (1,))
-    return new_factors, new_momenta, new_loadings.T, endl.T, energy
+    energy = pl.pallas_call(
+        functools.partial(energy_kernel, n_site * cells * n_sp * species),
+        in_specs=[VMEM] * 2,
+        out_specs=SMEM,
+        out_shape=jax.ShapeDtypeStruct((1,), f32),
+        name="energy",
+        compiler_params=pltpu.CompilerParams(vmem_limit_bytes=1 << 20),
+    )(total, swap(total, "sp", 1))
+    return new_factors, new_momenta, new_loadings.T, end_loadings.T, energy
 
 
 def solution(mesh):

time: 68.3 us -> 66.8 us (0.978)
  waiting for transfers between devices: 20.5 us -> 22.5 us
  between operations: 3.86 us -> 2.1 us
  Pallas kernels: 20.1 us -> 19.2 us
    ppermute x20 -> x18, waiting for transfers between devices: 20.5 us -> 22.5 us  [swap(): lax.ppermute(block, axis, [(i, i ^ mask) for i in range(lax.axis_size(axi...]
    pallas_call x1, Pallas kernels: 8.05 us -> 6.12 us  [local(): call(functools.partial(first_kernel, k, half, sub), [HBM, HBM, HBM], [(k,...]
    pallas_call x1 -> x2, Pallas kernels: 1.49 us -> 2.99 us  [local(): call(functools.partial(factor_kernel, k, half, sub), [VMEM] * 3, [(k, hal...]
    pallas_call x8 -> x11, Pallas kernels: 2.67 us -> 3.41 us  [the longest x2 1.53 us: local(): call(functools.partial(pair_kernel, half), [VMEM] * 3, [(1, k, cells), (k...]
    ppermute x20 -> x18, starting transfers between devices: 22.9 us -> 22.6 us  [swap(): lax.ppermute(block, axis, [(i, i ^ mask) for i in range(lax.axis_size(axi...]
  transfers between devices with their start and end apart: 20 -> 18, of which waited for: 10 -> 11; matrix products, arithmetic and copies ran while one was open for 1% -> 0% of each run, Pallas kernels for 13% -> 12%
where the time goes in v4:
time: 66.8 us; the launch traced here: 66.6 us
  starting transfers between devices  22.6 us (34%)
  waiting for transfers between devices  22.5 us (34%)
  Pallas kernels  19.2 us (29%)
  between operations  2.1 us (3%)
    ppermute x18, starting transfers between devices, swap(): lax.ppermute(block, axis, [(i, i ^ mask) for i in range(lax.axis_size(axi...  22.6 us
    ppermute x18, waiting for transfers between devices, swap(): lax.ppermute(block, axis, [(i, i ^ mask) for i in range(lax.axis_size(axi...  22.5 us
    pallas_call x1, Pallas kernels, local(): call(functools.partial(first_kernel, k, half, sub), [HBM, HBM, HBM], [(k,...  6.12 us
    pallas_call x2, Pallas kernels, local(): call(functools.partial(second_kernel, k, half, sub, start), [VMEM] * 4, [...  5.06 us
    pallas_call x2, Pallas kernels, local(): call(functools.partial(factor_kernel, k, half, sub), [VMEM] * 3, [(k, hal...  2.99 us
    pallas_call x1, Pallas kernels, local(): call(functools.partial(loading_kernel, k, half, sub), [VMEM] * 8, [(k + 8...  1.6 us
    pallas_call x2, Pallas kernels, local(): call(functools.partial(pair_kernel, half), [VMEM] * 3, [(1, k, cells), (k...  1.53 us
  transfers between devices with their start and end apart: 18, of which 11 were waited for; matrix products, arithmetic and copies ran while one was open for 0% of the time, Pallas kernels for 12%

profile of v4, /device:TPU:0, one launch (start us, length us, event | category | flops | bytes accessed | tf_op | source)
XLA Modules:
  0.0 66.6 jit_solution(5635182072720763699)
XLA Ops:
  0.6 6.1 %shard_map.119 = (f32[16,768]{1,0:T(8,128)S(1)}, bf16[32,512]{1,0:T(8,128)(2,1)S(1)}, f32[5120,512]{1,0:T(8,128)S(1)}, bf16[2560,512]{1,0:T(8,128)(2,1)S(1)}, bf...) custom-call(f32[1,16,5120]{2,1,0:T(8,128)} %z_ref.1, f32[16,512]{1,0:T(8,128)} %bitcast.4, ...), custom_call_target="tpu_custom_call" | custom-call | tf_op jit(solution)/shard_map/pallas_call | solution.py:442
  6.8 1.5 %shard_map.121 = f32[16,2560]{1,0:T(8,128)S(1)} custom-call(bf16[32,512]{1,0:T(8,128)(2,1)S(1)} %get-tuple-element.39.lg_ref, bf16[2560,512]{1,0:T(8,128)(2,1)S(1)} %get-tuple-element.42.rh_ref, bf16[2560,512]{1,0:T(8,128)(2,1)S(1)} %get-tuple-element.43.rl_ref), custom_call_target="tpu_custom_call" | custom-call | tf_op jit(solution)/shard_map/pallas_call | solution.py:459
  8.8 1.5 %shard_map.120 = f32[16,2560]{1,0:T(8,128)S(1)} custom-call(bf16[32,512]{1,0:T(8,128)(2,1)S(1)} %get-tuple-element.39.lg_ref, bf16[2560,512]{1,0:T(8,128)(2,1)S(1)} %get-tuple-element.40.rh_ref, bf16[2560,512]{1,0:T(8,128)(2,1)S(1)} %get-tuple-element.41.rl_ref), custom_call_target="tpu_custom_call" | custom-call | tf_op jit(solution)/shard_map/pallas_call | solution.py:459
  10.3 2.6 %collective-permute-start.1 = (f32[16,2560]{1,0:T(8,128)S(1)}, f32[16,2560]{1,0:T(8,128)S(1)}, u32[]{:S(2)}, u32[]{:S(2)}) collective-permute-start(f32[16,2560]{1,0:T(8,128)S(1)} %add.24.own_ref), channel_id=1, source_target_pairs={{0,2},{1,3},{2,0},{3,1},{4,6},{5,7},{6,4},{7,5},{8,10},{9,11},{10,... | collective-permute-start | bytes 491528 | tf_op jit(solution)/shard_map/ppermute | solution.py:27
  12.9 1.5 %collective-permute-start.2 = (f32[16,768]{1,0:T(8,128)S(1)}, f32[16,768]{1,0:T(8,128)S(1)}, u32[]{:S(2)}, u32[]{:S(2)}) collective-permute-start(f32[16,768]{1,0:T(8,128)S(1)} %get-tuple-element.47.own_ref), channel_id=1, source_target_pairs={{0,4},{4,0},{8,12},{12,8},{16,20},{20,16},{24,28},{28,24},{1,5},{5... | collective-permute-start | bytes 147464 | tf_op jit(solution)/shard_map/ppermute | solution.py:27
  14.4 2.6 %collective-permute-done.2.got_ref.refs_0_ = f32[16,768]{1,0:T(8,128)S(1)} collective-permute-done((f32[16,768]{1,0:T(8,128)S(1)}, f32[16,768]{1,0:T(8,128)S(1)}, u32[]{:S(2)}, u32[]{:S(2)}) %collective-permute-start.2) | collective-permute-done | bytes 49184 | tf_op jit(solution)/shard_map/ppermute | solution.py:27
  17.0 1.6 %collective-permute-start.3 = (f32[16,640]{1,0:T(8,128)S(1)}, f32[16,640]{1,0:T(8,128)S(1)}, u32[]{:S(2)}, u32[]{:S(2)}) collective-permute-start(f32[16,640]{1,0:T(8,128)S(1)} %shard_map.123.refs_0_), channel_id=1, source_target_pairs={{0,8},{4,12},{8,0},{12,4},{16,24},{20,28},{24,16},{28,20},{1,9},{5... | collective-permute-start | bytes 122888 | tf_op jit(solution)/shard_map/ppermute | solution.py:27
  18.6 2.4 %collective-permute-done.3.refs_1_ = f32[16,640]{1,0:T(8,128)S(1)} collective-permute-done((f32[16,640]{1,0:T(8,128)S(1)}, f32[16,640]{1,0:T(8,128)S(1)}, u32[]{:S(2)}, u32[]{:S(2)}) %collective-permute-start.3) | collective-permute-done | bytes 40992 | tf_op jit(solution)/shard_map/ppermute | solution.py:27
  21.1 3.7 %collective-permute-start.4 = (f32[16,640]{1,0:T(8,128)S(1)}, f32[16,640]{1,0:T(8,128)S(1)}, u32[]{:S(2)}, u32[]{:S(2)}) collective-permute-start(f32[16,640]{1,0:T(8,128)S(1)} %shard_map.124.refs_0_), channel_id=1, source_target_pairs={{0,24},{4,28},{8,16},{12,20},{16,8},{20,12},{24,0},{28,4},{1,25},{... | collective-permute-start | bytes 122888 | tf_op jit(solution)/shard_map/ppermute | solution.py:27
  25.8 1.1 %collective-permute-done.4.refs_2_.refs_1_ = f32[16,640]{1,0:T(8,128)S(1)} collective-permute-done((f32[16,640]{1,0:T(8,128)S(1)}, f32[16,640]{1,0:T(8,128)S(1)}, u32[]{:S(2)}, u32[]{:S(2)}) %collective-permute-start.4) | collective-permute-done | bytes 40992 | tf_op jit(solution)/shard_map/ppermute | solution.py:27
  28.7 2.5 %shard_map.129 = (f32[16,2560]{1,0:T(8,128)S(1)}, f32[8,512]{1,0:T(8,128)S(1)}, bf16[2560,512]{1,0:T(8,128)(2,1)S(1)}, bf16[2560,512]{1,0:T(8,128)(2,1)S(1)}) custom-call(f32[16,2560]{1,0:T(8,128)S(1)} %collective-permute-done.5.oth_ref.z_ref.zo_ref, bf16[96,512]{1,0:T(8,128)(2,1)S(1)} %get-tuple-element.51.ly_ref, ...), custom_call_target="tpu_custom_call" | custom-call | tf_op jit(solution)/shard_map/pallas_call | solution.py:484
  31.4 2.5 %shard_map.128 = (f32[16,2560]{1,0:T(8,128)S(1)}, f32[8,512]{1,0:T(8,128)S(1)}, bf16[2560,512]{1,0:T(8,128)(2,1)S(1)}, bf16[2560,512]{1,0:T(8,128)(2,1)S(1)}) custom-call(f32[16,2560]{1,0:T(8,128)S(1)} %get-tuple-element.48.own_ref.z_ref.zw_ref, bf16[96,512]{1,0:T(8,128)(2,1)S(1)} %get-tuple-element.51.ly_ref, bf16[32,512]{1,0:T(8,128)(2,1)S(1)} %get-tuple-element.52.lg_ref, ...), custom_call_target="tpu_custom_call" | custom-call | tf_op jit(solution)/shard_map/pallas_call | solution.py:484
  33.9 1.6 %shard_map.131.own_ref = f32[24,768]{1,0:T(8,128)S(1)} custom-call(f32[16,2560]{1,0:T(8,128)S(1)} %collective-permute-done.5.oth_ref.z_ref.zo_ref, bf16[2560,512]{1,0:T(8,128)(2,1)S(1)} %get-tuple-element.59.rho_ref, bf16[2560,512]{1,0:T(8,128)(2,1)S(1)} %get-tuple-element.60.rlo_ref, f32[16,2560]{1,0:T(8,128)S(1)} %get-tuple-element.48.own_ref.z_ref.zw_ref, ...), custom_call_target="tpu_custom_call" | custom-call | tf_op jit(solution)/shard_map/pallas_call | solution.py:493
  35.5 1.5 %collective-permute-start.8 = (f32[24,768]{1,0:T(8,128)S(1)}, f32[24,768]{1,0:T(8,128)S(1)}, u32[]{:S(2)}, u32[]{:S(2)}) collective-permute-start(f32[24,768]{1,0:T(8,128)S(1)} %shard_map.131.own_ref), channel_id=1, source_target_pairs={{0,4},{4,0},{8,12},{12,8},{16,20},{20,16},{24,28},{28,24},{1,5},{5... | collective-permute-start | bytes 221192 | tf_op jit(solution)/shard_map/ppermute | solution.py:27
  37.7 2.4 %collective-permute-done.8.got_ref.refs_0_ = f32[24,768]{1,0:T(8,128)S(1)} collective-permute-done((f32[24,768]{1,0:T(8,128)S(1)}, f32[24,768]{1,0:T(8,128)S(1)}, u32[]{:S(2)}, u32[]{:S(2)}) %collective-permute-start.8) | collective-permute-done | bytes 73760 | tf_op jit(solution)/shard_map/ppermute | solution.py:27
  40.2 4.2 %collective-permute-done.9.refs_1_ = f32[24,640]{1,0:T(8,128)S(1)} collective-permute-done((f32[24,640]{1,0:T(8,128)S(1)}, f32[24,640]{1,0:T(8,128)S(1)}, u32[]{:S(2)}, u32[]{:S(2)}) %collective-permute-start.9) | collective-permute-done | bytes 61472 | tf_op jit(solution)/shard_map/ppermute | solution.py:27
  44.4 3.7 %collective-permute-start.10 = (f32[24,640]{1,0:T(8,128)S(1)}, f32[24,640]{1,0:T(8,128)S(1)}, u32[]{:S(2)}, u32[]{:S(2)}) collective-permute-start(f32[24,640]{1,0:T(8,128)S(1)} %shard_map.133.refs_0_), channel_id=1, source_target_pairs={{0,24},{4,28},{8,16},{12,20},{16,8},{20,12},{24,0},{28,4},{1,25},{... | collective-permute-start | bytes 184328 | tf_op jit(solution)/shard_map/ppermute | solution.py:27
  48.4 2.1 %collective-permute-done.10.refs_2_.refs_1_ = f32[24,640]{1,0:T(8,128)S(1)} collective-permute-done((f32[24,640]{1,0:T(8,128)S(1)}, f32[24,640]{1,0:T(8,128)S(1)}, u32[]{:S(2)}, u32[]{:S(2)}) %collective-permute-start.10) | collective-permute-done | bytes 61472 | tf_op jit(solution)/shard_map/ppermute | solution.py:27
  50.7 1.6 %collective-permute-start.13 = (f32[8,128]{1,0:T(8,128)S(1)}, f32[8,128]{1,0:T(8,128)S(1)}, u32[]{:S(2)}, u32[]{:S(2)}) collective-permute-start(f32[8,128]{1,0:T(8,128)S(1)} %get-tuple-element.72), channel_id=1, source_target_pairs={{0,4},{4,0},{8,12},{12,8},{16,20},{20,16},{24,28},{28,24},{1,5},{5... | collective-permute-start | bytes 12296 | tf_op jit(solution)/shard_map/ppermute | solution.py:27
  52.9 1.5 %collective-permute-done.13 = f32[8,128]{1,0:T(8,128)S(1)} collective-permute-done((f32[8,128]{1,0:T(8,128)S(1)}, f32[8,128]{1,0:T(8,128)S(1)}, u32[]{:S(2)}, u32[]{:S(2)}) %collective-permute-start.13) | collective-permute-done | bytes 4128 | tf_op jit(solution)/shard_map/ppermute | solution.py:27
  54.4 4.2 %collective-permute-start.15 = (f32[8,128]{1,0:T(8,128)S(1)}, f32[8,128]{1,0:T(8,128)S(1)}, u32[]{:S(2)}, u32[]{:S(2)}) collective-permute-start(f32[8,128]{1,0:T(8,128)S(1)} %add.27), channel_id=1, source_target_pairs={{0,16},{4,20},{8,24},{12,28},{16,0},{20,4},{24,8},{28,12},{1,17},{... | collective-permute-start | bytes 12296 | tf_op jit(solution)/shard_map/ppermute | solution.py:27
  58.8 1.4 %collective-permute-done.15 = f32[8,128]{1,0:T(8,128)S(1)} collective-permute-done((f32[8,128]{1,0:T(8,128)S(1)}, f32[8,128]{1,0:T(8,128)S(1)}, u32[]{:S(2)}, u32[]{:S(2)}) %collective-permute-start.15) | collective-permute-done | bytes 4128 | tf_op jit(solution)/shard_map/ppermute | solution.py:27
  60.2 3.8 %collective-permute-done.16 = f32[8,128]{1,0:T(8,128)S(1)} collective-permute-done((f32[8,128]{1,0:T(8,128)S(1)}, f32[8,128]{1,0:T(8,128)S(1)}, u32[]{:S(2)}, u32[]{:S(2)}) %collective-permute-start.16) | collective-permute-done | bytes 4128 | tf_op jit(solution)/shard_map/ppermute | solution.py:27
  64.0 0.8 %shard_map.127 = (f32[1,16,5120]{2,1,0:T(8,128)}, f32[16,512]{1,0:T(8,128)}) custom-call(f32[16,2560]{1,0:T(8,128)S(1)} %get-tuple-element.48.own_ref.z_ref.zw_ref, f32[16,2560]{1,0:T(8,128)S(1)} %collective-permute-done.5.oth_ref.z_ref.zo_ref, f32[16,512]{1,0:T(8,128)S(1)} %get-tuple-element.49.loadings_ref.refs_2_), custom_call_target="tpu_custom_call" | custom-call | tf_op jit(solution)/shard_map/pallas_call | solution.py:480
  (47 shorter events, 6.2 us)
Async XLA Ops:
  8.3 2.0 %collective-permute-start = (f32[16,2560]{1,0:T(8,128)S(1)}, f32[16,2560]{1,0:T(8,128)S(1)}, u32[]{:S(2)}, u32[]{:S(2)}) collective-permute-start(f32[16,2560]{1,0:T(8,128)S(1)} %shard_map.121), channel_id=1, source_target_pairs={{0,1},{1,0},{2,3},{3,2},{4,5},{5,4},{6,7},{7,6},{8,9},{9,8},{10,11... | collective-permute-start | bytes 491528 | tf_op jit(solution)/shard_map/ppermute | solution.py:27
  8.8 16.6 %copy-start.4 = (f32[16]{0:T(128)S(1)}, f32[16]{0:T(128)}, u32[]{:S(2)}) copy-start(f32[16]{0:T(128)} %param.13) | copy-start | bytes 196
  8.8 16.7 %copy-start = (f32[1,16,5120]{2,1,0:T(8,128)S(1)}, f32[1,16,5120]{2,1,0:T(8,128)}, u32[]{:S(2)}) copy-start(f32[1,16,5120]{2,1,0:T(8,128)} %z_ref.1) | copy-start | bytes 983044
  8.8 16.7 %copy-start.1 = (f32[1,16,5120]{2,1,0:T(8,128)S(1)}, f32[1,16,5120]{2,1,0:T(8,128)}, u32[]{:S(2)}) copy-start(f32[1,16,5120]{2,1,0:T(8,128)} %mom_ref.1) | copy-start | bytes 983044
  8.8 19.1 %copy-start.2 = (f32[512,16]{0,1:T(8,128)S(1)}, f32[512,16]{0,1:T(8,128)}, u32[]{:S(2)}) copy-start(f32[512,16]{0,1:T(8,128)} %param.10) | copy-start | bytes 98308
  8.8 19.2 %copy-start.3 = (f32[512,16]{0,1:T(8,128)S(1)}, f32[512,16]{0,1:T(8,128)}, u32[]{:S(2)}) copy-start(f32[512,16]{0,1:T(8,128)} %param.12) | copy-start | bytes 98308
  10.3 16.6 %collective-permute-start.1 = (f32[16,2560]{1,0:T(8,128)S(1)}, f32[16,2560]{1,0:T(8,128)S(1)}, u32[]{:S(2)}, u32[]{:S(2)}) collective-permute-start(f32[16,2560]{1,0:T(8,128)S(1)} %add.24.own_ref), channel_id=1, source_target_pairs={{0,2},{1,3},{2,0},{3,1},{4,6},{5,7},{6,4},{7,5},{8,10},{9,11},{10,... | collective-permute-start | bytes 491528 | tf_op jit(solution)/shard_map/ppermute | solution.py:27
  12.9 4.1 %collective-permute-start.2 = (f32[16,768]{1,0:T(8,128)S(1)}, f32[16,768]{1,0:T(8,128)S(1)}, u32[]{:S(2)}, u32[]{:S(2)}) collective-permute-start(f32[16,768]{1,0:T(8,128)S(1)} %get-tuple-element.47.own_ref), channel_id=1, source_target_pairs={{0,4},{4,0},{8,12},{12,8},{16,20},{20,16},{24,28},{28,24},{1,5},{5... | collective-permute-start | bytes 147464 | tf_op jit(solution)/shard_map/ppermute | solution.py:27
  17.0 4.1 %collective-permute-start.3 = (f32[16,640]{1,0:T(8,128)S(1)}, f32[16,640]{1,0:T(8,128)S(1)}, u32[]{:S(2)}, u32[]{:S(2)}) collective-permute-start(f32[16,640]{1,0:T(8,128)S(1)} %shard_map.123.refs_0_), channel_id=1, source_target_pairs={{0,8},{4,12},{8,0},{12,4},{16,24},{20,28},{24,16},{28,20},{1,9},{5... | collective-permute-start | bytes 122888 | tf_op jit(solution)/shard_map/ppermute | solution.py:27
  21.1 5.9 %collective-permute-start.4 = (f32[16,640]{1,0:T(8,128)S(1)}, f32[16,640]{1,0:T(8,128)S(1)}, u32[]{:S(2)}, u32[]{:S(2)}) collective-permute-start(f32[16,640]{1,0:T(8,128)S(1)} %shard_map.124.refs_0_), channel_id=1, source_target_pairs={{0,24},{4,28},{8,16},{12,20},{16,8},{20,12},{24,0},{28,4},{1,25},{... | collective-permute-start | bytes 122888 | tf_op jit(solution)/shard_map/ppermute | solution.py:27
  27.2 1.5 %collective-permute-start.5 = (f32[16,2560]{1,0:T(8,128)S(1)}, f32[16,2560]{1,0:T(8,128)S(1)}, u32[]{:S(2)}, u32[]{:S(2)}) collective-permute-start(f32[16,2560]{1,0:T(8,128)S(1)} %get-tuple-element.48.own_ref.z_ref.zw_ref), channel_id=1, source_target_pairs={{0,1},{1,0},{2,3},{3,2},{4,5},{5,4},{6,7},{7,6},{8,9},{9,8},{10,11... | collective-permute-start | bytes 491528 | tf_op jit(solution)/shard_map/ppermute | solution.py:27
  31.2 5.8 %collective-permute-start.6 = (f32[16,2560]{1,0:T(8,128)S(1)}, f32[16,2560]{1,0:T(8,128)S(1)}, u32[]{:S(2)}, u32[]{:S(2)}) collective-permute-start(f32[16,2560]{1,0:T(8,128)S(1)} %get-tuple-element.55), channel_id=1, source_target_pairs={{0,1},{1,0},{2,3},{3,2},{4,5},{5,4},{6,7},{7,6},{8,9},{9,8},{10,11... | collective-permute-start | bytes 491528 | tf_op jit(solution)/shard_map/ppermute | solution.py:27
  35.5 4.6 %collective-permute-start.8 = (f32[24,768]{1,0:T(8,128)S(1)}, f32[24,768]{1,0:T(8,128)S(1)}, u32[]{:S(2)}, u32[]{:S(2)}) collective-permute-start(f32[24,768]{1,0:T(8,128)S(1)} %shard_map.131.own_ref), channel_id=1, source_target_pairs={{0,4},{4,0},{8,12},{12,8},{16,20},{20,16},{24,28},{28,24},{1,5},{5... | collective-permute-start | bytes 221192 | tf_op jit(solution)/shard_map/ppermute | solution.py:27
  37.1 13.4 %collective-permute-start.7 = (f32[16,2560]{1,0:T(8,128)S(1)}, f32[16,2560]{1,0:T(8,128)S(1)}, u32[]{:S(2)}, u32[]{:S(2)}) collective-permute-start(f32[16,2560]{1,0:T(8,128)S(1)} %add.25.own_ref), channel_id=1, source_target_pairs={{0,2},{1,3},{2,0},{3,1},{4,6},{5,7},{6,4},{7,5},{8,10},{9,11},{10,... | collective-permute-start | bytes 491528 | tf_op jit(solution)/shard_map/ppermute | solution.py:27
  40.1 4.3 %collective-permute-start.9 = (f32[24,640]{1,0:T(8,128)S(1)}, f32[24,640]{1,0:T(8,128)S(1)}, u32[]{:S(2)}, u32[]{:S(2)}) collective-permute-start(f32[24,640]{1,0:T(8,128)S(1)} %shard_map.132.refs_0_), channel_id=1, source_target_pairs={{0,8},{4,12},{8,0},{12,4},{16,24},{20,28},{24,16},{28,20},{1,9},{5... | collective-permute-start | bytes 184328 | tf_op jit(solution)/shard_map/ppermute | solution.py:27
  44.4 6.1 %collective-permute-start.10 = (f32[24,640]{1,0:T(8,128)S(1)}, f32[24,640]{1,0:T(8,128)S(1)}, u32[]{:S(2)}, u32[]{:S(2)}) collective-permute-start(f32[24,640]{1,0:T(8,128)S(1)} %shard_map.133.refs_0_), channel_id=1, source_target_pairs={{0,24},{4,28},{8,16},{12,20},{16,8},{20,12},{24,0},{28,4},{1,25},{... | collective-permute-start | bytes 184328 | tf_op jit(solution)/shard_map/ppermute | solution.py:27
  50.7 3.7 %collective-permute-start.13 = (f32[8,128]{1,0:T(8,128)S(1)}, f32[8,128]{1,0:T(8,128)S(1)}, u32[]{:S(2)}, u32[]{:S(2)}) collective-permute-start(f32[8,128]{1,0:T(8,128)S(1)} %get-tuple-element.72), channel_id=1, source_target_pairs={{0,4},{4,0},{8,12},{12,8},{16,20},{20,16},{24,28},{28,24},{1,5},{5... | collective-permute-start | bytes 12296 | tf_op jit(solution)/shard_map/ppermute | solution.py:27
  52.3 6.5 %collective-permute-start.12 = (f32[8,128]{1,0:T(8,128)S(1)}, f32[8,128]{1,0:T(8,128)S(1)}, u32[]{:S(2)}, u32[]{:S(2)}) collective-permute-start(f32[8,128]{1,0:T(8,128)S(1)} %get-tuple-element.71), channel_id=1, source_target_pairs={{0,2},{1,3},{2,0},{3,1},{4,6},{5,7},{6,4},{7,5},{8,10},{9,11},{10,... | collective-permute-start | bytes 12296 | tf_op jit(solution)/shard_map/ppermute | solution.py:27
  54.4 4.4 %collective-permute-start.14 = (f32[8,128]{1,0:T(8,128)S(1)}, f32[8,128]{1,0:T(8,128)S(1)}, u32[]{:S(2)}, u32[]{:S(2)}) collective-permute-start(f32[8,128]{1,0:T(8,128)S(1)} %add.27), channel_id=1, source_target_pairs={{0,8},{4,12},{8,0},{12,4},{16,24},{20,28},{24,16},{28,20},{1,9},{5... | collective-permute-start | bytes 12296 | tf_op jit(solution)/shard_map/ppermute | solution.py:27
  54.4 5.8 %collective-permute-start.15 = (f32[8,128]{1,0:T(8,128)S(1)}, f32[8,128]{1,0:T(8,128)S(1)}, u32[]{:S(2)}, u32[]{:S(2)}) collective-permute-start(f32[8,128]{1,0:T(8,128)S(1)} %add.27), channel_id=1, source_target_pairs={{0,16},{4,20},{8,24},{12,28},{16,0},{20,4},{24,8},{28,12},{1,17},{... | collective-permute-start | bytes 12296 | tf_op jit(solution)/shard_map/ppermute | solution.py:27
  58.6 5.4 %collective-permute-start.16 = (f32[8,128]{1,0:T(8,128)S(1)}, f32[8,128]{1,0:T(8,128)S(1)}, u32[]{:S(2)}, u32[]{:S(2)}) collective-permute-start(f32[8,128]{1,0:T(8,128)S(1)} %add.27), channel_id=1, source_target_pairs={{0,24},{4,28},{8,16},{12,20},{16,8},{20,12},{24,0},{28,4},{1,25},{... | collective-permute-start | bytes 12296 | tf_op jit(solution)/shard_map/ppermute | solution.py:27
  58.8 7.0 %collective-permute-start.11 = (f32[16,2560]{1,0:T(8,128)S(1)}, f32[16,2560]{1,0:T(8,128)S(1)}, u32[]{:S(2)}, u32[]{:S(2)}) collective-permute-start(f32[16,2560]{1,0:T(8,128)S(1)} %get-tuple-element.65.own_ref), channel_id=1, source_target_pairs={{0,1},{1,0},{2,3},{3,2},{4,5},{5,4},{6,7},{7,6},{8,9},{9,8},{10,11... | collective-permute-start | bytes 491528 | tf_op jit(solution)/shard_map/ppermute | solution.py:27
  64.0 1.2 %collective-permute-start.17 = (f32[8,128]{1,0:T(8,128)S(1)}, f32[8,128]{1,0:T(8,128)S(1)}, u32[]{:S(2)}, u32[]{:S(2)}) collective-permute-start(f32[8,128]{1,0:T(8,128)S(1)} %add_add_fusion.own_ref), channel_id=1, source_target_pairs={{0,1},{1,0},{2,3},{3,2},{4,5},{5,4},{6,7},{7,6},{8,9},{9,8},{10,11... | collective-permute-start | bytes 12296 | tf_op jit(solution)/shard_map/ppermute | solution.py:27

commit v5 on v4

--- a/solution.py
+++ b/solution.py
@@ -68,7 +68,7 @@
     return pl.pallas_call(
         kernel,
         in_specs=in_specs,
-        out_specs=[VMEM] * len(outs),
+        out_specs=[SMEM if s == (1,) else VMEM for s in outs],
         out_shape=[jax.ShapeDtypeStruct(s, bf16 if i in packed else f32) for i, s in enumerate(outs)],
         scratch_shapes=list(scratch),
         compiler_params=pltpu.CompilerParams(vmem_limit_bytes=limit << 20),
@@ -116,6 +116,10 @@
     lg_ref[...] = jnp.concatenate([m, h], 0)
 
 
+def fold_lanes(x):
+    return add([x[:, j * LANES : (j + 1) * LANES] for j in range(x.shape[1] // LANES)])
+
+
 def rows_to_8(x):
     return jnp.sum(x.reshape(x.shape[0] // 8, 8, x.shape[1]), 0)
 
@@ -128,16 +132,17 @@
     ly_ref, z_ref, lt_ref, buf_ref, sem, sems
 ):
     c = core()
-    steps = half // sub
-    slots = DEPTH + 1
+    pieces = [(rho, at) for rho in (1, 0) for at in range(0, half, sub)]
 
     def place(i):
-        return pl.multiple_of(lax.rem((1 - i // steps) + c, 2) * half + (i % steps) * sub, sub)
+        rho, at = pieces[i]
+        return pl.multiple_of(lax.rem(rho + c, 2) * half + at, LANES)
+
+    def kept(i):
+        return pl.ds(i * sub, sub)
 
     def copy(i):
-        return pltpu.make_async_copy(
-            cnt_ref.at[0, pl.ds(place(i), sub)], buf_ref.at[pl.ds((i % slots) * sub, sub)], sem.at[i]
-        )
+        return pltpu.make_async_copy(cnt_ref.at[0, pl.ds(place(i), sub)], buf_ref.at[kept(i)], sem.at[i])
 
     small = [
         pltpu.make_async_copy(lt_hbm, lt_ref, sems.at[0]),
@@ -145,7 +150,7 @@
     ]
     for job in small:
         job.start()
-    for i in range(min(DEPTH, 2 * steps)):
+    for i in range(min(DEPTH, len(pieces))):
         copy(i).start()
     small[0].wait()
     fill_loadings(lt_ref[...], ly_ref, lg_ref)
@@ -153,19 +158,17 @@
     load_ref[:, -2 * LANES : -LANES], load_ref[:, -LANES:] = pack_rims(vregs_of(z_ref[0]), k)
     ly = ly_ref[...]
     loads = []
-    for i in range(2 * steps):
+    for i, (rho, at) in enumerate(pieces):
         copy(i).wait()
-        if i + DEPTH < 2 * steps:
+        if i + DEPTH < len(pieces):
             copy(i + DEPTH).start()
-        cf = buf_ref[pl.ds((i % slots) * sub, sub), :].astype(f32)
-        rows = pl.ds(i * sub, sub)
-        held_ref[rows, :] = cf
+        cf = buf_ref[kept(i), :].astype(f32)
+        held_ref[kept(i), :] = cf
         _, _, rh, rl, h, m = residuals(z_ref[0, :, pl.ds(place(i), sub)], cf, ly)
         loads.append(loading_terms(h, m, rh, rl, k))
-        rh_ref, rl_ref = (rho_ref, rlo_ref) if i < steps else (rhw_ref, rlw_ref)
-        rows = pl.ds((i % steps) * sub, sub)
-        rh_ref[rows, :] = rh
-        rl_ref[rows, :] = rl
+        rh_ref, rl_ref = (rho_ref, rlo_ref) if rho else (rhw_ref, rlw_ref)
+        rh_ref[pl.ds(at, sub), :] = rh
+        rl_ref[pl.ds(at, sub), :] = rl
     load_ref[:, : -2 * LANES] = add(loads)
 
 
@@ -179,7 +182,7 @@
 def move_loadings_kernel(n_terms, *refs):
     terms = refs[:n_terms]
     lt_ref, lm_ref, sl_ref, newl_ref, halfl_ref, ly_ref, lg_ref = refs[n_terms:]
-    step = sl_ref[0]
+    step = jnp.tile(sl_ref[...], (1, lt_ref.shape[1] // LANES))
     halfl = lm_ref[...] + 0.5 * step * (add([t[:, : lt_ref.shape[1]] for t in terms]) - lt_ref[...])
     newl = lt_ref[...] + step * halfl
     halfl_ref[...] = halfl
@@ -209,18 +212,22 @@
             rows = pl.ds(i * sub, sub)
             h, m, _ = split3(z_ref[:, rows])
             loads.append(loading_terms(h, m, rh_ref[rows, :], rl_ref[rows, :], k))
-    load_ref[:k, : -2 * LANES] = add(loads)
-    load_ref[k:, : -2 * LANES] = liko_ref[...] + likw_ref[...]
-    load_ref[k:, -2 * LANES :] = jnp.zeros((load_ref.shape[0] - k, 2 * LANES), f32)
-    rims = pack_rims(in_order(zw_ref[...], zo_ref[...]), k)
-    load_ref[:k, -2 * LANES : -LANES], load_ref[:k, -LANES:] = rims
+    load_ref[:, : -2 * LANES] = add(loads)
+    first, load_ref[:, -LANES:] = pack_rims(in_order(zw_ref[...], zo_ref[...]), k)
+    like = jnp.sum(fold_lanes(liko_ref[...] + likw_ref[...]), 1, keepdims=True)
+    like = jnp.concatenate([like, jnp.zeros((k - 8, 1), f32)], 0)
+    load_ref[:, -2 * LANES : -LANES] = jnp.where(lane(first.shape) == SPARE, like, first)
 
 
 def lane(shape):
     return lax.broadcasted_iota(jnp.int32, shape, len(shape) - 1)
 
 
+SPARE = TY - 1
+
+
 def pack_rims(vregs, k):
+    assert len(vregs) < TY
     q = lax.rem(lane((k, LANES)), TY)
     first = jnp.zeros((k, LANES), f32)
     last = jnp.zeros((k, LANES), f32)
@@ -260,15 +267,15 @@
     return out
 
 
-def sides(ride, refs, k):
+def sides(ride, refs):
     me, n = lax.axis_index("site"), lax.axis_size("site")
     even = lax.rem(me, 2) == 0
     if ride:
-        pair, one, three = refs
-        near = jnp.where(even, pair[:k, -2 * LANES : -LANES], pair[:k, -LANES:])
+        pair, one, two = refs
+        near = jnp.where(even, pair[:, -2 * LANES : -LANES], pair[:, -LANES:])
         row = me // 2
         close = (lax.rem(row, 2) == 1) == even
-        far = jnp.where(close, one[:k, -LANES:], three[:k, -LANES:])
+        far = jnp.where(close, one[:, -2 * LANES : -LANES], two[:, -LANES:])
     else:
         near, far = refs[0][...], refs[1][...]
     left = jnp.where(me == 0, 0.0, jnp.where(even, far, near))
@@ -290,19 +297,28 @@
     near_ref[...], far_ref[...] = rims_of(vregs_of(z_ref[0]), k)
 
 
-def stage_kernel(near, own_ref, got_ref, *refs):
-    *sums, out_ref = refs
-    a, b = sums if sums else (own_ref, got_ref)
-    width = own_ref.shape[1] - 2 * LANES
-    out_ref[:, :width] = a[:, :width] + b[:, :width]
+def pair_stage_kernel(own_ref, got_ref, out_ref):
     site = lax.axis_index("site")
+    out_ref[:, : -2 * LANES] = own_ref[:, : -2 * LANES] + got_ref[:, : -2 * LANES]
     even = lax.rem(site, 2) == 0
-    first = jnp.where(even, own_ref[:, -2 * LANES : -LANES], got_ref[:, -2 * LANES : -LANES])
+    own_first, got_first = own_ref[:, -2 * LANES : -LANES], got_ref[:, -2 * LANES : -LANES]
+    first = jnp.where(even, own_first, got_first)
     last = jnp.where(even, got_ref[:, -LANES:], own_ref[:, -LANES:])
-    out_ref[:, width:] = jnp.where((lax.rem(site // 2, 2) == 0) == near, last, first)
-
-
-def ahead_kernel(k, half, z_ref, mom_ref, upper_ref, lower_ref, gain_ref, sf_ref, a_ref, z_own_ref, s_ref):
+    low = lax.rem(site // 2, 2) == 0
+    spare = lane(first.shape) == SPARE
+    out_ref[:, -2 * LANES : -LANES] = jnp.where(spare, own_first + got_first, jnp.where(low, last, first))
+    out_ref[:, -LANES:] = jnp.where(low, first, last)
+
+
+def row_stage_kernel(own_ref, got_ref, out_ref):
+    wide = slice(None), slice(0, own_ref.shape[1] - LANES)
+    both = own_ref[wide] + got_ref[wide]
+    out_ref[:, :-LANES] = both[:, :-LANES]
+    rim = both[:, -LANES:]
+    out_ref[:, -LANES:] = jnp.where(lane(rim.shape) == SPARE, rim, got_ref[:, -LANES:])
+
+
+def ahead_kernel(k, half, z_ref, mom_ref, upper_ref, lower_ref, gain_ref, sf_ref, sl_ref, a_ref, z_own_ref, s_ref, l_ref):
     c = core()
     step = sf_ref[0]
     out = prior_of(vregs_of(z_ref[0]), upper_ref[...], lower_ref[...], k)
@@ -315,11 +331,12 @@
         a_ref[:, at] = mom_ref[0, :, src] - gain * own
         z_own_ref[:, at] = z_ref[0, :, src]
     s_ref[...] = jnp.full(s_ref.shape, step, f32)
+    l_ref[...] = jnp.full(l_ref.shape, sl_ref[0], f32)
 
 
 def move_kernel(ride, k, half, own_ref, other_ref, a_ref, z_ref, s_ref, gain_ref, *refs):
     *halo, half_ref, moved_ref = refs
-    beside = beside_of(*sides(ride, halo, k), half, k)
+    beside = beside_of(*sides(ride, halo), half, k)
     step, gain = s_ref[...], gain_ref[...]
     for j in range(half // LANES):
         at = pl.ds(j * LANES, LANES)
@@ -352,9 +369,11 @@
     e_ref[...] = energy
 
 
-def end_kernel(ride, k, half, own_ref, other_ref, a_ref, z_ref, s_ref, gain_ref, pe_ref, *refs):
-    *halo, end_ref, b_ref = refs
-    beside = beside_of(*sides(ride, halo, k), half, k)
+def finish_kernel(ride, k, half, n_terms, shares, *refs):
+    terms = refs[:n_terms]
+    own_ref, other_ref, a_ref, z_ref, s_ref, gain_ref, pe_ref, newl_ref, halfl_ref, sl_ref = refs[n_terms : n_terms + 10]
+    *halo, end_ref, endl_ref, share_ref = refs[n_terms + 10 :]
+    beside = beside_of(*sides(ride, halo), half, k)
     step, gain = s_ref[...], gain_ref[...]
     energy = pe_ref[...]
     for j in range(half // LANES):
@@ -363,10 +382,19 @@
         e = a_ref[:, at] + (0.5 * step) * ((own_ref[:, at] + other_ref[:, at]) + rim)
         end_ref[:, at] = e
         energy = energy + (e * e - z_ref[:, at] * rim)
-    b_ref[...] = 0.5 * sum(energy[g * 8 : (g + 1) * 8] for g in range(k // 8))
-
-
-def pair_kernel(half, own_ref, oth_ref, loadings_ref, full_ref, out_ref):
+    newl = newl_ref[...]
+    species = newl.shape[1]
+    load = add([t[:, :species] for t in terms])
+    step = jnp.tile(sl_ref[...], (1, species // LANES))
+    endl = halfl_ref[...] + (0.5 * step) * (load - newl)
+    endl_ref[...] = endl
+    rim = add([t[:, species : species + LANES] for t in terms])
+    loadings = 0.5 * fold_lanes(endl * endl + newl * newl) + jnp.where(lane(rim.shape) == SPARE, rim, 0.0)
+    share = jnp.sum((0.5 / shares[0]) * energy + (1.0 / shares[1]) * loadings, 0, keepdims=True)
+    share_ref[...] = jnp.broadcast_to(share, share_ref.shape)
+
+
+def output_kernel(half, own_ref, oth_ref, loadings_ref, full_ref, out_ref):
     c = core()
     own, oth = own_ref[...], oth_ref[...]
     full_ref[0, :, :half] = jnp.where(c == 0, own, oth)
@@ -374,20 +402,9 @@
     out_ref[...] = loadings_ref[...]
 
 
-def energy_kernel(entries, own_ref, got_ref, out_ref):
-    out_ref[0] = jnp.sum(own_ref[...] + got_ref[...]) / entries
-
-
-def loading_end_kernel(k, n_terms, *refs):
-    terms = refs[:n_terms]
-    newl_ref, halfl_ref, sl_ref, end_ref, s_ref = refs[n_terms:]
-    newl = newl_ref[...]
-    total = add([t[:, : newl.shape[1]] for t in terms])
-    end = halfl_ref[...] + (0.5 * sl_ref[0]) * (total[:k] - newl)
-    end_ref[...] = end
-    squares = 0.5 * (end * end + newl * newl)
-    energy = total[k:] + sum(squares[g * 8 : (g + 1) * 8] for g in range(k // 8))
-    s_ref[...] = sum(energy[:, j * LANES : (j + 1) * LANES] for j in range(energy.shape[1] // LANES))
+def last_kernel(half, entries, own_ref, oth_ref, loadings_ref, shares_ref, full_ref, out_ref, energy_ref):
+    output_kernel(half, own_ref, oth_ref, loadings_ref, full_ref, out_ref)
+    energy_ref[0] = jnp.sum(shares_ref[...]) / entries
 
 
 def local(
@@ -408,17 +425,11 @@
     def exchange(load):
         if not ride:
             return sum_terms(load, "site", site), ()
-        shape = (load.shape[0], species + LANES)
-
-        def stage(near, *args):
-            kernel = functools.partial(stage_kernel, near)
-            return call(kernel, [VMEM] * len(args), [shape])(*args)[0]
-
         got = swap(load, "site", 1)
-        two = stage(True, load, got)
+        (two,) = call(pair_stage_kernel, [VMEM] * 2, [load.shape])(load, got)
         got_two = swap(two, "site", 2)
-        four = stage(False, load, got, two, got_two)
-        got_four = swap(four, "site", 6)
+        (four,) = call(row_stage_kernel, [VMEM] * 2, [(k, species + LANES)])(two, got_two)
+        got_four = swap(four, "site", 4)
         return [four, got_four], (got, got_two, got_four)
 
     def upright(low, high):
@@ -447,11 +458,11 @@
             pltpu.VMEM(rates, bf16),
             pltpu.VMEM((1, k, cells), f32),
             pltpu.VMEM((k, species), f32),
-            pltpu.VMEM(((DEPTH + 1) * sub, species), jnp.int32),
+            pltpu.VMEM((cells, species), jnp.int32),
             pltpu.SemaphoreType.DMA((cells // sub,)),
             pltpu.SemaphoreType.DMA((2,)),
         ],
-        12,
+        16,
         (1, 3, 4, 5, 6),
     )(*[pltpu.with_memory_space_constraint(x, pltpu.HBM) for x in (factors, lt, counts)])
     load_terms, halo = exchange(load)
@@ -463,9 +474,11 @@
 
     halo = sideways(rims_kernel, halo, factors)
     edges = upright(factors[0, :, :TY], factors[0, :, cells - TY :])
-    a1, z_own, svec = call(
-        functools.partial(ahead_kernel, k, half), [VMEM] * 5 + [SMEM], [(k, half), (k, half), (k, LANES)]
-    )(factors, factor_momenta, *edges, gain, factor_step)
+    a1, z_own, svec, lvec = call(
+        functools.partial(ahead_kernel, k, half),
+        [VMEM] * 5 + [SMEM] * 2,
+        [(k, half), (k, half), (k, LANES), (k, LANES)],
+    )(factors, factor_momenta, *edges, gain, factor_step, loading_step)
     half_own, moved_own = call(
         functools.partial(move_kernel, ride, k, half), [VMEM] * (6 + len(halo)), [(k, half)] * 2
     )(own, other, a1, z_own, svec, gain, *halo)
@@ -473,12 +486,12 @@
 
     newl, halfl, ly, lg = call(
         functools.partial(move_loadings_kernel, len(load_terms)),
-        [VMEM] * (len(load_terms) + 2) + [SMEM],
+        [VMEM] * (len(load_terms) + 3),
         [(k, species)] * 2 + [rates, grads],
         packed=(2, 3),
-    )(*load_terms, lt, lm, loading_step)
+    )(*load_terms, lt, lm, lvec)
     new_factors, new_loadings = call(
-        functools.partial(pair_kernel, half), [VMEM] * 3, [(1, k, cells), (k, species)]
+        functools.partial(output_kernel, half), [VMEM] * 3, [(1, k, cells), (k, species)]
     )(moved_own, moved_oth, newl)
     (own, lik_own, *parts_own), (oth, lik_oth, *parts_oth) = [
         call(
@@ -490,7 +503,7 @@
         )(z, ly, lg, held)
         for start, z in ((half, moved_own), (0, moved_oth))
     ]
-    (load,) = call(functools.partial(loading_kernel, k, half, sub), [VMEM] * 8, [(k + 8, species + 2 * LANES)])(
+    (load,) = call(functools.partial(loading_kernel, k, half, sub), [VMEM] * 8, [(k, species + 2 * LANES)])(
         moved_oth, *parts_oth, moved_own, *parts_own, lik_oth, lik_own
     )
     load_terms, halo = exchange(load)
@@ -501,27 +514,19 @@
     a2, prior_energy = call(
         functools.partial(behind_kernel, k, half), [VMEM] * 7, [(k, half), (k, LANES)]
     )(moved_own, moved_oth, half_own, *edges, gain, svec)
-    end_own, b_part = call(
-        functools.partial(end_kernel, ride, k, half), [VMEM] * (7 + len(halo)), [(k, half), (8, LANES)]
-    )(own, other, a2, moved_own, svec, gain, prior_energy, *halo)
+    n_devices = n_site * n_sp
+    end_own, endl, shares = call(
+        functools.partial(finish_kernel, ride, k, half, len(load_terms), (n_sp // 2, n_site)),
+        [VMEM] * (len(load_terms) + 10 + len(halo)),
+        [(k, half), (k, species), (n_devices, LANES)],
+    )(*load_terms, own, other, a2, moved_own, svec, gain, prior_energy, newl, halfl, lvec, *halo)
     end_oth = swap(end_own, "sp", 1)
-    endl, s_part = call(
-        functools.partial(loading_end_kernel, k, len(load_terms)),
-        [VMEM] * (len(load_terms) + 2) + [SMEM],
-        [(k, species), (8, LANES)],
-    )(*load_terms, newl, halfl, loading_step)
-    new_momenta, end_loadings = call(
-        functools.partial(pair_kernel, half), [VMEM] * 3, [(1, k, cells), (k, species)]
-    )(end_own, end_oth, endl)
-    total = add(sum_terms(s_part, "sp", chips) + sum_terms(b_part, "site", site))
-    energy = pl.pallas_call(
-        functools.partial(energy_kernel, n_site * cells * n_sp * species),
-        in_specs=[VMEM] * 2,
-        out_specs=SMEM,
-        out_shape=jax.ShapeDtypeStruct((1,), f32),
-        name="energy",
-        compiler_params=pltpu.CompilerParams(vmem_limit_bytes=1 << 20),
-    )(total, swap(total, "sp", 1))
+    shares = lax.all_to_all(shares, ("site", "sp"), 0, 0, tiled=True)
+    new_momenta, end_loadings, energy = call(
+        functools.partial(last_kernel, half, n_site * cells * n_sp * species),
+        [VMEM] * 4,
+        [(1, k, cells), (k, species), (1,)],
+    )(end_own, end_oth, endl, shares)
     return new_factors, new_momenta, new_loadings.T, end_loadings.T, energy
 
 

time: 66.8 us -> 63.8 us (0.955)
  waiting for transfers between devices: 22.5 us -> 19.4 us
    ppermute x18 -> x12, waiting for transfers between devices: 22.5 us -> 13.1 us  [swap(): lax.ppermute(block, axis, [(i, i ^ mask) for i in range(lax.axis_size(axi...]
    all_to_all x0 -> x1, starting transfers between devices: none -> 6.6 us  [local(): shares = lax.all_to_all(shares, ('site', 'sp'), 0, 0, tiled=True)]
    ppermute x18 -> x12, starting transfers between devices: 22.6 us -> 16.2 us  [swap(): lax.ppermute(block, axis, [(i, i ^ mask) for i in range(lax.axis_size(axi...]
    all_to_all x0 -> x1, waiting for transfers between devices: none -> 6.34 us  [local(): shares = lax.all_to_all(shares, ('site', 'sp'), 0, 0, tiled=True)]
    pallas_call x11 -> x9, Pallas kernels: 4.44 us -> 4.36 us  [the longest x1 1.57 us: local(): call(functools.partial(loading_kernel, k, half, sub), [VMEM] * 8, [(k, sp...]
  transfers between devices with their start and end apart: 18 -> 13, of which waited for: 11 -> 8; matrix products, arithmetic and copies ran while one was open for 0% -> 0% of each run, Pallas kernels for 12% -> 11%
where the time goes in v5:
time: 63.8 us; the launch traced here: 63.6 us
  starting transfers between devices  22.8 us (36%)
  waiting for transfers between devices  19.4 us (30%)
  Pallas kernels  19.1 us (30%)
  between operations  2.06 us (3%)
    ppermute x12, starting transfers between devices, swap(): lax.ppermute(block, axis, [(i, i ^ mask) for i in range(lax.axis_size(axi...  16.2 us
    ppermute x12, waiting for transfers between devices, swap(): lax.ppermute(block, axis, [(i, i ^ mask) for i in range(lax.axis_size(axi...  13.1 us
    all_to_all x1, starting transfers between devices, local(): shares = lax.all_to_all(shares, ('site', 'sp'), 0, 0, tiled=True)  6.6 us
    all_to_all x1, waiting for transfers between devices, local(): shares = lax.all_to_all(shares, ('site', 'sp'), 0, 0, tiled=True)  6.34 us
    pallas_call x1, Pallas kernels, local(): call(functools.partial(first_kernel, k, half, sub), [HBM, HBM, HBM], [(k,...  6.12 us
    pallas_call x2, Pallas kernels, local(): call(functools.partial(second_kernel, k, half, sub, start), [VMEM] * 4, [...  5.04 us
    pallas_call x2, Pallas kernels, local(): call(functools.partial(factor_kernel, k, half, sub), [VMEM] * 3, [(k, hal...  2.99 us
    pallas_call x1, Pallas kernels, local(): call(functools.partial(loading_kernel, k, half, sub), [VMEM] * 8, [(k, sp...  1.57 us
  transfers between devices with their start and end apart: 13, of which 8 were waited for; matrix products, arithmetic and copies ran while one was open for 0% of the time, Pallas kernels for 11%

profile of v5, /device:TPU:0, one launch (start us, length us, event | category | flops | bytes accessed | tf_op | source)
XLA Modules:
  0.0 63.6 jit_solution(12159197283488543640)
XLA Ops:
  0.6 6.1 %shard_map.119 = (f32[16,768]{1,0:T(8,128)S(1)}, bf16[32,512]{1,0:T(8,128)(2,1)S(1)}, f32[5120,512]{1,0:T(8,128)S(1)}, bf16[2560,512]{1,0:T(8,128)(2,1)S(1)}, bf...) custom-call(f32[1,16,5120]{2,1,0:T(8,128)} %z_ref.1, f32[16,512]{1,0:T(8,128)} %bitcast.8, ...), custom_call_target="tpu_custom_call" | custom-call | tf_op jit(solution)/shard_map/pallas_call | solution.py:453
  6.8 1.5 %shard_map.121 = f32[16,2560]{1,0:T(8,128)S(1)} custom-call(bf16[32,512]{1,0:T(8,128)(2,1)S(1)} %get-tuple-element.40.lg_ref, bf16[2560,512]{1,0:T(8,128)(2,1)S(1)} %get-tuple-element.43.rh_ref, bf16[2560,512]{1,0:T(8,128)(2,1)S(1)} %get-tuple-element.44.rl_ref), custom_call_target="tpu_custom_call" | custom-call | tf_op jit(solution)/shard_map/pallas_call | solution.py:470
  8.8 1.5 %shard_map.120 = f32[16,2560]{1,0:T(8,128)S(1)} custom-call(bf16[32,512]{1,0:T(8,128)(2,1)S(1)} %get-tuple-element.40.lg_ref, bf16[2560,512]{1,0:T(8,128)(2,1)S(1)} %get-tuple-element.41.rh_ref, bf16[2560,512]{1,0:T(8,128)(2,1)S(1)} %get-tuple-element.42.rl_ref), custom_call_target="tpu_custom_call" | custom-call | tf_op jit(solution)/shard_map/pallas_call | solution.py:470
  10.3 2.5 %collective-permute-start.1 = (f32[16,2560]{1,0:T(8,128)S(1)}, f32[16,2560]{1,0:T(8,128)S(1)}, u32[]{:S(2)}, u32[]{:S(2)}) collective-permute-start(f32[16,2560]{1,0:T(8,128)S(1)} %add.6.own_ref), channel_id=1, source_target_pairs={{0,2},{1,3},{2,0},{3,1},{4,6},{5,7},{6,4},{7,5},{8,10},{9,11},{10,... | collective-permute-start | bytes 491528 | tf_op jit(solution)/shard_map/ppermute | solution.py:27
  12.9 1.5 %collective-permute-start.2 = (f32[16,768]{1,0:T(8,128)S(1)}, f32[16,768]{1,0:T(8,128)S(1)}, u32[]{:S(2)}, u32[]{:S(2)}) collective-permute-start(f32[16,768]{1,0:T(8,128)S(1)} %get-tuple-element.48.own_ref), channel_id=1, source_target_pairs={{0,4},{4,0},{8,12},{12,8},{16,20},{20,16},{24,28},{28,24},{1,5},{5... | collective-permute-start | bytes 147464 | tf_op jit(solution)/shard_map/ppermute | solution.py:27
  14.4 2.6 %collective-permute-done.2.got_ref.refs_0_ = f32[16,768]{1,0:T(8,128)S(1)} collective-permute-done((f32[16,768]{1,0:T(8,128)S(1)}, f32[16,768]{1,0:T(8,128)S(1)}, u32[]{:S(2)}, u32[]{:S(2)}) %collective-permute-start.2) | collective-permute-done | bytes 49184 | tf_op jit(solution)/shard_map/ppermute | solution.py:27
  17.0 1.6 %collective-permute-start.3 = (f32[16,768]{1,0:T(8,128)S(1)}, f32[16,768]{1,0:T(8,128)S(1)}, u32[]{:S(2)}, u32[]{:S(2)}) collective-permute-start(f32[16,768]{1,0:T(8,128)S(1)} %shard_map.123.own_ref), channel_id=1, source_target_pairs={{0,8},{4,12},{8,0},{12,4},{16,24},{20,28},{24,16},{28,20},{1,9},{5... | collective-permute-start | bytes 147464 | tf_op jit(solution)/shard_map/ppermute | solution.py:27
  18.6 2.5 %collective-permute-done.3.got_ref.refs_1_ = f32[16,768]{1,0:T(8,128)S(1)} collective-permute-done((f32[16,768]{1,0:T(8,128)S(1)}, f32[16,768]{1,0:T(8,128)S(1)}, u32[]{:S(2)}, u32[]{:S(2)}) %collective-permute-start.3) | collective-permute-done | bytes 49184 | tf_op jit(solution)/shard_map/ppermute | solution.py:27
  21.2 2.7 %collective-permute-start.4 = (f32[16,640]{1,0:T(8,128)S(1)}, f32[16,640]{1,0:T(8,128)S(1)}, u32[]{:S(2)}, u32[]{:S(2)}) collective-permute-start(f32[16,640]{1,0:T(8,128)S(1)} %shard_map.124.refs_0_), channel_id=1, source_target_pairs={{0,16},{4,20},{8,24},{12,28},{16,0},{20,4},{24,8},{28,12},{1,17},{... | collective-permute-start | bytes 122888 | tf_op jit(solution)/shard_map/ppermute | solution.py:27
  26.5 1.3 %collective-permute-done.5.oth_ref.z_ref.zo_ref = f32[16,2560]{1,0:T(8,128)S(1)} collective-permute-done((f32[16,2560]{1,0:T(8,128)S(1)}, f32[16,2560]{1,0:T(8,128)S(1)}, u32[]{:S(2)}, u32[]{:S(2)}) %collective-permute-start.5) | collective-permute-done | bytes 163872 | tf_op jit(solution)/shard_map/ppermute | solution.py:27
  27.8 2.5 %shard_map.128 = (f32[16,2560]{1,0:T(8,128)S(1)}, f32[8,512]{1,0:T(8,128)S(1)}, bf16[2560,512]{1,0:T(8,128)(2,1)S(1)}, bf16[2560,512]{1,0:T(8,128)(2,1)S(1)}) custom-call(f32[16,2560]{1,0:T(8,128)S(1)} %collective-permute-done.5.oth_ref.z_ref.zo_ref, bf16[96,512]{1,0:T(8,128)(2,1)S(1)} %get-tuple-element.53.ly_ref, ...), custom_call_target="tpu_custom_call" | custom-call | tf_op jit(solution)/shard_map/pallas_call | solution.py:497
  30.5 2.5 %shard_map.129 = (f32[16,2560]{1,0:T(8,128)S(1)}, f32[8,512]{1,0:T(8,128)S(1)}, bf16[2560,512]{1,0:T(8,128)(2,1)S(1)}, bf16[2560,512]{1,0:T(8,128)(2,1)S(1)}) custom-call(f32[16,2560]{1,0:T(8,128)S(1)} %get-tuple-element.49.own_ref.z_ref.zw_ref.refs_5_, bf16[96,512]{1,0:T(8,128)(2,1)S(1)} %get-tuple-element.53.ly_ref, ...), custom_call_target="tpu_custom_call" | custom-call | tf_op jit(solution)/shard_map/pallas_call | solution.py:497
  33.4 1.6 %shard_map.130.own_ref = f32[16,768]{1,0:T(8,128)S(1)} custom-call(f32[16,2560]{1,0:T(8,128)S(1)} %collective-permute-done.5.oth_ref.z_ref.zo_ref, bf16[2560,512]{1,0:T(8,128)(2,1)S(1)} %get-tuple-element.56.rho_ref, bf16[2560,512]{1,0:T(8,128)(2,1)S(1)} %get-tuple-element.57.rlo_ref, f32[16,2560]{1,0:T(8,128)S(1)} %get-tuple-element.49.own_ref.z_ref.zw_ref.refs_5_, ...), custom_call_target="tpu_custom_call" | custom-call | tf_op jit(solution)/shard_map/pallas_call | solution.py:506
  35.0 1.9 %collective-permute-start.6 = (f32[16,768]{1,0:T(8,128)S(1)}, f32[16,768]{1,0:T(8,128)S(1)}, u32[]{:S(2)}, u32[]{:S(2)}) collective-permute-start(f32[16,768]{1,0:T(8,128)S(1)} %shard_map.130.own_ref), channel_id=1, source_target_pairs={{0,4},{4,0},{8,12},{12,8},{16,20},{20,16},{24,28},{28,24},{1,5},{5... | collective-permute-start | bytes 147464 | tf_op jit(solution)/shard_map/ppermute | solution.py:27
  36.8 2.3 %collective-permute-done.6.got_ref.refs_12_ = f32[16,768]{1,0:T(8,128)S(1)} collective-permute-done((f32[16,768]{1,0:T(8,128)S(1)}, f32[16,768]{1,0:T(8,128)S(1)}, u32[]{:S(2)}, u32[]{:S(2)}) %collective-permute-start.6) | collective-permute-done | bytes 49184 | tf_op jit(solution)/shard_map/ppermute | solution.py:27
  39.1 2.0 %collective-permute-start.7 = (f32[16,768]{1,0:T(8,128)S(1)}, f32[16,768]{1,0:T(8,128)S(1)}, u32[]{:S(2)}, u32[]{:S(2)}) collective-permute-start(f32[16,768]{1,0:T(8,128)S(1)} %shard_map.131.own_ref), channel_id=1, source_target_pairs={{0,8},{4,12},{8,0},{12,4},{16,24},{20,28},{24,16},{28,20},{1,9},{5... | collective-permute-start | bytes 147464 | tf_op jit(solution)/shard_map/ppermute | solution.py:27
  41.1 2.2 %collective-permute-done.7.got_ref.refs_13_ = f32[16,768]{1,0:T(8,128)S(1)} collective-permute-done((f32[16,768]{1,0:T(8,128)S(1)}, f32[16,768]{1,0:T(8,128)S(1)}, u32[]{:S(2)}, u32[]{:S(2)}) %collective-permute-start.7) | collective-permute-done | bytes 49184 | tf_op jit(solution)/shard_map/ppermute | solution.py:27
  43.3 3.0 %collective-permute-start.8 = (f32[16,640]{1,0:T(8,128)S(1)}, f32[16,640]{1,0:T(8,128)S(1)}, u32[]{:S(2)}, u32[]{:S(2)}) collective-permute-start(f32[16,640]{1,0:T(8,128)S(1)} %shard_map.132.refs_0_), channel_id=1, source_target_pairs={{0,16},{4,20},{8,24},{12,28},{16,0},{20,4},{24,8},{28,12},{1,17},{... | collective-permute-start | bytes 122888 | tf_op jit(solution)/shard_map/ppermute | solution.py:27
  46.6 1.6 %collective-permute-done.8.refs_1_.refs_14_ = f32[16,640]{1,0:T(8,128)S(1)} collective-permute-done((f32[16,640]{1,0:T(8,128)S(1)}, f32[16,640]{1,0:T(8,128)S(1)}, u32[]{:S(2)}, u32[]{:S(2)}) %collective-permute-start.8) | collective-permute-done | bytes 40992 | tf_op jit(solution)/shard_map/ppermute | solution.py:27
  48.3 0.9 %shard_map.134 = (f32[16,2560]{1,0:T(8,128)S(1)}, f32[16,512]{1,0:T(8,128)S(1)}, f32[32,128]{1,0:T(8,128)}) custom-call(f32[16,640]{1,0:T(8,128)S(1)} %shard_map.132.refs_0_, f32[16,640]{1,0:T(8,128)S(1)} %collective-permute-done.8.refs_1_.refs_14_, f32[16,2560]{1,0:T(8,128)S(1)} %add.7.refs_2_, f32[16,2560]{1,0:T(8,128)S(1)} %collective-permute-done.10.refs_3_, ...), custom_call_target="tpu_custom_call" | custom-call | tf_op jit(solution)/shard_map/pallas_call | solution.py:518
  49.1 6.6 %all-to-all-start = ((f32[32,1,128]{2,1,0:T(1,128)}), f32[32,1,128]{2,1,0:T(1,128)S(1)}, u32[]{:S(2)}, u32[]{:S(2)}) async-start(f32[32,1,128]{2,1,0:T(1,128)} %bitcast.3), calls=%async_computation | async-start | bytes 32768 | tf_op jit(solution)/shard_map/all_to_all | solution.py:524
  55.8 0.8 %shard_map.127 = (f32[1,16,5120]{2,1,0:T(8,128)}, f32[16,512]{1,0:T(8,128)}) custom-call(f32[16,2560]{1,0:T(8,128)S(1)} %get-tuple-element.49.own_ref.z_ref.zw_ref.refs_5_, f32[16,2560]{1,0:T(8,128)S(1)} %collective-permute-done.5.oth_ref.z_ref.zo_ref, f32[16,512]{1,0:T(8,128)S(1)} %get-tuple-element.51.loadings_ref.refs_9_), custom_call_target="tpu_custom_call" | custom-call | tf_op jit(solution)/shard_map/pallas_call | solution.py:493
  56.5 6.3 %all-to-all-done = f32[32,1,128]{2,1,0:T(1,128)S(1)} async-done(((f32[32,1,128]{2,1,0:T(1,128)}), f32[32,1,128]{2,1,0:T(1,128)S(1)}, u32[]{:S(2)}, u32[]{:S(2)}) %all-to-all-start) | async-done | bytes 16416 | tf_op jit(solution)/shard_map/all_to_all | solution.py:524
  62.9 0.8 %shard_map.135 = (f32[1,16,5120]{2,1,0:T(8,128)}, f32[16,512]{1,0:T(8,128)}, f32[1]{0:T(128)}) custom-call(f32[16,2560]{1,0:T(8,128)S(1)} %get-tuple-element.68.own_ref, f32[16,2560]{1,0:T(8,128)S(1)} %collective-permute-done.11.oth_ref, f32[16,512]{1,0:T(8,128)S(1)} %get-tuple-element.69.loadings_ref, f32[32,128]{1,0:T(8,128)S(1)} %bitcast.10), custom_call_target="tpu_custom_call" | custom-call | tf_op jit(solution)/shard_map/pallas_call | solution.py:525
  (33 shorter events, 2.8 us)
Async XLA Ops:
  8.3 2.0 %collective-permute-start = (f32[16,2560]{1,0:T(8,128)S(1)}, f32[16,2560]{1,0:T(8,128)S(1)}, u32[]{:S(2)}, u32[]{:S(2)}) collective-permute-start(f32[16,2560]{1,0:T(8,128)S(1)} %shard_map.121), channel_id=1, source_target_pairs={{0,1},{1,0},{2,3},{3,2},{4,5},{5,4},{6,7},{7,6},{8,9},{9,8},{10,11... | collective-permute-start | bytes 491528 | tf_op jit(solution)/shard_map/ppermute | solution.py:27
  8.8 16.3 %copy-start.4 = (f32[16]{0:T(128)S(1)}, f32[16]{0:T(128)}, u32[]{:S(2)}) copy-start(f32[16]{0:T(128)} %param.13) | copy-start | bytes 196
  8.8 16.4 %copy-start = (f32[1,16,5120]{2,1,0:T(8,128)S(1)}, f32[1,16,5120]{2,1,0:T(8,128)}, u32[]{:S(2)}) copy-start(f32[1,16,5120]{2,1,0:T(8,128)} %z_ref.1) | copy-start | bytes 983044
  8.8 16.4 %copy-start.1 = (f32[1,16,5120]{2,1,0:T(8,128)S(1)}, f32[1,16,5120]{2,1,0:T(8,128)}, u32[]{:S(2)}) copy-start(f32[1,16,5120]{2,1,0:T(8,128)} %mom_ref.1) | copy-start | bytes 983044
  8.8 17.7 %copy-start.2 = (f32[512,16]{0,1:T(8,128)S(1)}, f32[512,16]{0,1:T(8,128)}, u32[]{:S(2)}) copy-start(f32[512,16]{0,1:T(8,128)} %param.10) | copy-start | bytes 98308
  8.8 17.7 %copy-start.3 = (f32[512,16]{0,1:T(8,128)S(1)}, f32[512,16]{0,1:T(8,128)}, u32[]{:S(2)}) copy-start(f32[512,16]{0,1:T(8,128)} %param.12) | copy-start | bytes 98308
  10.3 15.8 %collective-permute-start.1 = (f32[16,2560]{1,0:T(8,128)S(1)}, f32[16,2560]{1,0:T(8,128)S(1)}, u32[]{:S(2)}, u32[]{:S(2)}) collective-permute-start(f32[16,2560]{1,0:T(8,128)S(1)} %add.6.own_ref), channel_id=1, source_target_pairs={{0,2},{1,3},{2,0},{3,1},{4,6},{5,7},{6,4},{7,5},{8,10},{9,11},{10,... | collective-permute-start | bytes 491528 | tf_op jit(solution)/shard_map/ppermute | solution.py:27
  12.9 4.1 %collective-permute-start.2 = (f32[16,768]{1,0:T(8,128)S(1)}, f32[16,768]{1,0:T(8,128)S(1)}, u32[]{:S(2)}, u32[]{:S(2)}) collective-permute-start(f32[16,768]{1,0:T(8,128)S(1)} %get-tuple-element.48.own_ref), channel_id=1, source_target_pairs={{0,4},{4,0},{8,12},{12,8},{16,20},{20,16},{24,28},{28,24},{1,5},{5... | collective-permute-start | bytes 147464 | tf_op jit(solution)/shard_map/ppermute | solution.py:27
  17.0 4.2 %collective-permute-start.3 = (f32[16,768]{1,0:T(8,128)S(1)}, f32[16,768]{1,0:T(8,128)S(1)}, u32[]{:S(2)}, u32[]{:S(2)}) collective-permute-start(f32[16,768]{1,0:T(8,128)S(1)} %shard_map.123.own_ref), channel_id=1, source_target_pairs={{0,8},{4,12},{8,0},{12,4},{16,24},{20,28},{24,16},{28,20},{1,9},{5... | collective-permute-start | bytes 147464 | tf_op jit(solution)/shard_map/ppermute | solution.py:27
  21.2 5.0 %collective-permute-start.4 = (f32[16,640]{1,0:T(8,128)S(1)}, f32[16,640]{1,0:T(8,128)S(1)}, u32[]{:S(2)}, u32[]{:S(2)}) collective-permute-start(f32[16,640]{1,0:T(8,128)S(1)} %shard_map.124.refs_0_), channel_id=1, source_target_pairs={{0,16},{4,20},{8,24},{12,28},{16,0},{20,4},{24,8},{28,12},{1,17},{... | collective-permute-start | bytes 122888 | tf_op jit(solution)/shard_map/ppermute | solution.py:27
  26.4 1.5 %collective-permute-start.5 = (f32[16,2560]{1,0:T(8,128)S(1)}, f32[16,2560]{1,0:T(8,128)S(1)}, u32[]{:S(2)}, u32[]{:S(2)}) collective-permute-start(f32[16,2560]{1,0:T(8,128)S(1)} %get-tuple-element.49.own_ref.z_ref.zw_ref.refs_5_), channel_id=1, source_target_pairs={{0,1},{1,0},{2,3},{3,2},{4,5},{5,4},{6,7},{7,6},{8,9},{9,8},{10,11... | collective-permute-start | bytes 491528 | tf_op jit(solution)/shard_map/ppermute | solution.py:27
  30.4 2.7 %collective-permute-start.9 = (f32[16,2560]{1,0:T(8,128)S(1)}, f32[16,2560]{1,0:T(8,128)S(1)}, u32[]{:S(2)}, u32[]{:S(2)}) collective-permute-start(f32[16,2560]{1,0:T(8,128)S(1)} %get-tuple-element.63), channel_id=1, source_target_pairs={{0,1},{1,0},{2,3},{3,2},{4,5},{5,4},{6,7},{7,6},{8,9},{9,8},{10,11... | collective-permute-start | bytes 491528 | tf_op jit(solution)/shard_map/ppermute | solution.py:27
  33.1 15.2 %collective-permute-start.10 = (f32[16,2560]{1,0:T(8,128)S(1)}, f32[16,2560]{1,0:T(8,128)S(1)}, u32[]{:S(2)}, u32[]{:S(2)}) collective-permute-start(f32[16,2560]{1,0:T(8,128)S(1)} %add.7.refs_2_), channel_id=1, source_target_pairs={{0,2},{1,3},{2,0},{3,1},{4,6},{5,7},{6,4},{7,5},{8,10},{9,11},{10,... | collective-permute-start | bytes 491528 | tf_op jit(solution)/shard_map/ppermute | solution.py:27
  35.0 4.1 %collective-permute-start.6 = (f32[16,768]{1,0:T(8,128)S(1)}, f32[16,768]{1,0:T(8,128)S(1)}, u32[]{:S(2)}, u32[]{:S(2)}) collective-permute-start(f32[16,768]{1,0:T(8,128)S(1)} %shard_map.130.own_ref), channel_id=1, source_target_pairs={{0,4},{4,0},{8,12},{12,8},{16,20},{20,16},{24,28},{28,24},{1,5},{5... | collective-permute-start | bytes 147464 | tf_op jit(solution)/shard_map/ppermute | solution.py:27
  39.1 4.2 %collective-permute-start.7 = (f32[16,768]{1,0:T(8,128)S(1)}, f32[16,768]{1,0:T(8,128)S(1)}, u32[]{:S(2)}, u32[]{:S(2)}) collective-permute-start(f32[16,768]{1,0:T(8,128)S(1)} %shard_map.131.own_ref), channel_id=1, source_target_pairs={{0,8},{4,12},{8,0},{12,4},{16,24},{20,28},{24,16},{28,20},{1,9},{5... | collective-permute-start | bytes 147464 | tf_op jit(solution)/shard_map/ppermute | solution.py:27
  43.3 5.0 %collective-permute-start.8 = (f32[16,640]{1,0:T(8,128)S(1)}, f32[16,640]{1,0:T(8,128)S(1)}, u32[]{:S(2)}, u32[]{:S(2)}) collective-permute-start(f32[16,640]{1,0:T(8,128)S(1)} %shard_map.132.refs_0_), channel_id=1, source_target_pairs={{0,16},{4,20},{8,24},{12,28},{16,0},{20,4},{24,8},{28,12},{1,17},{... | collective-permute-start | bytes 122888 | tf_op jit(solution)/shard_map/ppermute | solution.py:27
  49.1 13.7 %collective-permute-start.11 = (f32[16,2560]{1,0:T(8,128)S(1)}, f32[16,2560]{1,0:T(8,128)S(1)}, u32[]{:S(2)}, u32[]{:S(2)}) collective-permute-start(f32[16,2560]{1,0:T(8,128)S(1)} %get-tuple-element.68.own_ref), channel_id=1, source_target_pairs={{0,1},{1,0},{2,3},{3,2},{4,5},{5,4},{6,7},{7,6},{8,9},{9,8},{10,11... | collective-permute-start | bytes 491528 | tf_op jit(solution)/shard_map/ppermute | solution.py:27
  49.1 13.7 %all-to-all-start = ((f32[32,1,128]{2,1,0:T(1,128)}), f32[32,1,128]{2,1,0:T(1,128)S(1)}, u32[]{:S(2)}, u32[]{:S(2)}) async-start(f32[32,1,128]{2,1,0:T(1,128)} %bitcast.3), calls=%async_computation | async-start | bytes 32768 | tf_op jit(solution)/shard_map/all_to_all | solution.py:524

commit v6 on v5

--- a/solution.py
+++ b/solution.py
@@ -205,7 +205,7 @@
     lik_ref[...] = add(sums) - f32(LN2) * add(likes)
 
 
-def loading_kernel(k, half, sub, zo_ref, rho_ref, rlo_ref, zw_ref, rhw_ref, rlw_ref, liko_ref, likw_ref, load_ref):
+def loading_kernel(k, half, sub, zo_ref, rho_ref, rlo_ref, zw_ref, rhw_ref, rlw_ref, load_ref):
     loads = []
     for z_ref, rh_ref, rl_ref in ((zo_ref, rho_ref, rlo_ref), (zw_ref, rhw_ref, rlw_ref)):
         for i in range(half // sub):
@@ -213,21 +213,15 @@
             h, m, _ = split3(z_ref[:, rows])
             loads.append(loading_terms(h, m, rh_ref[rows, :], rl_ref[rows, :], k))
     load_ref[:, : -2 * LANES] = add(loads)
-    first, load_ref[:, -LANES:] = pack_rims(in_order(zw_ref[...], zo_ref[...]), k)
-    like = jnp.sum(fold_lanes(liko_ref[...] + likw_ref[...]), 1, keepdims=True)
-    like = jnp.concatenate([like, jnp.zeros((k - 8, 1), f32)], 0)
-    load_ref[:, -2 * LANES : -LANES] = jnp.where(lane(first.shape) == SPARE, like, first)
+    load_ref[:, -2 * LANES : -LANES], load_ref[:, -LANES:] = pack_rims(in_order(zw_ref[...], zo_ref[...]), k)
 
 
 def lane(shape):
     return lax.broadcasted_iota(jnp.int32, shape, len(shape) - 1)
 
 
-SPARE = TY - 1
-
-
 def pack_rims(vregs, k):
-    assert len(vregs) < TY
+    assert len(vregs) <= TY
     q = lax.rem(lane((k, LANES)), TY)
     first = jnp.zeros((k, LANES), f32)
     last = jnp.zeros((k, LANES), f32)
@@ -271,11 +265,11 @@
     me, n = lax.axis_index("site"), lax.axis_size("site")
     even = lax.rem(me, 2) == 0
     if ride:
-        pair, one, two = refs
+        pair, one, three = refs
         near = jnp.where(even, pair[:, -2 * LANES : -LANES], pair[:, -LANES:])
         row = me // 2
         close = (lax.rem(row, 2) == 1) == even
-        far = jnp.where(close, one[:, -2 * LANES : -LANES], two[:, -LANES:])
+        far = jnp.where(close, one[:, -LANES:], three[:, -LANES:])
     else:
         near, far = refs[0][...], refs[1][...]
     left = jnp.where(me == 0, 0.0, jnp.where(even, far, near))
@@ -297,25 +291,18 @@
     near_ref[...], far_ref[...] = rims_of(vregs_of(z_ref[0]), k)
 
 
-def pair_stage_kernel(own_ref, got_ref, out_ref):
+def stage_kernel(own_ref, got_ref, one_ref, two_ref, three_ref):
+    both = own_ref[:, : -2 * LANES] + got_ref[:, : -2 * LANES]
     site = lax.axis_index("site")
-    out_ref[:, : -2 * LANES] = own_ref[:, : -2 * LANES] + got_ref[:, : -2 * LANES]
     even = lax.rem(site, 2) == 0
-    own_first, got_first = own_ref[:, -2 * LANES : -LANES], got_ref[:, -2 * LANES : -LANES]
-    first = jnp.where(even, own_first, got_first)
+    first = jnp.where(even, own_ref[:, -2 * LANES : -LANES], got_ref[:, -2 * LANES : -LANES])
     last = jnp.where(even, got_ref[:, -LANES:], own_ref[:, -LANES:])
     low = lax.rem(site // 2, 2) == 0
-    spare = lane(first.shape) == SPARE
-    out_ref[:, -2 * LANES : -LANES] = jnp.where(spare, own_first + got_first, jnp.where(low, last, first))
-    out_ref[:, -LANES:] = jnp.where(low, first, last)
-
-
-def row_stage_kernel(own_ref, got_ref, out_ref):
-    wide = slice(None), slice(0, own_ref.shape[1] - LANES)
-    both = own_ref[wide] + got_ref[wide]
-    out_ref[:, :-LANES] = both[:, :-LANES]
-    rim = both[:, -LANES:]
-    out_ref[:, -LANES:] = jnp.where(lane(rim.shape) == SPARE, rim, got_ref[:, -LANES:])
+    one_ref[:, :-LANES] = both
+    one_ref[:, -LANES:] = jnp.where(low, last, first)
+    two_ref[...] = both
+    three_ref[:, :-LANES] = both
+    three_ref[:, -LANES:] = jnp.where(low, first, last)
 
 
 def ahead_kernel(k, half, z_ref, mom_ref, upper_ref, lower_ref, gain_ref, sf_ref, sl_ref, a_ref, z_own_ref, s_ref, l_ref):
@@ -372,7 +359,7 @@
 def finish_kernel(ride, k, half, n_terms, shares, *refs):
     terms = refs[:n_terms]
     own_ref, other_ref, a_ref, z_ref, s_ref, gain_ref, pe_ref, newl_ref, halfl_ref, sl_ref = refs[n_terms : n_terms + 10]
-    *halo, end_ref, endl_ref, share_ref = refs[n_terms + 10 :]
+    liko_ref, likw_ref, *halo, end_ref, endl_ref, share_ref = refs[n_terms + 10 :]
     beside = beside_of(*sides(ride, halo), half, k)
     step, gain = s_ref[...], gain_ref[...]
     energy = pe_ref[...]
@@ -388,9 +375,8 @@
     step = jnp.tile(sl_ref[...], (1, species // LANES))
     endl = halfl_ref[...] + (0.5 * step) * (load - newl)
     endl_ref[...] = endl
-    rim = add([t[:, species : species + LANES] for t in terms])
-    loadings = 0.5 * fold_lanes(endl * endl + newl * newl) + jnp.where(lane(rim.shape) == SPARE, rim, 0.0)
-    share = jnp.sum((0.5 / shares[0]) * energy + (1.0 / shares[1]) * loadings, 0, keepdims=True)
+    share = (0.5 / shares[0]) * energy + (0.5 / shares[1]) * fold_lanes(endl * endl + newl * newl)
+    share = jnp.sum(share, 0, keepdims=True) + jnp.sum(fold_lanes(liko_ref[...] + likw_ref[...]), 0, keepdims=True)
     share_ref[...] = jnp.broadcast_to(share, share_ref.shape)
 
 
@@ -426,11 +412,10 @@
         if not ride:
             return sum_terms(load, "site", site), ()
         got = swap(load, "site", 1)
-        (two,) = call(pair_stage_kernel, [VMEM] * 2, [load.shape])(load, got)
-        got_two = swap(two, "site", 2)
-        (four,) = call(row_stage_kernel, [VMEM] * 2, [(k, species + LANES)])(two, got_two)
-        got_four = swap(four, "site", 4)
-        return [four, got_four], (got, got_two, got_four)
+        wide, narrow = (k, species + LANES), (k, species)
+        stage = call(stage_kernel, [VMEM] * 2, [wide, narrow, wide])(load, got)
+        terms = [swap(t, "site", m) for t, m in zip(stage, site[1])]
+        return [stage[1], *terms], (got, terms[0], terms[2])
 
     def upright(low, high):
         if n_site <= TGY:
@@ -503,8 +488,8 @@
         )(z, ly, lg, held)
         for start, z in ((half, moved_own), (0, moved_oth))
     ]
-    (load,) = call(functools.partial(loading_kernel, k, half, sub), [VMEM] * 8, [(k, species + 2 * LANES)])(
-        moved_oth, *parts_oth, moved_own, *parts_own, lik_oth, lik_own
+    (load,) = call(functools.partial(loading_kernel, k, half, sub), [VMEM] * 6, [(k, species + 2 * LANES)])(
+        moved_oth, *parts_oth, moved_own, *parts_own
     )
     load_terms, halo = exchange(load)
     own, other = share(own, oth)
@@ -517,9 +502,9 @@
     n_devices = n_site * n_sp
     end_own, endl, shares = call(
         functools.partial(finish_kernel, ride, k, half, len(load_terms), (n_sp // 2, n_site)),
-        [VMEM] * (len(load_terms) + 10 + len(halo)),
+        [VMEM] * (len(load_terms) + 12 + len(halo)),
         [(k, half), (k, species), (n_devices, LANES)],
-    )(*load_terms, own, other, a2, moved_own, svec, gain, prior_energy, newl, halfl, lvec, *halo)
+    )(*load_terms, own, other, a2, moved_own, svec, gain, prior_energy, newl, halfl, lvec, lik_oth, lik_own, *halo)
     end_oth = swap(end_own, "sp", 1)
     shares = lax.all_to_all(shares, ("site", "sp"), 0, 0, tiled=True)
     new_momenta, end_loadings, energy = call(

time: 63.8 us -> 62.2 us (0.975)
  starting transfers between devices: 22.8 us -> 21 us
    all_to_all x1, starting transfers between devices: 6.6 us -> 4.68 us  [local(): shares = lax.all_to_all(shares, ('site', 'sp'), 0, 0, tiled=True)]
    ppermute x12 -> x14, waiting for transfers between devices: 13.1 us -> 13.3 us  [swap(): lax.ppermute(block, axis, [(i, i ^ mask) for i in range(lax.axis_size(axi...]
    ppermute x12 -> x14, starting transfers between devices: 16.2 us -> 16.3 us  [swap(): lax.ppermute(block, axis, [(i, i ^ mask) for i in range(lax.axis_size(axi...]
    pallas_call x5 -> x3, Pallas kernels: 1.61 us -> 1.61 us  [the longest x1 1.57 us: local(): call(functools.partial(loading_kernel, k, half, sub), [VMEM] * 6, [(k, sp...]
  transfers between devices with their start and end apart: 13 -> 15, of which waited for: 8 -> 6; matrix products, arithmetic and copies ran while one was open for 0% -> 0% of each run, Pallas kernels for 11% -> 11%
where the time goes in v6:
time: 62.2 us; the launch traced here: 62 us
  starting transfers between devices  21 us (34%)
  waiting for transfers between devices  19.6 us (32%)
  Pallas kernels  19.1 us (31%)
  between operations  2.06 us (3%)
    ppermute x14, starting transfers between devices, swap(): lax.ppermute(block, axis, [(i, i ^ mask) for i in range(lax.axis_size(axi...  16.3 us
    ppermute x14, waiting for transfers between devices, swap(): lax.ppermute(block, axis, [(i, i ^ mask) for i in range(lax.axis_size(axi...  13.3 us
    all_to_all x1, waiting for transfers between devices, local(): shares = lax.all_to_all(shares, ('site', 'sp'), 0, 0, tiled=True)  6.34 us
    pallas_call x1, Pallas kernels, local(): call(functools.partial(first_kernel, k, half, sub), [HBM, HBM, HBM], [(k,...  6.12 us
    pallas_call x2, Pallas kernels, local(): call(functools.partial(second_kernel, k, half, sub, start), [VMEM] * 4, [...  5.04 us
    all_to_all x1, starting transfers between devices, local(): shares = lax.all_to_all(shares, ('site', 'sp'), 0, 0, tiled=True)  4.68 us
    pallas_call x2, Pallas kernels, local(): call(functools.partial(factor_kernel, k, half, sub), [VMEM] * 3, [(k, hal...  2.99 us
    pallas_call x1, Pallas kernels, local(): call(functools.partial(loading_kernel, k, half, sub), [VMEM] * 6, [(k, sp...  1.57 us
  transfers between devices with their start and end apart: 15, of which 6 were waited for; matrix products, arithmetic and copies ran while one was open for 0% of the time, Pallas kernels for 11%

profile of v6, /device:TPU:0, one launch (start us, length us, event | category | flops | bytes accessed | tf_op | source)
XLA Modules:
  0.0 62.0 jit_solution(5447306678013932381)
XLA Ops:
  0.6 6.1 %shard_map.119 = (f32[16,768]{1,0:T(8,128)S(1)}, bf16[32,512]{1,0:T(8,128)(2,1)S(1)}, f32[5120,512]{1,0:T(8,128)S(1)}, bf16[2560,512]{1,0:T(8,128)(2,1)S(1)}, bf...) custom-call(f32[1,16,5120]{2,1,0:T(8,128)} %z_ref.1, f32[16,512]{1,0:T(8,128)} %bitcast.8, ...), custom_call_target="tpu_custom_call" | custom-call | tf_op jit(solution)/shard_map/pallas_call | solution.py:438
  6.8 1.5 %shard_map.121 = f32[16,2560]{1,0:T(8,128)S(1)} custom-call(bf16[32,512]{1,0:T(8,128)(2,1)S(1)} %get-tuple-element.46.lg_ref, bf16[2560,512]{1,0:T(8,128)(2,1)S(1)} %get-tuple-element.49.rh_ref, bf16[2560,512]{1,0:T(8,128)(2,1)S(1)} %get-tuple-element.50.rl_ref), custom_call_target="tpu_custom_call" | custom-call | tf_op jit(solution)/shard_map/pallas_call | solution.py:455
  8.8 1.5 %shard_map.120 = f32[16,2560]{1,0:T(8,128)S(1)} custom-call(bf16[32,512]{1,0:T(8,128)(2,1)S(1)} %get-tuple-element.46.lg_ref, bf16[2560,512]{1,0:T(8,128)(2,1)S(1)} %get-tuple-element.47.rh_ref, bf16[2560,512]{1,0:T(8,128)(2,1)S(1)} %get-tuple-element.48.rl_ref), custom_call_target="tpu_custom_call" | custom-call | tf_op jit(solution)/shard_map/pallas_call | solution.py:455
  10.3 2.5 %collective-permute-start.1 = (f32[16,2560]{1,0:T(8,128)S(1)}, f32[16,2560]{1,0:T(8,128)S(1)}, u32[]{:S(2)}, u32[]{:S(2)}) collective-permute-start(f32[16,2560]{1,0:T(8,128)S(1)} %add.6.own_ref), channel_id=1, source_target_pairs={{0,2},{1,3},{2,0},{3,1},{4,6},{5,7},{6,4},{7,5},{8,10},{9,11},{10,... | collective-permute-start | bytes 491528 | tf_op jit(solution)/shard_map/ppermute | solution.py:27
  12.9 1.5 %collective-permute-start.2 = (f32[16,768]{1,0:T(8,128)S(1)}, f32[16,768]{1,0:T(8,128)S(1)}, u32[]{:S(2)}, u32[]{:S(2)}) collective-permute-start(f32[16,768]{1,0:T(8,128)S(1)} %get-tuple-element.54.own_ref), channel_id=1, source_target_pairs={{0,4},{4,0},{8,12},{12,8},{16,20},{20,16},{24,28},{28,24},{1,5},{5... | collective-permute-start | bytes 147464 | tf_op jit(solution)/shard_map/ppermute | solution.py:27
  14.4 2.6 %collective-permute-done.2.got_ref.refs_0_ = f32[16,768]{1,0:T(8,128)S(1)} collective-permute-done((f32[16,768]{1,0:T(8,128)S(1)}, f32[16,768]{1,0:T(8,128)S(1)}, u32[]{:S(2)}, u32[]{:S(2)}) %collective-permute-start.2) | collective-permute-done | bytes 49184 | tf_op jit(solution)/shard_map/ppermute | solution.py:27
  17.0 1.6 %collective-permute-start.3 = (f32[16,640]{1,0:T(8,128)S(1)}, f32[16,640]{1,0:T(8,128)S(1)}, u32[]{:S(2)}, u32[]{:S(2)}) collective-permute-start(f32[16,640]{1,0:T(8,128)S(1)} %get-tuple-element.55), channel_id=1, source_target_pairs={{0,8},{4,12},{8,0},{12,4},{16,24},{20,28},{24,16},{28,20},{1,9},{5... | collective-permute-start | bytes 122888 | tf_op jit(solution)/shard_map/ppermute | solution.py:27
  18.6 2.5 %collective-permute-start.4 = (f32[16,640]{1,0:T(8,128)S(1)}, f32[16,640]{1,0:T(8,128)S(1)}, u32[]{:S(2)}, u32[]{:S(2)}) collective-permute-start(f32[16,640]{1,0:T(8,128)S(1)} %get-tuple-element.56), channel_id=1, source_target_pairs={{0,24},{4,28},{8,16},{12,20},{16,8},{20,12},{24,0},{28,4},{1,25},{... | collective-permute-start | bytes 122888 | tf_op jit(solution)/shard_map/ppermute | solution.py:27
  22.9 1.6 %collective-permute-done.4.refs_2_.refs_3_ = f32[16,640]{1,0:T(8,128)S(1)} collective-permute-done((f32[16,640]{1,0:T(8,128)S(1)}, f32[16,640]{1,0:T(8,128)S(1)}, u32[]{:S(2)}, u32[]{:S(2)}) %collective-permute-start.4) | collective-permute-done | bytes 40992 | tf_op jit(solution)/shard_map/ppermute | solution.py:27
  24.8 0.9 %collective-permute-start.6 = (f32[16,512]{1,0:T(8,128)S(1)}, f32[16,512]{1,0:T(8,128)S(1)}, u32[]{:S(2)}, u32[]{:S(2)}) collective-permute-start(f32[16,512]{1,0:T(8,128)S(1)} %get-tuple-element.58.refs_0_), channel_id=1, source_target_pairs={{0,16},{4,20},{8,24},{12,28},{16,0},{20,4},{24,8},{28,12},{1,17},{... | collective-permute-start | bytes 98312 | tf_op jit(solution)/shard_map/ppermute | solution.py:27
  25.6 4.4 %collective-permute-done.6.refs_2_ = f32[16,512]{1,0:T(8,128)S(1)} collective-permute-done((f32[16,512]{1,0:T(8,128)S(1)}, f32[16,512]{1,0:T(8,128)S(1)}, u32[]{:S(2)}, u32[]{:S(2)}) %collective-permute-start.6) | collective-permute-done | bytes 32800 | tf_op jit(solution)/shard_map/ppermute | solution.py:27
  30.1 2.5 %shard_map.127 = (f32[16,2560]{1,0:T(8,128)S(1)}, f32[8,512]{1,0:T(8,128)S(1)}, bf16[2560,512]{1,0:T(8,128)(2,1)S(1)}, bf16[2560,512]{1,0:T(8,128)(2,1)S(1)}) custom-call(f32[16,2560]{1,0:T(8,128)S(1)} %collective-permute-done.5.oth_ref.z_ref.zo_ref, bf16[96,512]{1,0:T(8,128)(2,1)S(1)} %get-tuple-element.62.ly_ref, ...), custom_call_target="tpu_custom_call" | custom-call | tf_op jit(solution)/shard_map/pallas_call | solution.py:482
  32.7 2.5 %shard_map.128 = (f32[16,2560]{1,0:T(8,128)S(1)}, f32[8,512]{1,0:T(8,128)S(1)}, bf16[2560,512]{1,0:T(8,128)(2,1)S(1)}, bf16[2560,512]{1,0:T(8,128)(2,1)S(1)}) custom-call(f32[16,2560]{1,0:T(8,128)S(1)} %get-tuple-element.57.own_ref.z_ref.zw_ref.refs_7_, bf16[96,512]{1,0:T(8,128)(2,1)S(1)} %get-tuple-element.62.ly_ref, ...), custom_call_target="tpu_custom_call" | custom-call | tf_op jit(solution)/shard_map/pallas_call | solution.py:482
  35.9 1.6 %shard_map.129.own_ref = f32[16,768]{1,0:T(8,128)S(1)} custom-call(f32[16,2560]{1,0:T(8,128)S(1)} %collective-permute-done.5.oth_ref.z_ref.zo_ref, bf16[2560,512]{1,0:T(8,128)(2,1)S(1)} %get-tuple-element.65.rho_ref, bf16[2560,512]{1,0:T(8,128)(2,1)S(1)} %get-tuple-element.66.rlo_ref, f32[16,2560]{1,0:T(8,128)S(1)} %get-tuple-element.57.own_ref.z_ref.zw_ref.refs_7_, ...), custom_call_target="tpu_custom_call" | custom-call | tf_op jit(solution)/shard_map/pallas_call | solution.py:491
  37.4 1.5 %collective-permute-start.7 = (f32[16,768]{1,0:T(8,128)S(1)}, f32[16,768]{1,0:T(8,128)S(1)}, u32[]{:S(2)}, u32[]{:S(2)}) collective-permute-start(f32[16,768]{1,0:T(8,128)S(1)} %shard_map.129.own_ref), channel_id=1, source_target_pairs={{0,4},{4,0},{8,12},{12,8},{16,20},{20,16},{24,28},{28,24},{1,5},{5... | collective-permute-start | bytes 147464 | tf_op jit(solution)/shard_map/ppermute | solution.py:27
  39.0 2.6 %collective-permute-done.7.got_ref.refs_16_ = f32[16,768]{1,0:T(8,128)S(1)} collective-permute-done((f32[16,768]{1,0:T(8,128)S(1)}, f32[16,768]{1,0:T(8,128)S(1)}, u32[]{:S(2)}, u32[]{:S(2)}) %collective-permute-start.7) | collective-permute-done | bytes 49184 | tf_op jit(solution)/shard_map/ppermute | solution.py:27
  41.6 2.1 %collective-permute-start.10 = (f32[16,640]{1,0:T(8,128)S(1)}, f32[16,640]{1,0:T(8,128)S(1)}, u32[]{:S(2)}, u32[]{:S(2)}) collective-permute-start(f32[16,640]{1,0:T(8,128)S(1)} %get-tuple-element.71), channel_id=1, source_target_pairs={{0,24},{4,28},{8,16},{12,20},{16,8},{20,12},{24,0},{28,4},{1,25},{... | collective-permute-start | bytes 122888 | tf_op jit(solution)/shard_map/ppermute | solution.py:27
  43.7 2.3 %collective-permute-start.9 = (f32[16,512]{1,0:T(8,128)S(1)}, f32[16,512]{1,0:T(8,128)S(1)}, u32[]{:S(2)}, u32[]{:S(2)}) collective-permute-start(f32[16,512]{1,0:T(8,128)S(1)} %get-tuple-element.69.refs_0_), channel_id=1, source_target_pairs={{0,16},{4,20},{8,24},{12,28},{16,0},{20,4},{24,8},{28,12},{1,17},{... | collective-permute-start | bytes 98312 | tf_op jit(solution)/shard_map/ppermute | solution.py:27
  46.4 2.1 %collective-permute-done.9.refs_2_ = f32[16,512]{1,0:T(8,128)S(1)} collective-permute-done((f32[16,512]{1,0:T(8,128)S(1)}, f32[16,512]{1,0:T(8,128)S(1)}, u32[]{:S(2)}, u32[]{:S(2)}) %collective-permute-start.9) | collective-permute-done | bytes 32800 | tf_op jit(solution)/shard_map/ppermute | solution.py:27
  48.5 0.9 %shard_map.132 = (f32[16,2560]{1,0:T(8,128)S(1)}, f32[16,512]{1,0:T(8,128)S(1)}, f32[32,128]{1,0:T(8,128)}) custom-call(f32[16,512]{1,0:T(8,128)S(1)} %get-tuple-element.69.refs_0_, f32[16,640]{1,0:T(8,128)S(1)} %collective-permute-done.8.refs_1_.refs_17_, f32[16,512]{1,0:T(8,128)S(1)} %collective-permute-done.9.refs_2_, ...), custom_call_target="tpu_custom_call" | custom-call | tf_op jit(solution)/shard_map/pallas_call | solution.py:503
  49.4 4.7 %all-to-all-start = ((f32[32,1,128]{2,1,0:T(1,128)}), f32[32,1,128]{2,1,0:T(1,128)S(1)}, u32[]{:S(2)}, u32[]{:S(2)}) async-start(f32[32,1,128]{2,1,0:T(1,128)} %bitcast.3), calls=%async_computation | async-start | bytes 32768 | tf_op jit(solution)/shard_map/all_to_all | solution.py:509
  54.1 0.8 %shard_map.126 = (f32[1,16,5120]{2,1,0:T(8,128)}, f32[16,512]{1,0:T(8,128)}) custom-call(f32[16,2560]{1,0:T(8,128)S(1)} %get-tuple-element.57.own_ref.z_ref.zw_ref.refs_7_, f32[16,2560]{1,0:T(8,128)S(1)} %collective-permute-done.5.oth_ref.z_ref.zo_ref, f32[16,512]{1,0:T(8,128)S(1)} %get-tuple-element.60.loadings_ref.refs_11_), custom_call_target="tpu_custom_call" | custom-call | tf_op jit(solution)/shard_map/pallas_call | solution.py:478
  54.9 6.3 %all-to-all-done = f32[32,1,128]{2,1,0:T(1,128)S(1)} async-done(((f32[32,1,128]{2,1,0:T(1,128)}), f32[32,1,128]{2,1,0:T(1,128)S(1)}, u32[]{:S(2)}, u32[]{:S(2)}) %all-to-all-start) | async-done | bytes 16416 | tf_op jit(solution)/shard_map/all_to_all | solution.py:509
  61.2 0.8 %shard_map.133 = (f32[1,16,5120]{2,1,0:T(8,128)}, f32[16,512]{1,0:T(8,128)}, f32[1]{0:T(128)}) custom-call(f32[16,2560]{1,0:T(8,128)S(1)} %get-tuple-element.80.own_ref, f32[16,2560]{1,0:T(8,128)S(1)} %collective-permute-done.13.oth_ref, f32[16,512]{1,0:T(8,128)S(1)} %get-tuple-element.81.loadings_ref, f32[32,128]{1,0:T(8,128)S(1)} %bitcast.10), custom_call_target="tpu_custom_call" | custom-call | tf_op jit(solution)/shard_map/pallas_call | solution.py:510
  (35 shorter events, 2.5 us)
Async XLA Ops:
  8.3 2.0 %collective-permute-start = (f32[16,2560]{1,0:T(8,128)S(1)}, f32[16,2560]{1,0:T(8,128)S(1)}, u32[]{:S(2)}, u32[]{:S(2)}) collective-permute-start(f32[16,2560]{1,0:T(8,128)S(1)} %shard_map.121), channel_id=1, source_target_pairs={{0,1},{1,0},{2,3},{3,2},{4,5},{5,4},{6,7},{7,6},{8,9},{9,8},{10,11... | collective-permute-start | bytes 491528 | tf_op jit(solution)/shard_map/ppermute | solution.py:27
  8.8 13.7 %copy-start.4 = (f32[16]{0:T(128)S(1)}, f32[16]{0:T(128)}, u32[]{:S(2)}) copy-start(f32[16]{0:T(128)} %param.13) | copy-start | bytes 196
  8.8 13.7 %copy-start = (f32[1,16,5120]{2,1,0:T(8,128)S(1)}, f32[1,16,5120]{2,1,0:T(8,128)}, u32[]{:S(2)}) copy-start(f32[1,16,5120]{2,1,0:T(8,128)} %z_ref.1) | copy-start | bytes 983044
  8.8 13.7 %copy-start.1 = (f32[1,16,5120]{2,1,0:T(8,128)S(1)}, f32[1,16,5120]{2,1,0:T(8,128)}, u32[]{:S(2)}) copy-start(f32[1,16,5120]{2,1,0:T(8,128)} %mom_ref.1) | copy-start | bytes 983044
  8.8 21.2 %copy-start.2 = (f32[512,16]{0,1:T(8,128)S(1)}, f32[512,16]{0,1:T(8,128)}, u32[]{:S(2)}) copy-start(f32[512,16]{0,1:T(8,128)} %param.10) | copy-start | bytes 98308
  8.8 21.2 %copy-start.3 = (f32[512,16]{0,1:T(8,128)S(1)}, f32[512,16]{0,1:T(8,128)}, u32[]{:S(2)}) copy-start(f32[512,16]{0,1:T(8,128)} %param.12) | copy-start | bytes 98308
  10.3 14.1 %collective-permute-start.1 = (f32[16,2560]{1,0:T(8,128)S(1)}, f32[16,2560]{1,0:T(8,128)S(1)}, u32[]{:S(2)}, u32[]{:S(2)}) collective-permute-start(f32[16,2560]{1,0:T(8,128)S(1)} %add.6.own_ref), channel_id=1, source_target_pairs={{0,2},{1,3},{2,0},{3,1},{4,6},{5,7},{6,4},{7,5},{8,10},{9,11},{10,... | collective-permute-start | bytes 491528 | tf_op jit(solution)/shard_map/ppermute | solution.py:27
  12.9 4.1 %collective-permute-start.2 = (f32[16,768]{1,0:T(8,128)S(1)}, f32[16,768]{1,0:T(8,128)S(1)}, u32[]{:S(2)}, u32[]{:S(2)}) collective-permute-start(f32[16,768]{1,0:T(8,128)S(1)} %get-tuple-element.54.own_ref), channel_id=1, source_target_pairs={{0,4},{4,0},{8,12},{12,8},{16,20},{20,16},{24,28},{28,24},{1,5},{5... | collective-permute-start | bytes 147464 | tf_op jit(solution)/shard_map/ppermute | solution.py:27
  17.0 5.9 %collective-permute-start.3 = (f32[16,640]{1,0:T(8,128)S(1)}, f32[16,640]{1,0:T(8,128)S(1)}, u32[]{:S(2)}, u32[]{:S(2)}) collective-permute-start(f32[16,640]{1,0:T(8,128)S(1)} %get-tuple-element.55), channel_id=1, source_target_pairs={{0,8},{4,12},{8,0},{12,4},{16,24},{20,28},{24,16},{28,20},{1,9},{5... | collective-permute-start | bytes 122888 | tf_op jit(solution)/shard_map/ppermute | solution.py:27
  18.6 5.8 %collective-permute-start.4 = (f32[16,640]{1,0:T(8,128)S(1)}, f32[16,640]{1,0:T(8,128)S(1)}, u32[]{:S(2)}, u32[]{:S(2)}) collective-permute-start(f32[16,640]{1,0:T(8,128)S(1)} %get-tuple-element.56), channel_id=1, source_target_pairs={{0,24},{4,28},{8,16},{12,20},{16,8},{20,12},{24,0},{28,4},{1,25},{... | collective-permute-start | bytes 122888 | tf_op jit(solution)/shard_map/ppermute | solution.py:27
  24.7 5.4 %collective-permute-start.5 = (f32[16,2560]{1,0:T(8,128)S(1)}, f32[16,2560]{1,0:T(8,128)S(1)}, u32[]{:S(2)}, u32[]{:S(2)}) collective-permute-start(f32[16,2560]{1,0:T(8,128)S(1)} %get-tuple-element.57.own_ref.z_ref.zw_ref.refs_7_), channel_id=1, source_target_pairs={{0,1},{1,0},{2,3},{3,2},{4,5},{5,4},{6,7},{7,6},{8,9},{9,8},{10,11... | collective-permute-start | bytes 491528 | tf_op jit(solution)/shard_map/ppermute | solution.py:27
  24.8 5.2 %collective-permute-start.6 = (f32[16,512]{1,0:T(8,128)S(1)}, f32[16,512]{1,0:T(8,128)S(1)}, u32[]{:S(2)}, u32[]{:S(2)}) collective-permute-start(f32[16,512]{1,0:T(8,128)S(1)} %get-tuple-element.58.refs_0_), channel_id=1, source_target_pairs={{0,16},{4,20},{8,24},{12,28},{16,0},{20,4},{24,8},{28,12},{1,17},{... | collective-permute-start | bytes 98312 | tf_op jit(solution)/shard_map/ppermute | solution.py:27
  32.6 2.6 %collective-permute-start.11 = (f32[16,2560]{1,0:T(8,128)S(1)}, f32[16,2560]{1,0:T(8,128)S(1)}, u32[]{:S(2)}, u32[]{:S(2)}) collective-permute-start(f32[16,2560]{1,0:T(8,128)S(1)} %get-tuple-element.73), channel_id=1, source_target_pairs={{0,1},{1,0},{2,3},{3,2},{4,5},{5,4},{6,7},{7,6},{8,9},{9,8},{10,11... | collective-permute-start | bytes 491528 | tf_op jit(solution)/shard_map/ppermute | solution.py:27
  35.3 13.3 %collective-permute-start.12 = (f32[16,2560]{1,0:T(8,128)S(1)}, f32[16,2560]{1,0:T(8,128)S(1)}, u32[]{:S(2)}, u32[]{:S(2)}) collective-permute-start(f32[16,2560]{1,0:T(8,128)S(1)} %add.7.refs_4_), channel_id=1, source_target_pairs={{0,2},{1,3},{2,0},{3,1},{4,6},{5,7},{6,4},{7,5},{8,10},{9,11},{10,... | collective-permute-start | bytes 491528 | tf_op jit(solution)/shard_map/ppermute | solution.py:27
  37.4 4.1 %collective-permute-start.7 = (f32[16,768]{1,0:T(8,128)S(1)}, f32[16,768]{1,0:T(8,128)S(1)}, u32[]{:S(2)}, u32[]{:S(2)}) collective-permute-start(f32[16,768]{1,0:T(8,128)S(1)} %shard_map.129.own_ref), channel_id=1, source_target_pairs={{0,4},{4,0},{8,12},{12,8},{16,20},{20,16},{24,28},{28,24},{1,5},{5... | collective-permute-start | bytes 147464 | tf_op jit(solution)/shard_map/ppermute | solution.py:27
  41.6 6.9 %collective-permute-start.10 = (f32[16,640]{1,0:T(8,128)S(1)}, f32[16,640]{1,0:T(8,128)S(1)}, u32[]{:S(2)}, u32[]{:S(2)}) collective-permute-start(f32[16,640]{1,0:T(8,128)S(1)} %get-tuple-element.71), channel_id=1, source_target_pairs={{0,24},{4,28},{8,16},{12,20},{16,8},{20,12},{24,0},{28,4},{1,25},{... | collective-permute-start | bytes 122888 | tf_op jit(solution)/shard_map/ppermute | solution.py:27
  43.7 4.8 %collective-permute-start.8 = (f32[16,640]{1,0:T(8,128)S(1)}, f32[16,640]{1,0:T(8,128)S(1)}, u32[]{:S(2)}, u32[]{:S(2)}) collective-permute-start(f32[16,640]{1,0:T(8,128)S(1)} %get-tuple-element.70), channel_id=1, source_target_pairs={{0,8},{4,12},{8,0},{12,4},{16,24},{20,28},{24,16},{28,20},{1,9},{5... | collective-permute-start | bytes 122888 | tf_op jit(solution)/shard_map/ppermute | solution.py:27
  43.7 4.8 %collective-permute-start.9 = (f32[16,512]{1,0:T(8,128)S(1)}, f32[16,512]{1,0:T(8,128)S(1)}, u32[]{:S(2)}, u32[]{:S(2)}) collective-permute-start(f32[16,512]{1,0:T(8,128)S(1)} %get-tuple-element.69.refs_0_), channel_id=1, source_target_pairs={{0,16},{4,20},{8,24},{12,28},{16,0},{20,4},{24,8},{28,12},{1,17},{... | collective-permute-start | bytes 98312 | tf_op jit(solution)/shard_map/ppermute | solution.py:27
  49.4 11.8 %collective-permute-start.13 = (f32[16,2560]{1,0:T(8,128)S(1)}, f32[16,2560]{1,0:T(8,128)S(1)}, u32[]{:S(2)}, u32[]{:S(2)}) collective-permute-start(f32[16,2560]{1,0:T(8,128)S(1)} %get-tuple-element.80.own_ref), channel_id=1, source_target_pairs={{0,1},{1,0},{2,3},{3,2},{4,5},{5,4},{6,7},{7,6},{8,9},{9,8},{10,11... | collective-permute-start | bytes 491528 | tf_op jit(solution)/shard_map/ppermute | solution.py:27
  49.4 11.8 %all-to-all-start = ((f32[32,1,128]{2,1,0:T(1,128)}), f32[32,1,128]{2,1,0:T(1,128)S(1)}, u32[]{:S(2)}, u32[]{:S(2)}) async-start(f32[32,1,128]{2,1,0:T(1,128)} %bitcast.3), calls=%async_computation | async-start | bytes 32768 | tf_op jit(solution)/shard_map/all_to_all | solution.py:509

commit v7 on v6

--- a/solution.py
+++ b/solution.py
@@ -99,9 +99,9 @@
     return y, i, rh, (r - rh.astype(f32)).astype(bf16), h, m
 
 
-def factor_terms(rh, rl, lg, k):
-    a = dotg(lg, rh, 1, 1)
-    return a[:k] + a[k:] + dotg(lg[k:], rl, 1, 1)
+def factor_terms(rh, rl, lg, k, axis):
+    a = dotg(lg, rh, 1, axis)
+    return a[:k] + a[k:] + dotg(lg[k:], rl, 1, 0)
 
 
 def loading_terms(h, m, rh, rl, k):
@@ -167,16 +167,16 @@
         _, _, rh, rl, h, m = residuals(z_ref[0, :, pl.ds(place(i), sub)], cf, ly)
         loads.append(loading_terms(h, m, rh, rl, k))
         rh_ref, rl_ref = (rho_ref, rlo_ref) if rho else (rhw_ref, rlw_ref)
-        rh_ref[pl.ds(at, sub), :] = rh
-        rl_ref[pl.ds(at, sub), :] = rl
+        rh_ref[:, at : at + sub] = rh.T
+        rl_ref[:, at : at + sub] = rl.T
     load_ref[:, : -2 * LANES] = add(loads)
 
 
 def factor_kernel(k, half, sub, lg_ref, rh_ref, rl_ref, fac_ref):
     lg = lg_ref[...]
     for i in range(half // sub):
-        rows = pl.ds(i * sub, sub)
-        fac_ref[:, i * sub : (i + 1) * sub] = factor_terms(rh_ref[rows, :], rl_ref[rows, :], lg, k)
+        here = pl.ds(i * sub, sub)
+        fac_ref[:, here] = factor_terms(rh_ref[:, here], rl_ref[:, here], lg, k, 0)
 
 
 def move_loadings_kernel(n_terms, *refs):
@@ -190,7 +190,7 @@
     fill_loadings(newl, ly_ref, lg_ref)
 
 
-def second_kernel(k, half, sub, start, z_ref, ly_ref, lg_ref, cnt_ref, fac_ref, lik_ref, rh_ref, rl_ref):
+def second_kernel(k, half, sub, start, z_ref, ly_ref, lg_ref, cnt_ref, fac_ref, lik_ref, rh_ref, rl_ref, turned_ref):
     ly, lg = ly_ref[...], lg_ref[...]
     likes, sums = [], []
     for i in range(half // sub):
@@ -199,7 +199,8 @@
         y, inten, rh, rl, _, _ = residuals(z_ref[:, rows], cf, ly)
         rh_ref[rows, :] = rh
         rl_ref[rows, :] = rl
-        fac_ref[:, rows] = factor_terms(rh, rl, lg, k)
+        turned_ref[:, rows] = rl.T
+        fac_ref[:, rows] = factor_terms(rh, turned_ref[:, rows], lg, k, 1)
         likes.append(rows_to_8(cf * y))
         sums.append(rows_to_8(inten))
     lik_ref[...] = add(sums) - f32(LN2) * add(likes)
@@ -438,7 +439,7 @@
     load, lg, held, rho, rlo, rhw, rlw = call(
         functools.partial(first_kernel, k, half, sub),
         [HBM, HBM, HBM],
-        [(k, species + 2 * LANES), grads, (cells, species)] + [(half, species)] * 4,
+        [(k, species + 2 * LANES), grads, (cells, species)] + [(species, half)] * 4,
         [
             pltpu.VMEM(rates, bf16),
             pltpu.VMEM((1, k, cells), f32),
@@ -483,7 +484,8 @@
             functools.partial(second_kernel, k, half, sub, start),
             [VMEM] * 4,
             [(k, half), (8, species), (half, species), (half, species)],
-            limit=8,
+            [pltpu.VMEM((species, half), bf16)],
+            limit=12,
             packed=(2, 3),
         )(z, ly, lg, held)
         for start, z in ((half, moved_own), (0, moved_oth))

time: 62.2 us -> 62.5 us (level)
    pallas_call x2, Pallas kernels: 2.99 us -> 1.69 us  [local(): call(functools.partial(factor_kernel, k, half, sub), [VMEM] * 3, [(k, hal...]
    pallas_call x1, Pallas kernels: 6.12 us -> 7.2 us  [local(): call(functools.partial(first_kernel, k, half, sub), [HBM, HBM, HBM], [(k,...]
  transfers between devices with their start and end apart: 15 -> 15, of which waited for: 6 -> 7; matrix products, arithmetic and copies ran while one was open for 0% -> 0% of each run, Pallas kernels for 11% -> 10%
where the time goes in v7:
time: 62.5 us; the launch traced here: 62.3 us
  starting transfers between devices  21.3 us (34%)
  waiting for transfers between devices  19.8 us (32%)
  Pallas kernels  19 us (30%)
  between operations  2.06 us (3%)
    ppermute x14, starting transfers between devices, swap(): lax.ppermute(block, axis, [(i, i ^ mask) for i in range(lax.axis_size(axi...  16.6 us
    ppermute x14, waiting for transfers between devices, swap(): lax.ppermute(block, axis, [(i, i ^ mask) for i in range(lax.axis_size(axi...  13.4 us
    pallas_call x1, Pallas kernels, local(): call(functools.partial(first_kernel, k, half, sub), [HBM, HBM, HBM], [(k,...  7.2 us
    all_to_all x1, waiting for transfers between devices, local(): shares = lax.all_to_all(shares, ('site', 'sp'), 0, 0, tiled=True)  6.34 us
    pallas_call x2, Pallas kernels, local(): call(functools.partial(second_kernel, k, half, sub, start), [VMEM] * 4, [...  5.16 us
    all_to_all x1, starting transfers between devices, local(): shares = lax.all_to_all(shares, ('site', 'sp'), 0, 0, tiled=True)  4.64 us
    pallas_call x2, Pallas kernels, local(): call(functools.partial(factor_kernel, k, half, sub), [VMEM] * 3, [(k, hal...  1.69 us
    pallas_call x1, Pallas kernels, local(): call(functools.partial(loading_kernel, k, half, sub), [VMEM] * 6, [(k, sp...  1.57 us
  transfers between devices with their start and end apart: 15, of which 7 were waited for; matrix products, arithmetic and copies ran while one was open for 0% of the time, Pallas kernels for 10%

profile of v7, /device:TPU:0, one launch (start us, length us, event | category | flops | bytes accessed | tf_op | source)
XLA Modules:
  0.0 62.3 jit_solution(12518206119428492543)
XLA Ops:
  0.6 7.2 %shard_map.119 = (f32[16,768]{1,0:T(8,128)S(1)}, bf16[32,512]{1,0:T(8,128)(2,1)S(1)}, f32[5120,512]{1,0:T(8,128)S(1)}, bf16[512,2560]{1,0:T(8,128)(2,1)S(1)}, bf...) custom-call(f32[1,16,5120]{2,1,0:T(8,128)} %z_ref.1, f32[16,512]{1,0:T(8,128)} %bitcast.8, ...), custom_call_target="tpu_custom_call" | custom-call | tf_op jit(solution)/shard_map/pallas_call | solution.py:439
  7.8 0.8 %shard_map.121 = f32[16,2560]{1,0:T(8,128)S(1)} custom-call(bf16[32,512]{1,0:T(8,128)(2,1)S(1)} %get-tuple-element.46.lg_ref, bf16[512,2560]{1,0:T(8,128)(2,1)S(1)} %get-tuple-element.49.rh_ref, bf16[512,2560]{1,0:T(8,128)(2,1)S(1)} %get-tuple-element.50.rl_ref), custom_call_target="tpu_custom_call" | custom-call | tf_op jit(solution)/shard_map/pallas_call | solution.py:456
  9.2 0.8 %shard_map.120 = f32[16,2560]{1,0:T(8,128)S(1)} custom-call(bf16[32,512]{1,0:T(8,128)(2,1)S(1)} %get-tuple-element.46.lg_ref, bf16[512,2560]{1,0:T(8,128)(2,1)S(1)} %get-tuple-element.47.rh_ref, bf16[512,2560]{1,0:T(8,128)(2,1)S(1)} %get-tuple-element.48.rl_ref), custom_call_target="tpu_custom_call" | custom-call | tf_op jit(solution)/shard_map/pallas_call | solution.py:456
  10.2 2.9 %collective-permute-start.1 = (f32[16,2560]{1,0:T(8,128)S(1)}, f32[16,2560]{1,0:T(8,128)S(1)}, u32[]{:S(2)}, u32[]{:S(2)}) collective-permute-start(f32[16,2560]{1,0:T(8,128)S(1)} %add.6.own_ref), channel_id=1, source_target_pairs={{0,2},{1,3},{2,0},{3,1},{4,6},{5,7},{6,4},{7,5},{8,10},{9,11},{10,... | collective-permute-start | bytes 491528 | tf_op jit(solution)/shard_map/ppermute | solution.py:27
  13.1 1.5 %collective-permute-start.2 = (f32[16,768]{1,0:T(8,128)S(1)}, f32[16,768]{1,0:T(8,128)S(1)}, u32[]{:S(2)}, u32[]{:S(2)}) collective-permute-start(f32[16,768]{1,0:T(8,128)S(1)} %get-tuple-element.54.own_ref), channel_id=1, source_target_pairs={{0,4},{4,0},{8,12},{12,8},{16,20},{20,16},{24,28},{28,24},{1,5},{5... | collective-permute-start | bytes 147464 | tf_op jit(solution)/shard_map/ppermute | solution.py:27
  14.6 2.6 %collective-permute-done.2.got_ref.refs_0_ = f32[16,768]{1,0:T(8,128)S(1)} collective-permute-done((f32[16,768]{1,0:T(8,128)S(1)}, f32[16,768]{1,0:T(8,128)S(1)}, u32[]{:S(2)}, u32[]{:S(2)}) %collective-permute-start.2) | collective-permute-done | bytes 49184 | tf_op jit(solution)/shard_map/ppermute | solution.py:27
  17.2 1.6 %collective-permute-start.3 = (f32[16,640]{1,0:T(8,128)S(1)}, f32[16,640]{1,0:T(8,128)S(1)}, u32[]{:S(2)}, u32[]{:S(2)}) collective-permute-start(f32[16,640]{1,0:T(8,128)S(1)} %get-tuple-element.55), channel_id=1, source_target_pairs={{0,8},{4,12},{8,0},{12,4},{16,24},{20,28},{24,16},{28,20},{1,9},{5... | collective-permute-start | bytes 122888 | tf_op jit(solution)/shard_map/ppermute | solution.py:27
  18.9 2.5 %collective-permute-start.4 = (f32[16,640]{1,0:T(8,128)S(1)}, f32[16,640]{1,0:T(8,128)S(1)}, u32[]{:S(2)}, u32[]{:S(2)}) collective-permute-start(f32[16,640]{1,0:T(8,128)S(1)} %get-tuple-element.56), channel_id=1, source_target_pairs={{0,24},{4,28},{8,16},{12,20},{16,8},{20,12},{24,0},{28,4},{1,25},{... | collective-permute-start | bytes 122888 | tf_op jit(solution)/shard_map/ppermute | solution.py:27
  23.1 1.6 %collective-permute-done.4.refs_2_.refs_3_ = f32[16,640]{1,0:T(8,128)S(1)} collective-permute-done((f32[16,640]{1,0:T(8,128)S(1)}, f32[16,640]{1,0:T(8,128)S(1)}, u32[]{:S(2)}, u32[]{:S(2)}) %collective-permute-start.4) | collective-permute-done | bytes 40992 | tf_op jit(solution)/shard_map/ppermute | solution.py:27
  25.0 0.9 %collective-permute-start.6 = (f32[16,512]{1,0:T(8,128)S(1)}, f32[16,512]{1,0:T(8,128)S(1)}, u32[]{:S(2)}, u32[]{:S(2)}) collective-permute-start(f32[16,512]{1,0:T(8,128)S(1)} %get-tuple-element.58.refs_0_), channel_id=1, source_target_pairs={{0,16},{4,20},{8,24},{12,28},{16,0},{20,4},{24,8},{28,12},{1,17},{... | collective-permute-start | bytes 98312 | tf_op jit(solution)/shard_map/ppermute | solution.py:27
  25.9 4.4 %collective-permute-done.6.refs_2_ = f32[16,512]{1,0:T(8,128)S(1)} collective-permute-done((f32[16,512]{1,0:T(8,128)S(1)}, f32[16,512]{1,0:T(8,128)S(1)}, u32[]{:S(2)}, u32[]{:S(2)}) %collective-permute-start.6) | collective-permute-done | bytes 32800 | tf_op jit(solution)/shard_map/ppermute | solution.py:27
  30.3 2.6 %shard_map.127 = (f32[16,2560]{1,0:T(8,128)S(1)}, f32[8,512]{1,0:T(8,128)S(1)}, bf16[2560,512]{1,0:T(8,128)(2,1)S(1)}, bf16[2560,512]{1,0:T(8,128)(2,1)S(1)}) custom-call(f32[16,2560]{1,0:T(8,128)S(1)} %collective-permute-done.5.oth_ref.z_ref.zo_ref, bf16[96,512]{1,0:T(8,128)(2,1)S(1)} %get-tuple-element.62.ly_ref, ...), custom_call_target="tpu_custom_call" | custom-call | tf_op jit(solution)/shard_map/pallas_call | solution.py:483
  33.0 2.6 %shard_map.128 = (f32[16,2560]{1,0:T(8,128)S(1)}, f32[8,512]{1,0:T(8,128)S(1)}, bf16[2560,512]{1,0:T(8,128)(2,1)S(1)}, bf16[2560,512]{1,0:T(8,128)(2,1)S(1)}) custom-call(f32[16,2560]{1,0:T(8,128)S(1)} %get-tuple-element.57.own_ref.z_ref.zw_ref.refs_7_, bf16[96,512]{1,0:T(8,128)(2,1)S(1)} %get-tuple-element.62.ly_ref, ...), custom_call_target="tpu_custom_call" | custom-call | tf_op jit(solution)/shard_map/pallas_call | solution.py:483
  36.2 1.6 %shard_map.129.own_ref = f32[16,768]{1,0:T(8,128)S(1)} custom-call(f32[16,2560]{1,0:T(8,128)S(1)} %collective-permute-done.5.oth_ref.z_ref.zo_ref, bf16[2560,512]{1,0:T(8,128)(2,1)S(1)} %get-tuple-element.65.rho_ref, bf16[2560,512]{1,0:T(8,128)(2,1)S(1)} %get-tuple-element.66.rlo_ref, f32[16,2560]{1,0:T(8,128)S(1)} %get-tuple-element.57.own_ref.z_ref.zw_ref.refs_7_, ...), custom_call_target="tpu_custom_call" | custom-call | tf_op jit(solution)/shard_map/pallas_call | solution.py:493
  37.8 1.5 %collective-permute-start.7 = (f32[16,768]{1,0:T(8,128)S(1)}, f32[16,768]{1,0:T(8,128)S(1)}, u32[]{:S(2)}, u32[]{:S(2)}) collective-permute-start(f32[16,768]{1,0:T(8,128)S(1)} %shard_map.129.own_ref), channel_id=1, source_target_pairs={{0,4},{4,0},{8,12},{12,8},{16,20},{20,16},{24,28},{28,24},{1,5},{5... | collective-permute-start | bytes 147464 | tf_op jit(solution)/shard_map/ppermute | solution.py:27
  39.3 2.6 %collective-permute-done.7.got_ref.refs_16_ = f32[16,768]{1,0:T(8,128)S(1)} collective-permute-done((f32[16,768]{1,0:T(8,128)S(1)}, f32[16,768]{1,0:T(8,128)S(1)}, u32[]{:S(2)}, u32[]{:S(2)}) %collective-permute-start.7) | collective-permute-done | bytes 49184 | tf_op jit(solution)/shard_map/ppermute | solution.py:27
  41.9 2.1 %collective-permute-start.10 = (f32[16,640]{1,0:T(8,128)S(1)}, f32[16,640]{1,0:T(8,128)S(1)}, u32[]{:S(2)}, u32[]{:S(2)}) collective-permute-start(f32[16,640]{1,0:T(8,128)S(1)} %get-tuple-element.71), channel_id=1, source_target_pairs={{0,24},{4,28},{8,16},{12,20},{16,8},{20,12},{24,0},{28,4},{1,25},{... | collective-permute-start | bytes 122888 | tf_op jit(solution)/shard_map/ppermute | solution.py:27
  44.0 2.3 %collective-permute-start.9 = (f32[16,512]{1,0:T(8,128)S(1)}, f32[16,512]{1,0:T(8,128)S(1)}, u32[]{:S(2)}, u32[]{:S(2)}) collective-permute-start(f32[16,512]{1,0:T(8,128)S(1)} %get-tuple-element.69.refs_0_), channel_id=1, source_target_pairs={{0,16},{4,20},{8,24},{12,28},{16,0},{20,4},{24,8},{28,12},{1,17},{... | collective-permute-start | bytes 98312 | tf_op jit(solution)/shard_map/ppermute | solution.py:27
  46.7 2.2 %collective-permute-done.9.refs_2_ = f32[16,512]{1,0:T(8,128)S(1)} collective-permute-done((f32[16,512]{1,0:T(8,128)S(1)}, f32[16,512]{1,0:T(8,128)S(1)}, u32[]{:S(2)}, u32[]{:S(2)}) %collective-permute-start.9) | collective-permute-done | bytes 32800 | tf_op jit(solution)/shard_map/ppermute | solution.py:27
  48.9 0.9 %shard_map.132 = (f32[16,2560]{1,0:T(8,128)S(1)}, f32[16,512]{1,0:T(8,128)S(1)}, f32[32,128]{1,0:T(8,128)}) custom-call(f32[16,512]{1,0:T(8,128)S(1)} %get-tuple-element.69.refs_0_, f32[16,640]{1,0:T(8,128)S(1)} %collective-permute-done.8.refs_1_.refs_17_, f32[16,512]{1,0:T(8,128)S(1)} %collective-permute-done.9.refs_2_, ...), custom_call_target="tpu_custom_call" | custom-call | tf_op jit(solution)/shard_map/pallas_call | solution.py:505
  49.7 4.6 %all-to-all-start = ((f32[32,1,128]{2,1,0:T(1,128)}), f32[32,1,128]{2,1,0:T(1,128)S(1)}, u32[]{:S(2)}, u32[]{:S(2)}) async-start(f32[32,1,128]{2,1,0:T(1,128)} %bitcast.3), calls=%async_computation | async-start | bytes 32768 | tf_op jit(solution)/shard_map/all_to_all | solution.py:511
  54.4 0.8 %shard_map.126 = (f32[1,16,5120]{2,1,0:T(8,128)}, f32[16,512]{1,0:T(8,128)}) custom-call(f32[16,2560]{1,0:T(8,128)S(1)} %get-tuple-element.57.own_ref.z_ref.zw_ref.refs_7_, f32[16,2560]{1,0:T(8,128)S(1)} %collective-permute-done.5.oth_ref.z_ref.zo_ref, f32[16,512]{1,0:T(8,128)S(1)} %get-tuple-element.60.loadings_ref.refs_11_), custom_call_target="tpu_custom_call" | custom-call | tf_op jit(solution)/shard_map/pallas_call | solution.py:479
  55.2 6.3 %all-to-all-done = f32[32,1,128]{2,1,0:T(1,128)S(1)} async-done(((f32[32,1,128]{2,1,0:T(1,128)}), f32[32,1,128]{2,1,0:T(1,128)S(1)}, u32[]{:S(2)}, u32[]{:S(2)}) %all-to-all-start) | async-done | bytes 16416 | tf_op jit(solution)/shard_map/all_to_all | solution.py:511
  61.5 0.8 %shard_map.133 = (f32[1,16,5120]{2,1,0:T(8,128)}, f32[16,512]{1,0:T(8,128)}, f32[1]{0:T(128)}) custom-call(f32[16,2560]{1,0:T(8,128)S(1)} %get-tuple-element.80.own_ref, f32[16,2560]{1,0:T(8,128)S(1)} %collective-permute-done.13.oth_ref, f32[16,512]{1,0:T(8,128)S(1)} %get-tuple-element.81.loadings_ref, f32[32,128]{1,0:T(8,128)S(1)} %bitcast.10), custom_call_target="tpu_custom_call" | custom-call | tf_op jit(solution)/shard_map/pallas_call | solution.py:512
  (35 shorter events, 2.6 us)
Async XLA Ops:
  8.7 1.5 %collective-permute-start = (f32[16,2560]{1,0:T(8,128)S(1)}, f32[16,2560]{1,0:T(8,128)S(1)}, u32[]{:S(2)}, u32[]{:S(2)}) collective-permute-start(f32[16,2560]{1,0:T(8,128)S(1)} %shard_map.121), channel_id=1, source_target_pairs={{0,1},{1,0},{2,3},{3,2},{4,5},{5,4},{6,7},{7,6},{8,9},{9,8},{10,11... | collective-permute-start | bytes 491528 | tf_op jit(solution)/shard_map/ppermute | solution.py:27
  9.2 13.5 %copy-start.4 = (f32[16]{0:T(128)S(1)}, f32[16]{0:T(128)}, u32[]{:S(2)}) copy-start(f32[16]{0:T(128)} %param.13) | copy-start | bytes 196
  9.2 13.6 %copy-start = (f32[1,16,5120]{2,1,0:T(8,128)S(1)}, f32[1,16,5120]{2,1,0:T(8,128)}, u32[]{:S(2)}) copy-start(f32[1,16,5120]{2,1,0:T(8,128)} %z_ref.1) | copy-start | bytes 983044
  9.2 13.6 %copy-start.1 = (f32[1,16,5120]{2,1,0:T(8,128)S(1)}, f32[1,16,5120]{2,1,0:T(8,128)}, u32[]{:S(2)}) copy-start(f32[1,16,5120]{2,1,0:T(8,128)} %mom_ref.1) | copy-start | bytes 983044
  9.2 21.1 %copy-start.2 = (f32[512,16]{0,1:T(8,128)S(1)}, f32[512,16]{0,1:T(8,128)}, u32[]{:S(2)}) copy-start(f32[512,16]{0,1:T(8,128)} %param.10) | copy-start | bytes 98308
  9.2 21.0 %copy-start.3 = (f32[512,16]{0,1:T(8,128)S(1)}, f32[512,16]{0,1:T(8,128)}, u32[]{:S(2)}) copy-start(f32[512,16]{0,1:T(8,128)} %param.12) | copy-start | bytes 98308
  10.2 14.4 %collective-permute-start.1 = (f32[16,2560]{1,0:T(8,128)S(1)}, f32[16,2560]{1,0:T(8,128)S(1)}, u32[]{:S(2)}, u32[]{:S(2)}) collective-permute-start(f32[16,2560]{1,0:T(8,128)S(1)} %add.6.own_ref), channel_id=1, source_target_pairs={{0,2},{1,3},{2,0},{3,1},{4,6},{5,7},{6,4},{7,5},{8,10},{9,11},{10,... | collective-permute-start | bytes 491528 | tf_op jit(solution)/shard_map/ppermute | solution.py:27
  13.1 4.1 %collective-permute-start.2 = (f32[16,768]{1,0:T(8,128)S(1)}, f32[16,768]{1,0:T(8,128)S(1)}, u32[]{:S(2)}, u32[]{:S(2)}) collective-permute-start(f32[16,768]{1,0:T(8,128)S(1)} %get-tuple-element.54.own_ref), channel_id=1, source_target_pairs={{0,4},{4,0},{8,12},{12,8},{16,20},{20,16},{24,28},{28,24},{1,5},{5... | collective-permute-start | bytes 147464 | tf_op jit(solution)/shard_map/ppermute | solution.py:27
  17.2 5.9 %collective-permute-start.3 = (f32[16,640]{1,0:T(8,128)S(1)}, f32[16,640]{1,0:T(8,128)S(1)}, u32[]{:S(2)}, u32[]{:S(2)}) collective-permute-start(f32[16,640]{1,0:T(8,128)S(1)} %get-tuple-element.55), channel_id=1, source_target_pairs={{0,8},{4,12},{8,0},{12,4},{16,24},{20,28},{24,16},{28,20},{1,9},{5... | collective-permute-start | bytes 122888 | tf_op jit(solution)/shard_map/ppermute | solution.py:27
  18.9 5.8 %collective-permute-start.4 = (f32[16,640]{1,0:T(8,128)S(1)}, f32[16,640]{1,0:T(8,128)S(1)}, u32[]{:S(2)}, u32[]{:S(2)}) collective-permute-start(f32[16,640]{1,0:T(8,128)S(1)} %get-tuple-element.56), channel_id=1, source_target_pairs={{0,24},{4,28},{8,16},{12,20},{16,8},{20,12},{24,0},{28,4},{1,25},{... | collective-permute-start | bytes 122888 | tf_op jit(solution)/shard_map/ppermute | solution.py:27
  24.9 5.4 %collective-permute-start.5 = (f32[16,2560]{1,0:T(8,128)S(1)}, f32[16,2560]{1,0:T(8,128)S(1)}, u32[]{:S(2)}, u32[]{:S(2)}) collective-permute-start(f32[16,2560]{1,0:T(8,128)S(1)} %get-tuple-element.57.own_ref.z_ref.zw_ref.refs_7_), channel_id=1, source_target_pairs={{0,1},{1,0},{2,3},{3,2},{4,5},{5,4},{6,7},{7,6},{8,9},{9,8},{10,11... | collective-permute-start | bytes 491528 | tf_op jit(solution)/shard_map/ppermute | solution.py:27
  25.0 5.2 %collective-permute-start.6 = (f32[16,512]{1,0:T(8,128)S(1)}, f32[16,512]{1,0:T(8,128)S(1)}, u32[]{:S(2)}, u32[]{:S(2)}) collective-permute-start(f32[16,512]{1,0:T(8,128)S(1)} %get-tuple-element.58.refs_0_), channel_id=1, source_target_pairs={{0,16},{4,20},{8,24},{12,28},{16,0},{20,4},{24,8},{28,12},{1,17},{... | collective-permute-start | bytes 98312 | tf_op jit(solution)/shard_map/ppermute | solution.py:27
  32.9 2.7 %collective-permute-start.11 = (f32[16,2560]{1,0:T(8,128)S(1)}, f32[16,2560]{1,0:T(8,128)S(1)}, u32[]{:S(2)}, u32[]{:S(2)}) collective-permute-start(f32[16,2560]{1,0:T(8,128)S(1)} %get-tuple-element.73), channel_id=1, source_target_pairs={{0,1},{1,0},{2,3},{3,2},{4,5},{5,4},{6,7},{7,6},{8,9},{9,8},{10,11... | collective-permute-start | bytes 491528 | tf_op jit(solution)/shard_map/ppermute | solution.py:27
  35.6 13.3 %collective-permute-start.12 = (f32[16,2560]{1,0:T(8,128)S(1)}, f32[16,2560]{1,0:T(8,128)S(1)}, u32[]{:S(2)}, u32[]{:S(2)}) collective-permute-start(f32[16,2560]{1,0:T(8,128)S(1)} %add.7.refs_4_), channel_id=1, source_target_pairs={{0,2},{1,3},{2,0},{3,1},{4,6},{5,7},{6,4},{7,5},{8,10},{9,11},{10,... | collective-permute-start | bytes 491528 | tf_op jit(solution)/shard_map/ppermute | solution.py:27
  37.8 4.1 %collective-permute-start.7 = (f32[16,768]{1,0:T(8,128)S(1)}, f32[16,768]{1,0:T(8,128)S(1)}, u32[]{:S(2)}, u32[]{:S(2)}) collective-permute-start(f32[16,768]{1,0:T(8,128)S(1)} %shard_map.129.own_ref), channel_id=1, source_target_pairs={{0,4},{4,0},{8,12},{12,8},{16,20},{20,16},{24,28},{28,24},{1,5},{5... | collective-permute-start | bytes 147464 | tf_op jit(solution)/shard_map/ppermute | solution.py:27
  41.9 7.0 %collective-permute-start.10 = (f32[16,640]{1,0:T(8,128)S(1)}, f32[16,640]{1,0:T(8,128)S(1)}, u32[]{:S(2)}, u32[]{:S(2)}) collective-permute-start(f32[16,640]{1,0:T(8,128)S(1)} %get-tuple-element.71), channel_id=1, source_target_pairs={{0,24},{4,28},{8,16},{12,20},{16,8},{20,12},{24,0},{28,4},{1,25},{... | collective-permute-start | bytes 122888 | tf_op jit(solution)/shard_map/ppermute | solution.py:27
  44.0 4.8 %collective-permute-start.8 = (f32[16,640]{1,0:T(8,128)S(1)}, f32[16,640]{1,0:T(8,128)S(1)}, u32[]{:S(2)}, u32[]{:S(2)}) collective-permute-start(f32[16,640]{1,0:T(8,128)S(1)} %get-tuple-element.70), channel_id=1, source_target_pairs={{0,8},{4,12},{8,0},{12,4},{16,24},{20,28},{24,16},{28,20},{1,9},{5... | collective-permute-start | bytes 122888 | tf_op jit(solution)/shard_map/ppermute | solution.py:27
  44.0 4.8 %collective-permute-start.9 = (f32[16,512]{1,0:T(8,128)S(1)}, f32[16,512]{1,0:T(8,128)S(1)}, u32[]{:S(2)}, u32[]{:S(2)}) collective-permute-start(f32[16,512]{1,0:T(8,128)S(1)} %get-tuple-element.69.refs_0_), channel_id=1, source_target_pairs={{0,16},{4,20},{8,24},{12,28},{16,0},{20,4},{24,8},{28,12},{1,17},{... | collective-permute-start | bytes 98312 | tf_op jit(solution)/shard_map/ppermute | solution.py:27
  49.7 11.8 %collective-permute-start.13 = (f32[16,2560]{1,0:T(8,128)S(1)}, f32[16,2560]{1,0:T(8,128)S(1)}, u32[]{:S(2)}, u32[]{:S(2)}) collective-permute-start(f32[16,2560]{1,0:T(8,128)S(1)} %get-tuple-element.80.own_ref), channel_id=1, source_target_pairs={{0,1},{1,0},{2,3},{3,2},{4,5},{5,4},{6,7},{7,6},{8,9},{9,8},{10,11... | collective-permute-start | bytes 491528 | tf_op jit(solution)/shard_map/ppermute | solution.py:27
  49.7 11.8 %all-to-all-start = ((f32[32,1,128]{2,1,0:T(1,128)}), f32[32,1,128]{2,1,0:T(1,128)S(1)}, u32[]{:S(2)}, u32[]{:S(2)}) async-start(f32[32,1,128]{2,1,0:T(1,128)} %bitcast.3), calls=%async_computation | async-start | bytes 32768 | tf_op jit(solution)/shard_map/all_to_all | solution.py:511

commit v8 on v6

--- a/solution.py
+++ b/solution.py
@@ -97,11 +97,6 @@
     r = c - i
     rh = r.astype(bf16)
     return y, i, rh, (r - rh.astype(f32)).astype(bf16), h, m
-
-
-def factor_terms(rh, rl, lg, k):
-    a = dotg(lg, rh, 1, 1)
-    return a[:k] + a[k:] + dotg(lg[k:], rl, 1, 1)
 
 
 def loading_terms(h, m, rh, rl, k):
@@ -172,11 +167,13 @@
     load_ref[:, : -2 * LANES] = add(loads)
 
 
-def factor_kernel(k, half, sub, lg_ref, rh_ref, rl_ref, fac_ref):
+def factor_kernel(k, half, sub, lg_ref, rh_ref, rl_ref, fac_ref, turned_ref):
     lg = lg_ref[...]
     for i in range(half // sub):
         rows = pl.ds(i * sub, sub)
-        fac_ref[:, i * sub : (i + 1) * sub] = factor_terms(rh_ref[rows, :], rl_ref[rows, :], lg, k)
+        turned_ref[:, rows] = rl_ref[rows, :].T
+        a = dotg(lg, rh_ref[rows, :], 1, 1)
+        fac_ref[:, rows] = a[:k] + a[k:] + dotg(lg[k:], turned_ref[:, rows], 1, 0)
 
 
 def move_loadings_kernel(n_terms, *refs):
@@ -190,30 +187,26 @@
     fill_loadings(newl, ly_ref, lg_ref)
 
 
-def second_kernel(k, half, sub, start, z_ref, ly_ref, lg_ref, cnt_ref, fac_ref, lik_ref, rh_ref, rl_ref):
-    ly, lg = ly_ref[...], lg_ref[...]
-    likes, sums = [], []
+def second_kernel(k, half, sub, start, z_ref, ly_ref, cnt_ref, *refs):
+    *before, load_ref, lik_ref, rh_ref, rl_ref = refs
+    ly = ly_ref[...]
+    loads, likes, sums = [], [], []
     for i in range(half // sub):
         rows = pl.ds(i * sub, sub)
         cf = cnt_ref[pl.ds(start + i * sub, sub), :]
-        y, inten, rh, rl, _, _ = residuals(z_ref[:, rows], cf, ly)
+        y, inten, rh, rl, h, m = residuals(z_ref[:, rows], cf, ly)
         rh_ref[rows, :] = rh
         rl_ref[rows, :] = rl
-        fac_ref[:, rows] = factor_terms(rh, rl, lg, k)
+        loads.append(loading_terms(h, m, rh, rl, k))
         likes.append(rows_to_8(cf * y))
         sums.append(rows_to_8(inten))
     lik_ref[...] = add(sums) - f32(LN2) * add(likes)
-
-
-def loading_kernel(k, half, sub, zo_ref, rho_ref, rlo_ref, zw_ref, rhw_ref, rlw_ref, load_ref):
-    loads = []
-    for z_ref, rh_ref, rl_ref in ((zo_ref, rho_ref, rlo_ref), (zw_ref, rhw_ref, rlw_ref)):
-        for i in range(half // sub):
-            rows = pl.ds(i * sub, sub)
-            h, m, _ = split3(z_ref[:, rows])
-            loads.append(loading_terms(h, m, rh_ref[rows, :], rl_ref[rows, :], k))
-    load_ref[:, : -2 * LANES] = add(loads)
-    load_ref[:, -2 * LANES : -LANES], load_ref[:, -LANES:] = pack_rims(in_order(zw_ref[...], zo_ref[...]), k)
+    if not before:
+        load_ref[...] = add(loads)
+        return
+    part_ref, zw_ref = before
+    load_ref[:, : -2 * LANES] = add(loads) + part_ref[...]
+    load_ref[:, -2 * LANES : -LANES], load_ref[:, -LANES:] = pack_rims(in_order(zw_ref[...], z_ref[...]), k)
 
 
 def lane(shape):
@@ -451,10 +444,14 @@
         (1, 3, 4, 5, 6),
     )(*[pltpu.with_memory_space_constraint(x, pltpu.HBM) for x in (factors, lt, counts)])
     load_terms, halo = exchange(load)
-    (oth,), (own,) = [
-        call(functools.partial(factor_kernel, k, half, sub), [VMEM] * 3, [(k, half)])(lg, rh, rl)
-        for rh, rl in ((rho, rlo), (rhw, rlw))
-    ]
+
+    def factors_of(lg, rh, rl):
+        kernel = functools.partial(factor_kernel, k, half, sub)
+        scratch = [pltpu.VMEM((species, half), bf16)]
+        return call(kernel, [VMEM] * 3, [(k, half)], scratch, limit=6)(lg, rh, rl)[0]
+
+    oth = factors_of(lg, rho, rlo)
+    own = factors_of(lg, rhw, rlw)
     own, other = share(own, oth)
 
     halo = sideways(rims_kernel, halo, factors)
@@ -478,19 +475,20 @@
     new_factors, new_loadings = call(
         functools.partial(output_kernel, half), [VMEM] * 3, [(1, k, cells), (k, species)]
     )(moved_own, moved_oth, newl)
-    (own, lik_own, *parts_own), (oth, lik_oth, *parts_oth) = [
-        call(
+
+    def second(start, z, before, load_shape):
+        return call(
             functools.partial(second_kernel, k, half, sub, start),
-            [VMEM] * 4,
-            [(k, half), (8, species), (half, species), (half, species)],
+            [VMEM] * (3 + len(before)),
+            [load_shape, (8, species), (half, species), (half, species)],
             limit=8,
             packed=(2, 3),
-        )(z, ly, lg, held)
-        for start, z in ((half, moved_own), (0, moved_oth))
-    ]
-    (load,) = call(functools.partial(loading_kernel, k, half, sub), [VMEM] * 6, [(k, species + 2 * LANES)])(
-        moved_oth, *parts_oth, moved_own, *parts_own
-    )
+        )(z, ly, held, *before)
+
+    load, lik_own, rhw, rlw = second(half, moved_own, (), (k, species))
+    load, lik_oth, rho, rlo = second(0, moved_oth, (load, moved_own), (k, species + 2 * LANES))
+    oth = factors_of(lg, rho, rlo)
+    own = factors_of(lg, rhw, rlw)
     load_terms, halo = exchange(load)
     own, other = share(own, oth)
 

time: 62.2 us -> 62.9 us (1.011)
    pallas_call x5 -> x6, Pallas kernels: 9.6 us -> 10.1 us  [the longest x4 5.19 us: factors_of(): call(kernel, [VMEM] * 3, [(k, half)], scratch, limit=6)(lg, rh, rl)[0]]
  transfers between devices with their start and end apart: 15 -> 15, of which waited for: 6 -> 7; matrix products, arithmetic and copies ran while one was open for 0% -> 0% of each run, Pallas kernels for 11% -> 10%
where the time goes in v8:
time: 62.9 us; the launch traced here: 62.7 us
  starting transfers between devices  21 us (33%)
  Pallas kernels  19.7 us (31%)
  waiting for transfers between devices  19.7 us (31%)
  between operations  2.21 us (4%)
    ppermute x14, starting transfers between devices, swap(): lax.ppermute(block, axis, [(i, i ^ mask) for i in range(lax.axis_size(axi...  16.4 us
    ppermute x14, waiting for transfers between devices, swap(): lax.ppermute(block, axis, [(i, i ^ mask) for i in range(lax.axis_size(axi...  13.4 us
    all_to_all x1, waiting for transfers between devices, local(): shares = lax.all_to_all(shares, ('site', 'sp'), 0, 0, tiled=True)  6.34 us
    pallas_call x1, Pallas kernels, local(): call(functools.partial(first_kernel, k, half, sub), [HBM, HBM, HBM], [(k,...  6.11 us
    pallas_call x4, Pallas kernels, factors_of(): call(kernel, [VMEM] * 3, [(k, half)], scratch, limit=6)(lg, rh, rl)[0]  5.19 us
    pallas_call x2, Pallas kernels, second(): call(functools.partial(second_kernel, k, half, sub, start), [VMEM] * (3 +...  4.95 us
    all_to_all x1, starting transfers between devices, local(): shares = lax.all_to_all(shares, ('site', 'sp'), 0, 0, tiled=True)  4.6 us
  transfers between devices with their start and end apart: 15, of which 7 were waited for; matrix products, arithmetic and copies ran while one was open for 0% of the time, Pallas kernels for 10%

profile of v8, /device:TPU:0, one launch (start us, length us, event | category | flops | bytes accessed | tf_op | source)
XLA Modules:
  0.0 62.7 jit_solution(8506488022323608183)
XLA Ops:
  0.6 6.1 %shard_map.119 = (f32[16,768]{1,0:T(8,128)S(1)}, bf16[32,512]{1,0:T(8,128)(2,1)S(1)}, f32[5120,512]{1,0:T(8,128)S(1)}, bf16[2560,512]{1,0:T(8,128)(2,1)S(1)}, bf...) custom-call(f32[1,16,5120]{2,1,0:T(8,128)} %z_ref.1, f32[16,512]{1,0:T(8,128)} %bitcast.8, ...), custom_call_target="tpu_custom_call" | custom-call | tf_op jit(solution)/shard_map/pallas_call | solution.py:431
  6.8 1.3 %shard_map.121 = f32[16,2560]{1,0:T(8,128)S(1)} custom-call(bf16[32,512]{1,0:T(8,128)(2,1)S(1)} %get-tuple-element.46.lg_ref, bf16[2560,512]{1,0:T(8,128)(2,1)S(1)} %get-tuple-element.49.rh_ref, bf16[2560,512]{1,0:T(8,128)(2,1)S(1)} %get-tuple-element.50.rl_ref), custom_call_target="tpu_custom_call" | custom-call | tf_op jit(solution)/shard_map/pallas_call | solution.py:451
  8.5 1.3 %shard_map.120 = f32[16,2560]{1,0:T(8,128)S(1)} custom-call(bf16[32,512]{1,0:T(8,128)(2,1)S(1)} %get-tuple-element.46.lg_ref, bf16[2560,512]{1,0:T(8,128)(2,1)S(1)} %get-tuple-element.47.rh_ref, bf16[2560,512]{1,0:T(8,128)(2,1)S(1)} %get-tuple-element.48.rl_ref), custom_call_target="tpu_custom_call" | custom-call | tf_op jit(solution)/shard_map/pallas_call | solution.py:451
  9.8 2.6 %collective-permute-start.1 = (f32[16,2560]{1,0:T(8,128)S(1)}, f32[16,2560]{1,0:T(8,128)S(1)}, u32[]{:S(2)}, u32[]{:S(2)}) collective-permute-start(f32[16,2560]{1,0:T(8,128)S(1)} %add.6.own_ref), channel_id=1, source_target_pairs={{0,2},{1,3},{2,0},{3,1},{4,6},{5,7},{6,4},{7,5},{8,10},{9,11},{10,... | collective-permute-start | bytes 491528 | tf_op jit(solution)/shard_map/ppermute | solution.py:27
  12.5 1.5 %collective-permute-start.2 = (f32[16,768]{1,0:T(8,128)S(1)}, f32[16,768]{1,0:T(8,128)S(1)}, u32[]{:S(2)}, u32[]{:S(2)}) collective-permute-start(f32[16,768]{1,0:T(8,128)S(1)} %get-tuple-element.54.own_ref), channel_id=1, source_target_pairs={{0,4},{4,0},{8,12},{12,8},{16,20},{20,16},{24,28},{28,24},{1,5},{5... | collective-permute-start | bytes 147464 | tf_op jit(solution)/shard_map/ppermute | solution.py:27
  14.0 2.6 %collective-permute-done.2.got_ref.refs_0_ = f32[16,768]{1,0:T(8,128)S(1)} collective-permute-done((f32[16,768]{1,0:T(8,128)S(1)}, f32[16,768]{1,0:T(8,128)S(1)}, u32[]{:S(2)}, u32[]{:S(2)}) %collective-permute-start.2) | collective-permute-done | bytes 49184 | tf_op jit(solution)/shard_map/ppermute | solution.py:27
  16.6 1.6 %collective-permute-start.3 = (f32[16,640]{1,0:T(8,128)S(1)}, f32[16,640]{1,0:T(8,128)S(1)}, u32[]{:S(2)}, u32[]{:S(2)}) collective-permute-start(f32[16,640]{1,0:T(8,128)S(1)} %get-tuple-element.55), channel_id=1, source_target_pairs={{0,8},{4,12},{8,0},{12,4},{16,24},{20,28},{24,16},{28,20},{1,9},{5... | collective-permute-start | bytes 122888 | tf_op jit(solution)/shard_map/ppermute | solution.py:27
  18.2 2.5 %collective-permute-start.4 = (f32[16,640]{1,0:T(8,128)S(1)}, f32[16,640]{1,0:T(8,128)S(1)}, u32[]{:S(2)}, u32[]{:S(2)}) collective-permute-start(f32[16,640]{1,0:T(8,128)S(1)} %get-tuple-element.56), channel_id=1, source_target_pairs={{0,24},{4,28},{8,16},{12,20},{16,8},{20,12},{24,0},{28,4},{1,25},{... | collective-permute-start | bytes 122888 | tf_op jit(solution)/shard_map/ppermute | solution.py:27
  22.4 1.6 %collective-permute-done.4.refs_2_.refs_3_ = f32[16,640]{1,0:T(8,128)S(1)} collective-permute-done((f32[16,640]{1,0:T(8,128)S(1)}, f32[16,640]{1,0:T(8,128)S(1)}, u32[]{:S(2)}, u32[]{:S(2)}) %collective-permute-start.4) | collective-permute-done | bytes 40992 | tf_op jit(solution)/shard_map/ppermute | solution.py:27
  24.3 0.9 %collective-permute-start.6 = (f32[16,512]{1,0:T(8,128)S(1)}, f32[16,512]{1,0:T(8,128)S(1)}, u32[]{:S(2)}, u32[]{:S(2)}) collective-permute-start(f32[16,512]{1,0:T(8,128)S(1)} %get-tuple-element.58.refs_0_), channel_id=1, source_target_pairs={{0,16},{4,20},{8,24},{12,28},{16,0},{20,4},{24,8},{28,12},{1,17},{... | collective-permute-start | bytes 98312 | tf_op jit(solution)/shard_map/ppermute | solution.py:27
  25.2 4.4 %collective-permute-done.6.refs_2_ = f32[16,512]{1,0:T(8,128)S(1)} collective-permute-done((f32[16,512]{1,0:T(8,128)S(1)}, f32[16,512]{1,0:T(8,128)S(1)}, u32[]{:S(2)}, u32[]{:S(2)}) %collective-permute-start.6) | collective-permute-done | bytes 32800 | tf_op jit(solution)/shard_map/ppermute | solution.py:27
  29.6 2.4 %shard_map.127 = (f32[16,512]{1,0:T(8,128)S(1)}, f32[8,512]{1,0:T(8,128)S(1)}, bf16[2560,512]{1,0:T(8,128)(2,1)S(1)}, bf16[2560,512]{1,0:T(8,128)(2,1)S(1)}) custom-call(f32[16,2560]{1,0:T(8,128)S(1)} %get-tuple-element.57.own_ref.z_ref.refs_1_.refs_7_, bf16[96,512]{1,0:T(8,128)(2,1)S(1)} %get-tuple-element.62.ly_ref, f32[5120,512]{1,0:T(8,128)S(1)} %get-tuple-element.63.cnt_ref), custom_call_target="tpu_custom_call" | custom-call | tf_op jit(solution)/shard_map/pallas_call | solution.py:480
  32.1 2.5 %shard_map.128 = (f32[16,768]{1,0:T(8,128)S(1)}, f32[8,512]{1,0:T(8,128)S(1)}, bf16[2560,512]{1,0:T(8,128)(2,1)S(1)}, bf16[2560,512]{1,0:T(8,128)(2,1)S(1)}) custom-call(f32[16,2560]{1,0:T(8,128)S(1)} %collective-permute-done.5.oth_ref.z_ref, bf16[96,512]{1,0:T(8,128)(2,1)S(1)} %get-tuple-element.62.ly_ref, f32[5120,512]{1,0:T(8,128)S(1)} %get-tuple-element.63.cnt_ref, ...), custom_call_target="tpu_custom_call" | custom-call | tf_op jit(solution)/shard_map/pallas_call | solution.py:480
  34.6 1.4 %shard_map.131 = f32[16,2560]{1,0:T(8,128)S(1)} custom-call(bf16[32,512]{1,0:T(8,128)(2,1)S(1)} %get-tuple-element.69.lg_ref, bf16[2560,512]{1,0:T(8,128)(2,1)S(1)} %get-tuple-element.72.rh_ref, bf16[2560,512]{1,0:T(8,128)(2,1)S(1)} %get-tuple-element.73.rl_ref), custom_call_target="tpu_custom_call" | custom-call | tf_op jit(solution)/shard_map/pallas_call | solution.py:451
  36.1 1.3 %shard_map.130 = f32[16,2560]{1,0:T(8,128)S(1)} custom-call(bf16[32,512]{1,0:T(8,128)(2,1)S(1)} %get-tuple-element.69.lg_ref, bf16[2560,512]{1,0:T(8,128)(2,1)S(1)} %get-tuple-element.70.rh_ref, bf16[2560,512]{1,0:T(8,128)(2,1)S(1)} %get-tuple-element.71.rl_ref), custom_call_target="tpu_custom_call" | custom-call | tf_op jit(solution)/shard_map/pallas_call | solution.py:451
  38.0 1.5 %collective-permute-start.7 = (f32[16,768]{1,0:T(8,128)S(1)}, f32[16,768]{1,0:T(8,128)S(1)}, u32[]{:S(2)}, u32[]{:S(2)}) collective-permute-start(f32[16,768]{1,0:T(8,128)S(1)} %get-tuple-element.65.own_ref), channel_id=1, source_target_pairs={{0,4},{4,0},{8,12},{12,8},{16,20},{20,16},{24,28},{28,24},{1,5},{5... | collective-permute-start | bytes 147464 | tf_op jit(solution)/shard_map/ppermute | solution.py:27
  39.6 2.6 %collective-permute-done.7.got_ref.refs_16_ = f32[16,768]{1,0:T(8,128)S(1)} collective-permute-done((f32[16,768]{1,0:T(8,128)S(1)}, f32[16,768]{1,0:T(8,128)S(1)}, u32[]{:S(2)}, u32[]{:S(2)}) %collective-permute-start.7) | collective-permute-done | bytes 49184 | tf_op jit(solution)/shard_map/ppermute | solution.py:27
  42.2 2.2 %collective-permute-start.10 = (f32[16,640]{1,0:T(8,128)S(1)}, f32[16,640]{1,0:T(8,128)S(1)}, u32[]{:S(2)}, u32[]{:S(2)}) collective-permute-start(f32[16,640]{1,0:T(8,128)S(1)} %get-tuple-element.68), channel_id=1, source_target_pairs={{0,24},{4,28},{8,16},{12,20},{16,8},{20,12},{24,0},{28,4},{1,25},{... | collective-permute-start | bytes 122888 | tf_op jit(solution)/shard_map/ppermute | solution.py:27
  44.3 2.3 %collective-permute-start.9 = (f32[16,512]{1,0:T(8,128)S(1)}, f32[16,512]{1,0:T(8,128)S(1)}, u32[]{:S(2)}, u32[]{:S(2)}) collective-permute-start(f32[16,512]{1,0:T(8,128)S(1)} %get-tuple-element.66.refs_0_), channel_id=1, source_target_pairs={{0,16},{4,20},{8,24},{12,28},{16,0},{20,4},{24,8},{28,12},{1,17},{... | collective-permute-start | bytes 98312 | tf_op jit(solution)/shard_map/ppermute | solution.py:27
  47.0 2.2 %collective-permute-done.9.refs_2_ = f32[16,512]{1,0:T(8,128)S(1)} collective-permute-done((f32[16,512]{1,0:T(8,128)S(1)}, f32[16,512]{1,0:T(8,128)S(1)}, u32[]{:S(2)}, u32[]{:S(2)}) %collective-permute-start.9) | collective-permute-done | bytes 32800 | tf_op jit(solution)/shard_map/ppermute | solution.py:27
  49.2 0.9 %shard_map.133 = (f32[16,2560]{1,0:T(8,128)S(1)}, f32[16,512]{1,0:T(8,128)S(1)}, f32[32,128]{1,0:T(8,128)}) custom-call(f32[16,512]{1,0:T(8,128)S(1)} %get-tuple-element.66.refs_0_, f32[16,640]{1,0:T(8,128)S(1)} %collective-permute-done.8.refs_1_.refs_17_, f32[16,512]{1,0:T(8,128)S(1)} %collective-permute-done.9.refs_2_, ...), custom_call_target="tpu_custom_call" | custom-call | tf_op jit(solution)/shard_map/pallas_call | solution.py:501
  50.1 4.6 %all-to-all-start = ((f32[32,1,128]{2,1,0:T(1,128)}), f32[32,1,128]{2,1,0:T(1,128)S(1)}, u32[]{:S(2)}, u32[]{:S(2)}) async-start(f32[32,1,128]{2,1,0:T(1,128)} %bitcast.3), calls=%async_computation | async-start | bytes 32768 | tf_op jit(solution)/shard_map/all_to_all | solution.py:507
  55.4 6.3 %all-to-all-done = f32[32,1,128]{2,1,0:T(1,128)S(1)} async-done(((f32[32,1,128]{2,1,0:T(1,128)}), f32[32,1,128]{2,1,0:T(1,128)S(1)}, u32[]{:S(2)}, u32[]{:S(2)}) %all-to-all-start) | async-done | bytes 16416 | tf_op jit(solution)/shard_map/all_to_all | solution.py:507
  61.8 0.8 %shard_map.134 = (f32[1,16,5120]{2,1,0:T(8,128)}, f32[16,512]{1,0:T(8,128)}, f32[1]{0:T(128)}) custom-call(f32[16,2560]{1,0:T(8,128)S(1)} %get-tuple-element.80.own_ref, f32[16,2560]{1,0:T(8,128)S(1)} %collective-permute-done.13.oth_ref, f32[16,512]{1,0:T(8,128)S(1)} %get-tuple-element.81.loadings_ref, f32[32,128]{1,0:T(8,128)S(1)} %bitcast.10), custom_call_target="tpu_custom_call" | custom-call | tf_op jit(solution)/shard_map/pallas_call | solution.py:508
  (36 shorter events, 3.3 us)
Async XLA Ops:
  8.0 1.8 %collective-permute-start = (f32[16,2560]{1,0:T(8,128)S(1)}, f32[16,2560]{1,0:T(8,128)S(1)}, u32[]{:S(2)}, u32[]{:S(2)}) collective-permute-start(f32[16,2560]{1,0:T(8,128)S(1)} %shard_map.121), channel_id=1, source_target_pairs={{0,1},{1,0},{2,3},{3,2},{4,5},{5,4},{6,7},{7,6},{8,9},{9,8},{10,11... | collective-permute-start | bytes 491528 | tf_op jit(solution)/shard_map/ppermute | solution.py:27
  8.5 13.5 %copy-start.4 = (f32[16]{0:T(128)S(1)}, f32[16]{0:T(128)}, u32[]{:S(2)}) copy-start(f32[16]{0:T(128)} %param.13) | copy-start | bytes 196
  8.5 13.6 %copy-start = (f32[1,16,5120]{2,1,0:T(8,128)S(1)}, f32[1,16,5120]{2,1,0:T(8,128)}, u32[]{:S(2)}) copy-start(f32[1,16,5120]{2,1,0:T(8,128)} %z_ref.1) | copy-start | bytes 983044
  8.5 13.6 %copy-start.1 = (f32[1,16,5120]{2,1,0:T(8,128)S(1)}, f32[1,16,5120]{2,1,0:T(8,128)}, u32[]{:S(2)}) copy-start(f32[1,16,5120]{2,1,0:T(8,128)} %mom_ref.1) | copy-start | bytes 983044
  8.5 21.1 %copy-start.2 = (f32[512,16]{0,1:T(8,128)S(1)}, f32[512,16]{0,1:T(8,128)}, u32[]{:S(2)}) copy-start(f32[512,16]{0,1:T(8,128)} %param.10) | copy-start | bytes 98308
  8.5 21.1 %copy-start.3 = (f32[512,16]{0,1:T(8,128)S(1)}, f32[512,16]{0,1:T(8,128)}, u32[]{:S(2)}) copy-start(f32[512,16]{0,1:T(8,128)} %param.12) | copy-start | bytes 98308
  9.8 14.2 %collective-permute-start.1 = (f32[16,2560]{1,0:T(8,128)S(1)}, f32[16,2560]{1,0:T(8,128)S(1)}, u32[]{:S(2)}, u32[]{:S(2)}) collective-permute-start(f32[16,2560]{1,0:T(8,128)S(1)} %add.6.own_ref), channel_id=1, source_target_pairs={{0,2},{1,3},{2,0},{3,1},{4,6},{5,7},{6,4},{7,5},{8,10},{9,11},{10,... | collective-permute-start | bytes 491528 | tf_op jit(solution)/shard_map/ppermute | solution.py:27
  12.5 4.1 %collective-permute-start.2 = (f32[16,768]{1,0:T(8,128)S(1)}, f32[16,768]{1,0:T(8,128)S(1)}, u32[]{:S(2)}, u32[]{:S(2)}) collective-permute-start(f32[16,768]{1,0:T(8,128)S(1)} %get-tuple-element.54.own_ref), channel_id=1, source_target_pairs={{0,4},{4,0},{8,12},{12,8},{16,20},{20,16},{24,28},{28,24},{1,5},{5... | collective-permute-start | bytes 147464 | tf_op jit(solution)/shard_map/ppermute | solution.py:27
  16.6 5.9 %collective-permute-start.3 = (f32[16,640]{1,0:T(8,128)S(1)}, f32[16,640]{1,0:T(8,128)S(1)}, u32[]{:S(2)}, u32[]{:S(2)}) collective-permute-start(f32[16,640]{1,0:T(8,128)S(1)} %get-tuple-element.55), channel_id=1, source_target_pairs={{0,8},{4,12},{8,0},{12,4},{16,24},{20,28},{24,16},{28,20},{1,9},{5... | collective-permute-start | bytes 122888 | tf_op jit(solution)/shard_map/ppermute | solution.py:27
  18.2 5.8 %collective-permute-start.4 = (f32[16,640]{1,0:T(8,128)S(1)}, f32[16,640]{1,0:T(8,128)S(1)}, u32[]{:S(2)}, u32[]{:S(2)}) collective-permute-start(f32[16,640]{1,0:T(8,128)S(1)} %get-tuple-element.56), channel_id=1, source_target_pairs={{0,24},{4,28},{8,16},{12,20},{16,8},{20,12},{24,0},{28,4},{1,25},{... | collective-permute-start | bytes 122888 | tf_op jit(solution)/shard_map/ppermute | solution.py:27
  24.3 7.8 %collective-permute-start.5 = (f32[16,2560]{1,0:T(8,128)S(1)}, f32[16,2560]{1,0:T(8,128)S(1)}, u32[]{:S(2)}, u32[]{:S(2)}) collective-permute-start(f32[16,2560]{1,0:T(8,128)S(1)} %get-tuple-element.57.own_ref.z_ref.refs_1_.refs_7_), channel_id=1, source_target_pairs={{0,1},{1,0},{2,3},{3,2},{4,5},{5,4},{6,7},{7,6},{8,9},{9,8},{10,11... | collective-permute-start | bytes 491528 | tf_op jit(solution)/shard_map/ppermute | solution.py:27
  24.3 5.2 %collective-permute-start.6 = (f32[16,512]{1,0:T(8,128)S(1)}, f32[16,512]{1,0:T(8,128)S(1)}, u32[]{:S(2)}, u32[]{:S(2)}) collective-permute-start(f32[16,512]{1,0:T(8,128)S(1)} %get-tuple-element.58.refs_0_), channel_id=1, source_target_pairs={{0,16},{4,20},{8,24},{12,28},{16,0},{20,4},{24,8},{28,12},{1,17},{... | collective-permute-start | bytes 98312 | tf_op jit(solution)/shard_map/ppermute | solution.py:27
  36.0 1.4 %collective-permute-start.11 = (f32[16,2560]{1,0:T(8,128)S(1)}, f32[16,2560]{1,0:T(8,128)S(1)}, u32[]{:S(2)}, u32[]{:S(2)}) collective-permute-start(f32[16,2560]{1,0:T(8,128)S(1)} %shard_map.131), channel_id=1, source_target_pairs={{0,1},{1,0},{2,3},{3,2},{4,5},{5,4},{6,7},{7,6},{8,9},{9,8},{10,11... | collective-permute-start | bytes 491528 | tf_op jit(solution)/shard_map/ppermute | solution.py:27
  37.4 11.7 %collective-permute-start.12 = (f32[16,2560]{1,0:T(8,128)S(1)}, f32[16,2560]{1,0:T(8,128)S(1)}, u32[]{:S(2)}, u32[]{:S(2)}) collective-permute-start(f32[16,2560]{1,0:T(8,128)S(1)} %add.7.refs_4_), channel_id=1, source_target_pairs={{0,2},{1,3},{2,0},{3,1},{4,6},{5,7},{6,4},{7,5},{8,10},{9,11},{10,... | collective-permute-start | bytes 491528 | tf_op jit(solution)/shard_map/ppermute | solution.py:27
  38.0 4.1 %collective-permute-start.7 = (f32[16,768]{1,0:T(8,128)S(1)}, f32[16,768]{1,0:T(8,128)S(1)}, u32[]{:S(2)}, u32[]{:S(2)}) collective-permute-start(f32[16,768]{1,0:T(8,128)S(1)} %get-tuple-element.65.own_ref), channel_id=1, source_target_pairs={{0,4},{4,0},{8,12},{12,8},{16,20},{20,16},{24,28},{28,24},{1,5},{5... | collective-permute-start | bytes 147464 | tf_op jit(solution)/shard_map/ppermute | solution.py:27
  42.2 7.0 %collective-permute-start.10 = (f32[16,640]{1,0:T(8,128)S(1)}, f32[16,640]{1,0:T(8,128)S(1)}, u32[]{:S(2)}, u32[]{:S(2)}) collective-permute-start(f32[16,640]{1,0:T(8,128)S(1)} %get-tuple-element.68), channel_id=1, source_target_pairs={{0,24},{4,28},{8,16},{12,20},{16,8},{20,12},{24,0},{28,4},{1,25},{... | collective-permute-start | bytes 122888 | tf_op jit(solution)/shard_map/ppermute | solution.py:27
  44.3 4.8 %collective-permute-start.8 = (f32[16,640]{1,0:T(8,128)S(1)}, f32[16,640]{1,0:T(8,128)S(1)}, u32[]{:S(2)}, u32[]{:S(2)}) collective-permute-start(f32[16,640]{1,0:T(8,128)S(1)} %get-tuple-element.67), channel_id=1, source_target_pairs={{0,8},{4,12},{8,0},{12,4},{16,24},{20,28},{24,16},{28,20},{1,9},{5... | collective-permute-start | bytes 122888 | tf_op jit(solution)/shard_map/ppermute | solution.py:27
  44.3 4.8 %collective-permute-start.9 = (f32[16,512]{1,0:T(8,128)S(1)}, f32[16,512]{1,0:T(8,128)S(1)}, u32[]{:S(2)}, u32[]{:S(2)}) collective-permute-start(f32[16,512]{1,0:T(8,128)S(1)} %get-tuple-element.66.refs_0_), channel_id=1, source_target_pairs={{0,16},{4,20},{8,24},{12,28},{16,0},{20,4},{24,8},{28,12},{1,17},{... | collective-permute-start | bytes 98312 | tf_op jit(solution)/shard_map/ppermute | solution.py:27
  50.1 11.7 %collective-permute-start.13 = (f32[16,2560]{1,0:T(8,128)S(1)}, f32[16,2560]{1,0:T(8,128)S(1)}, u32[]{:S(2)}, u32[]{:S(2)}) collective-permute-start(f32[16,2560]{1,0:T(8,128)S(1)} %get-tuple-element.80.own_ref), channel_id=1, source_target_pairs={{0,1},{1,0},{2,3},{3,2},{4,5},{5,4},{6,7},{7,6},{8,9},{9,8},{10,11... | collective-permute-start | bytes 491528 | tf_op jit(solution)/shard_map/ppermute | solution.py:27
  50.1 11.7 %all-to-all-start = ((f32[32,1,128]{2,1,0:T(1,128)}), f32[32,1,128]{2,1,0:T(1,128)S(1)}, u32[]{:S(2)}, u32[]{:S(2)}) async-start(f32[32,1,128]{2,1,0:T(1,128)} %bitcast.3), calls=%async_computation | async-start | bytes 32768 | tf_op jit(solution)/shard_map/all_to_all | solution.py:507

commit v9 on v8

--- a/solution.py
+++ b/solution.py
@@ -37,6 +37,12 @@
     n = lax.axis_size(axis)
     route = [(i, i + 1 if (i - first) % 2 == 0 else i - 1) for i in range(n)]
     return lax.ppermute(block, axis, [(i, j) for i, j in route if 0 <= j < n])
+
+
+def split_swap(block, masks):
+    n_site, n_sp = lax.axis_size("site"), lax.axis_size("sp")
+    route = [(i * n_sp + j, (i ^ masks[j % 2]) * n_sp + j) for i in range(n_site) for j in range(n_sp)]
+    return lax.ppermute(block, ("site", "sp"), route)
 
 
 def mask_groups(n):
@@ -262,7 +268,7 @@
         near = jnp.where(even, pair[:, -2 * LANES : -LANES], pair[:, -LANES:])
         row = me // 2
         close = (lax.rem(row, 2) == 1) == even
-        far = jnp.where(close, one[:, -LANES:], three[:, -LANES:])
+        far = jnp.where(close == (core() == 0), one[:, -LANES:], three[:, -LANES:])
     else:
         near, far = refs[0][...], refs[1][...]
     left = jnp.where(me == 0, 0.0, jnp.where(even, far, near))
@@ -290,7 +296,7 @@
     even = lax.rem(site, 2) == 0
     first = jnp.where(even, own_ref[:, -2 * LANES : -LANES], got_ref[:, -2 * LANES : -LANES])
     last = jnp.where(even, got_ref[:, -LANES:], own_ref[:, -LANES:])
-    low = lax.rem(site // 2, 2) == 0
+    low = (lax.rem(site // 2, 2) == 0) == (core() == 0)
     one_ref[:, :-LANES] = both
     one_ref[:, -LANES:] = jnp.where(low, last, first)
     two_ref[...] = both
@@ -407,7 +413,8 @@
         got = swap(load, "site", 1)
         wide, narrow = (k, species + LANES), (k, species)
         stage = call(stage_kernel, [VMEM] * 2, [wide, narrow, wide])(load, got)
-        terms = [swap(t, "site", m) for t, m in zip(stage, site[1])]
+        masks = zip(site[1], site[1][::-1])
+        terms = [split_swap(t, m) for t, m in zip(stage, masks)]
         return [stage[1], *terms], (got, terms[0], terms[2])
 
     def upright(low, high):

time: 62.9 us -> 62.9 us (level)
    ppermute x14 -> x8, starting transfers between devices: 16.4 us -> 6.95 us  [swap(): lax.ppermute(block, axis, [(i, i ^ mask) for i in range(lax.axis_size(axi...]
    ppermute x0 -> x6, starting transfers between devices: none -> 9.43 us  [split_swap(): return lax.ppermute(block, ('site', 'sp'), route)]
    ppermute x0 -> x6, waiting for transfers between devices: none -> 8.16 us  [split_swap(): return lax.ppermute(block, ('site', 'sp'), route)]
    ppermute x14 -> x8, waiting for transfers between devices: 13.4 us -> 5.22 us  [swap(): lax.ppermute(block, axis, [(i, i ^ mask) for i in range(lax.axis_size(axi...]
where the time goes in v9:
time: 62.9 us; the launch traced here: 62.7 us
  starting transfers between devices  21 us (33%)
  Pallas kernels  19.7 us (31%)
  waiting for transfers between devices  19.7 us (31%)
  between operations  2.21 us (4%)
    ppermute x6, starting transfers between devices, split_swap(): return lax.ppermute(block, ('site', 'sp'), route)  9.43 us
    ppermute x6, waiting for transfers between devices, split_swap(): return lax.ppermute(block, ('site', 'sp'), route)  8.16 us
    ppermute x8, starting transfers between devices, swap(): lax.ppermute(block, axis, [(i, i ^ mask) for i in range(lax.axis_size(axi...  6.95 us
    all_to_all x1, waiting for transfers between devices, local(): shares = lax.all_to_all(shares, ('site', 'sp'), 0, 0, tiled=True)  6.34 us
    pallas_call x1, Pallas kernels, local(): call(functools.partial(first_kernel, k, half, sub), [HBM, HBM, HBM], [(k,...  6.11 us
    ppermute x8, waiting for transfers between devices, swap(): lax.ppermute(block, axis, [(i, i ^ mask) for i in range(lax.axis_size(axi...  5.22 us
    pallas_call x4, Pallas kernels, factors_of(): call(kernel, [VMEM] * 3, [(k, half)], scratch, limit=6)(lg, rh, rl)[0]  5.18 us
    pallas_call x2, Pallas kernels, second(): call(functools.partial(second_kernel, k, half, sub, start), [VMEM] * (3 +...  4.95 us
  transfers between devices with their start and end apart: 15, of which 7 were waited for; matrix products, arithmetic and copies ran while one was open for 0% of the time, Pallas kernels for 10%

profile of v9, /device:TPU:0, one launch (start us, length us, event | category | flops | bytes accessed | tf_op | source)
XLA Modules:
  0.0 62.7 jit_solution(7823854702132347490)
XLA Ops:
  0.6 6.1 %shard_map.119 = (f32[16,768]{1,0:T(8,128)S(1)}, bf16[32,512]{1,0:T(8,128)(2,1)S(1)}, f32[5120,512]{1,0:T(8,128)S(1)}, bf16[2560,512]{1,0:T(8,128)(2,1)S(1)}, bf...) custom-call(f32[1,16,5120]{2,1,0:T(8,128)} %z_ref.1, f32[16,512]{1,0:T(8,128)} %bitcast.8, ...), custom_call_target="tpu_custom_call" | custom-call | tf_op jit(solution)/shard_map/pallas_call | solution.py:438
  6.8 1.3 %shard_map.121 = f32[16,2560]{1,0:T(8,128)S(1)} custom-call(bf16[32,512]{1,0:T(8,128)(2,1)S(1)} %get-tuple-element.46.lg_ref, bf16[2560,512]{1,0:T(8,128)(2,1)S(1)} %get-tuple-element.49.rh_ref, bf16[2560,512]{1,0:T(8,128)(2,1)S(1)} %get-tuple-element.50.rl_ref), custom_call_target="tpu_custom_call" | custom-call | tf_op jit(solution)/shard_map/pallas_call | solution.py:458
  8.5 1.3 %shard_map.120 = f32[16,2560]{1,0:T(8,128)S(1)} custom-call(bf16[32,512]{1,0:T(8,128)(2,1)S(1)} %get-tuple-element.46.lg_ref, bf16[2560,512]{1,0:T(8,128)(2,1)S(1)} %get-tuple-element.47.rh_ref, bf16[2560,512]{1,0:T(8,128)(2,1)S(1)} %get-tuple-element.48.rl_ref), custom_call_target="tpu_custom_call" | custom-call | tf_op jit(solution)/shard_map/pallas_call | solution.py:458
  9.8 2.6 %collective-permute-start.1 = (f32[16,2560]{1,0:T(8,128)S(1)}, f32[16,2560]{1,0:T(8,128)S(1)}, u32[]{:S(2)}, u32[]{:S(2)}) collective-permute-start(f32[16,2560]{1,0:T(8,128)S(1)} %add.6.own_ref), channel_id=1, source_target_pairs={{0,2},{1,3},{2,0},{3,1},{4,6},{5,7},{6,4},{7,5},{8,10},{9,11},{10,... | collective-permute-start | bytes 491528 | tf_op jit(solution)/shard_map/ppermute | solution.py:27
  12.5 1.5 %collective-permute-start.2 = (f32[16,768]{1,0:T(8,128)S(1)}, f32[16,768]{1,0:T(8,128)S(1)}, u32[]{:S(2)}, u32[]{:S(2)}) collective-permute-start(f32[16,768]{1,0:T(8,128)S(1)} %get-tuple-element.54.own_ref), channel_id=1, source_target_pairs={{0,4},{4,0},{8,12},{12,8},{16,20},{20,16},{24,28},{28,24},{1,5},{5... | collective-permute-start | bytes 147464 | tf_op jit(solution)/shard_map/ppermute | solution.py:27
  14.0 2.6 %collective-permute-done.2.got_ref.refs_0_ = f32[16,768]{1,0:T(8,128)S(1)} collective-permute-done((f32[16,768]{1,0:T(8,128)S(1)}, f32[16,768]{1,0:T(8,128)S(1)}, u32[]{:S(2)}, u32[]{:S(2)}) %collective-permute-start.2) | collective-permute-done | bytes 49184 | tf_op jit(solution)/shard_map/ppermute | solution.py:27
  16.6 1.6 %collective-permute-start.3 = (f32[16,640]{1,0:T(8,128)S(1)}, f32[16,640]{1,0:T(8,128)S(1)}, u32[]{:S(2)}, u32[]{:S(2)}) collective-permute-start(f32[16,640]{1,0:T(8,128)S(1)} %get-tuple-element.55), channel_id=1, source_target_pairs={{0,8},{1,25},{2,10},{3,27},{4,12},{5,29},{6,14},{7,31},{8,0},{9,17... | collective-permute-start | bytes 122888 | tf_op jit(solution)/shard_map/ppermute | solution.py:45
  18.2 2.5 %collective-permute-start.4 = (f32[16,640]{1,0:T(8,128)S(1)}, f32[16,640]{1,0:T(8,128)S(1)}, u32[]{:S(2)}, u32[]{:S(2)}) collective-permute-start(f32[16,640]{1,0:T(8,128)S(1)} %get-tuple-element.56), channel_id=1, source_target_pairs={{0,24},{1,9},{2,26},{3,11},{4,28},{5,13},{6,30},{7,15},{8,16},{9,1... | collective-permute-start | bytes 122888 | tf_op jit(solution)/shard_map/ppermute | solution.py:45
  22.4 1.6 %collective-permute-done.4.refs_2_.refs_3_ = f32[16,640]{1,0:T(8,128)S(1)} collective-permute-done((f32[16,640]{1,0:T(8,128)S(1)}, f32[16,640]{1,0:T(8,128)S(1)}, u32[]{:S(2)}, u32[]{:S(2)}) %collective-permute-start.4) | collective-permute-done | bytes 40992 | tf_op jit(solution)/shard_map/ppermute | solution.py:45
  24.4 0.9 %collective-permute-start.6 = (f32[16,512]{1,0:T(8,128)S(1)}, f32[16,512]{1,0:T(8,128)S(1)}, u32[]{:S(2)}, u32[]{:S(2)}) collective-permute-start(f32[16,512]{1,0:T(8,128)S(1)} %get-tuple-element.58.refs_0_), channel_id=1, source_target_pairs={{0,16},{1,17},{2,18},{3,19},{4,20},{5,21},{6,22},{7,23},{8,24},{9,... | collective-permute-start | bytes 98312 | tf_op jit(solution)/shard_map/ppermute | solution.py:45
  25.2 4.4 %collective-permute-done.6.refs_2_ = f32[16,512]{1,0:T(8,128)S(1)} collective-permute-done((f32[16,512]{1,0:T(8,128)S(1)}, f32[16,512]{1,0:T(8,128)S(1)}, u32[]{:S(2)}, u32[]{:S(2)}) %collective-permute-start.6) | collective-permute-done | bytes 32800 | tf_op jit(solution)/shard_map/ppermute | solution.py:45
  29.6 2.5 %shard_map.127 = (f32[16,512]{1,0:T(8,128)S(1)}, f32[8,512]{1,0:T(8,128)S(1)}, bf16[2560,512]{1,0:T(8,128)(2,1)S(1)}, bf16[2560,512]{1,0:T(8,128)(2,1)S(1)}) custom-call(f32[16,2560]{1,0:T(8,128)S(1)} %get-tuple-element.57.own_ref.z_ref.refs_1_.refs_7_, bf16[96,512]{1,0:T(8,128)(2,1)S(1)} %get-tuple-element.62.ly_ref, f32[5120,512]{1,0:T(8,128)S(1)} %get-tuple-element.63.cnt_ref), custom_call_target="tpu_custom_call" | custom-call | tf_op jit(solution)/shard_map/pallas_call | solution.py:487
  32.1 2.5 %shard_map.128 = (f32[16,768]{1,0:T(8,128)S(1)}, f32[8,512]{1,0:T(8,128)S(1)}, bf16[2560,512]{1,0:T(8,128)(2,1)S(1)}, bf16[2560,512]{1,0:T(8,128)(2,1)S(1)}) custom-call(f32[16,2560]{1,0:T(8,128)S(1)} %collective-permute-done.5.oth_ref.z_ref, bf16[96,512]{1,0:T(8,128)(2,1)S(1)} %get-tuple-element.62.ly_ref, f32[5120,512]{1,0:T(8,128)S(1)} %get-tuple-element.63.cnt_ref, ...), custom_call_target="tpu_custom_call" | custom-call | tf_op jit(solution)/shard_map/pallas_call | solution.py:487
  34.6 1.4 %shard_map.131 = f32[16,2560]{1,0:T(8,128)S(1)} custom-call(bf16[32,512]{1,0:T(8,128)(2,1)S(1)} %get-tuple-element.69.lg_ref, bf16[2560,512]{1,0:T(8,128)(2,1)S(1)} %get-tuple-element.72.rh_ref, bf16[2560,512]{1,0:T(8,128)(2,1)S(1)} %get-tuple-element.73.rl_ref), custom_call_target="tpu_custom_call" | custom-call | tf_op jit(solution)/shard_map/pallas_call | solution.py:458
  36.1 1.2 %shard_map.130 = f32[16,2560]{1,0:T(8,128)S(1)} custom-call(bf16[32,512]{1,0:T(8,128)(2,1)S(1)} %get-tuple-element.69.lg_ref, bf16[2560,512]{1,0:T(8,128)(2,1)S(1)} %get-tuple-element.70.rh_ref, bf16[2560,512]{1,0:T(8,128)(2,1)S(1)} %get-tuple-element.71.rl_ref), custom_call_target="tpu_custom_call" | custom-call | tf_op jit(solution)/shard_map/pallas_call | solution.py:458
  38.0 1.5 %collective-permute-start.7 = (f32[16,768]{1,0:T(8,128)S(1)}, f32[16,768]{1,0:T(8,128)S(1)}, u32[]{:S(2)}, u32[]{:S(2)}) collective-permute-start(f32[16,768]{1,0:T(8,128)S(1)} %get-tuple-element.65.own_ref), channel_id=1, source_target_pairs={{0,4},{4,0},{8,12},{12,8},{16,20},{20,16},{24,28},{28,24},{1,5},{5... | collective-permute-start | bytes 147464 | tf_op jit(solution)/shard_map/ppermute | solution.py:27
  39.6 2.6 %collective-permute-done.7.got_ref.refs_16_ = f32[16,768]{1,0:T(8,128)S(1)} collective-permute-done((f32[16,768]{1,0:T(8,128)S(1)}, f32[16,768]{1,0:T(8,128)S(1)}, u32[]{:S(2)}, u32[]{:S(2)}) %collective-permute-start.7) | collective-permute-done | bytes 49184 | tf_op jit(solution)/shard_map/ppermute | solution.py:27
  42.2 2.2 %collective-permute-start.10 = (f32[16,640]{1,0:T(8,128)S(1)}, f32[16,640]{1,0:T(8,128)S(1)}, u32[]{:S(2)}, u32[]{:S(2)}) collective-permute-start(f32[16,640]{1,0:T(8,128)S(1)} %get-tuple-element.68), channel_id=1, source_target_pairs={{0,24},{1,9},{2,26},{3,11},{4,28},{5,13},{6,30},{7,15},{8,16},{9,1... | collective-permute-start | bytes 122888 | tf_op jit(solution)/shard_map/ppermute | solution.py:45
  44.4 2.3 %collective-permute-start.9 = (f32[16,512]{1,0:T(8,128)S(1)}, f32[16,512]{1,0:T(8,128)S(1)}, u32[]{:S(2)}, u32[]{:S(2)}) collective-permute-start(f32[16,512]{1,0:T(8,128)S(1)} %get-tuple-element.66.refs_0_), channel_id=1, source_target_pairs={{0,16},{1,17},{2,18},{3,19},{4,20},{5,21},{6,22},{7,23},{8,24},{9,... | collective-permute-start | bytes 98312 | tf_op jit(solution)/shard_map/ppermute | solution.py:45
  47.0 2.2 %collective-permute-done.9.refs_2_ = f32[16,512]{1,0:T(8,128)S(1)} collective-permute-done((f32[16,512]{1,0:T(8,128)S(1)}, f32[16,512]{1,0:T(8,128)S(1)}, u32[]{:S(2)}, u32[]{:S(2)}) %collective-permute-start.9) | collective-permute-done | bytes 32800 | tf_op jit(solution)/shard_map/ppermute | solution.py:45
  49.2 0.9 %shard_map.133 = (f32[16,2560]{1,0:T(8,128)S(1)}, f32[16,512]{1,0:T(8,128)S(1)}, f32[32,128]{1,0:T(8,128)}) custom-call(f32[16,512]{1,0:T(8,128)S(1)} %get-tuple-element.66.refs_0_, f32[16,640]{1,0:T(8,128)S(1)} %collective-permute-done.8.refs_1_.refs_17_, f32[16,512]{1,0:T(8,128)S(1)} %collective-permute-done.9.refs_2_, ...), custom_call_target="tpu_custom_call" | custom-call | tf_op jit(solution)/shard_map/pallas_call | solution.py:508
  50.1 4.6 %all-to-all-start = ((f32[32,1,128]{2,1,0:T(1,128)}), f32[32,1,128]{2,1,0:T(1,128)S(1)}, u32[]{:S(2)}, u32[]{:S(2)}) async-start(f32[32,1,128]{2,1,0:T(1,128)} %bitcast.3), calls=%async_computation | async-start | bytes 32768 | tf_op jit(solution)/shard_map/all_to_all | solution.py:514
  55.5 6.3 %all-to-all-done = f32[32,1,128]{2,1,0:T(1,128)S(1)} async-done(((f32[32,1,128]{2,1,0:T(1,128)}), f32[32,1,128]{2,1,0:T(1,128)S(1)}, u32[]{:S(2)}, u32[]{:S(2)}) %all-to-all-start) | async-done | bytes 16416 | tf_op jit(solution)/shard_map/all_to_all | solution.py:514
  61.8 0.8 %shard_map.134 = (f32[1,16,5120]{2,1,0:T(8,128)}, f32[16,512]{1,0:T(8,128)}, f32[1]{0:T(128)}) custom-call(f32[16,2560]{1,0:T(8,128)S(1)} %get-tuple-element.80.own_ref, f32[16,2560]{1,0:T(8,128)S(1)} %collective-permute-done.13.oth_ref, f32[16,512]{1,0:T(8,128)S(1)} %get-tuple-element.81.loadings_ref, f32[32,128]{1,0:T(8,128)S(1)} %bitcast.10), custom_call_target="tpu_custom_call" | custom-call | tf_op jit(solution)/shard_map/pallas_call | solution.py:515
  (36 shorter events, 3.3 us)
Async XLA Ops:
  8.0 1.8 %collective-permute-start = (f32[16,2560]{1,0:T(8,128)S(1)}, f32[16,2560]{1,0:T(8,128)S(1)}, u32[]{:S(2)}, u32[]{:S(2)}) collective-permute-start(f32[16,2560]{1,0:T(8,128)S(1)} %shard_map.121), channel_id=1, source_target_pairs={{0,1},{1,0},{2,3},{3,2},{4,5},{5,4},{6,7},{7,6},{8,9},{9,8},{10,11... | collective-permute-start | bytes 491528 | tf_op jit(solution)/shard_map/ppermute | solution.py:27
  8.5 13.5 %copy-start.4 = (f32[16]{0:T(128)S(1)}, f32[16]{0:T(128)}, u32[]{:S(2)}) copy-start(f32[16]{0:T(128)} %param.13) | copy-start | bytes 196
  8.5 13.6 %copy-start = (f32[1,16,5120]{2,1,0:T(8,128)S(1)}, f32[1,16,5120]{2,1,0:T(8,128)}, u32[]{:S(2)}) copy-start(f32[1,16,5120]{2,1,0:T(8,128)} %z_ref.1) | copy-start | bytes 983044
  8.5 13.6 %copy-start.1 = (f32[1,16,5120]{2,1,0:T(8,128)S(1)}, f32[1,16,5120]{2,1,0:T(8,128)}, u32[]{:S(2)}) copy-start(f32[1,16,5120]{2,1,0:T(8,128)} %mom_ref.1) | copy-start | bytes 983044
  8.5 21.1 %copy-start.2 = (f32[512,16]{0,1:T(8,128)S(1)}, f32[512,16]{0,1:T(8,128)}, u32[]{:S(2)}) copy-start(f32[512,16]{0,1:T(8,128)} %param.10) | copy-start | bytes 98308
  8.5 21.1 %copy-start.3 = (f32[512,16]{0,1:T(8,128)S(1)}, f32[512,16]{0,1:T(8,128)}, u32[]{:S(2)}) copy-start(f32[512,16]{0,1:T(8,128)} %param.12) | copy-start | bytes 98308
  9.8 14.2 %collective-permute-start.1 = (f32[16,2560]{1,0:T(8,128)S(1)}, f32[16,2560]{1,0:T(8,128)S(1)}, u32[]{:S(2)}, u32[]{:S(2)}) collective-permute-start(f32[16,2560]{1,0:T(8,128)S(1)} %add.6.own_ref), channel_id=1, source_target_pairs={{0,2},{1,3},{2,0},{3,1},{4,6},{5,7},{6,4},{7,5},{8,10},{9,11},{10,... | collective-permute-start | bytes 491528 | tf_op jit(solution)/shard_map/ppermute | solution.py:27
  12.5 4.1 %collective-permute-start.2 = (f32[16,768]{1,0:T(8,128)S(1)}, f32[16,768]{1,0:T(8,128)S(1)}, u32[]{:S(2)}, u32[]{:S(2)}) collective-permute-start(f32[16,768]{1,0:T(8,128)S(1)} %get-tuple-element.54.own_ref), channel_id=1, source_target_pairs={{0,4},{4,0},{8,12},{12,8},{16,20},{20,16},{24,28},{28,24},{1,5},{5... | collective-permute-start | bytes 147464 | tf_op jit(solution)/shard_map/ppermute | solution.py:27
  16.6 5.9 %collective-permute-start.3 = (f32[16,640]{1,0:T(8,128)S(1)}, f32[16,640]{1,0:T(8,128)S(1)}, u32[]{:S(2)}, u32[]{:S(2)}) collective-permute-start(f32[16,640]{1,0:T(8,128)S(1)} %get-tuple-element.55), channel_id=1, source_target_pairs={{0,8},{1,25},{2,10},{3,27},{4,12},{5,29},{6,14},{7,31},{8,0},{9,17... | collective-permute-start | bytes 122888 | tf_op jit(solution)/shard_map/ppermute | solution.py:45
  18.2 5.8 %collective-permute-start.4 = (f32[16,640]{1,0:T(8,128)S(1)}, f32[16,640]{1,0:T(8,128)S(1)}, u32[]{:S(2)}, u32[]{:S(2)}) collective-permute-start(f32[16,640]{1,0:T(8,128)S(1)} %get-tuple-element.56), channel_id=1, source_target_pairs={{0,24},{1,9},{2,26},{3,11},{4,28},{5,13},{6,30},{7,15},{8,16},{9,1... | collective-permute-start | bytes 122888 | tf_op jit(solution)/shard_map/ppermute | solution.py:45
  24.3 7.8 %collective-permute-start.5 = (f32[16,2560]{1,0:T(8,128)S(1)}, f32[16,2560]{1,0:T(8,128)S(1)}, u32[]{:S(2)}, u32[]{:S(2)}) collective-permute-start(f32[16,2560]{1,0:T(8,128)S(1)} %get-tuple-element.57.own_ref.z_ref.refs_1_.refs_7_), channel_id=1, source_target_pairs={{0,1},{1,0},{2,3},{3,2},{4,5},{5,4},{6,7},{7,6},{8,9},{9,8},{10,11... | collective-permute-start | bytes 491528 | tf_op jit(solution)/shard_map/ppermute | solution.py:27
  24.4 5.2 %collective-permute-start.6 = (f32[16,512]{1,0:T(8,128)S(1)}, f32[16,512]{1,0:T(8,128)S(1)}, u32[]{:S(2)}, u32[]{:S(2)}) collective-permute-start(f32[16,512]{1,0:T(8,128)S(1)} %get-tuple-element.58.refs_0_), channel_id=1, source_target_pairs={{0,16},{1,17},{2,18},{3,19},{4,20},{5,21},{6,22},{7,23},{8,24},{9,... | collective-permute-start | bytes 98312 | tf_op jit(solution)/shard_map/ppermute | solution.py:45
  36.0 1.4 %collective-permute-start.11 = (f32[16,2560]{1,0:T(8,128)S(1)}, f32[16,2560]{1,0:T(8,128)S(1)}, u32[]{:S(2)}, u32[]{:S(2)}) collective-permute-start(f32[16,2560]{1,0:T(8,128)S(1)} %shard_map.131), channel_id=1, source_target_pairs={{0,1},{1,0},{2,3},{3,2},{4,5},{5,4},{6,7},{7,6},{8,9},{9,8},{10,11... | collective-permute-start | bytes 491528 | tf_op jit(solution)/shard_map/ppermute | solution.py:27
  37.4 11.7 %collective-permute-start.12 = (f32[16,2560]{1,0:T(8,128)S(1)}, f32[16,2560]{1,0:T(8,128)S(1)}, u32[]{:S(2)}, u32[]{:S(2)}) collective-permute-start(f32[16,2560]{1,0:T(8,128)S(1)} %add.7.refs_4_), channel_id=1, source_target_pairs={{0,2},{1,3},{2,0},{3,1},{4,6},{5,7},{6,4},{7,5},{8,10},{9,11},{10,... | collective-permute-start | bytes 491528 | tf_op jit(solution)/shard_map/ppermute | solution.py:27
  38.0 4.1 %collective-permute-start.7 = (f32[16,768]{1,0:T(8,128)S(1)}, f32[16,768]{1,0:T(8,128)S(1)}, u32[]{:S(2)}, u32[]{:S(2)}) collective-permute-start(f32[16,768]{1,0:T(8,128)S(1)} %get-tuple-element.65.own_ref), channel_id=1, source_target_pairs={{0,4},{4,0},{8,12},{12,8},{16,20},{20,16},{24,28},{28,24},{1,5},{5... | collective-permute-start | bytes 147464 | tf_op jit(solution)/shard_map/ppermute | solution.py:27
  42.2 7.0 %collective-permute-start.10 = (f32[16,640]{1,0:T(8,128)S(1)}, f32[16,640]{1,0:T(8,128)S(1)}, u32[]{:S(2)}, u32[]{:S(2)}) collective-permute-start(f32[16,640]{1,0:T(8,128)S(1)} %get-tuple-element.68), channel_id=1, source_target_pairs={{0,24},{1,9},{2,26},{3,11},{4,28},{5,13},{6,30},{7,15},{8,16},{9,1... | collective-permute-start | bytes 122888 | tf_op jit(solution)/shard_map/ppermute | solution.py:45
  44.4 4.8 %collective-permute-start.8 = (f32[16,640]{1,0:T(8,128)S(1)}, f32[16,640]{1,0:T(8,128)S(1)}, u32[]{:S(2)}, u32[]{:S(2)}) collective-permute-start(f32[16,640]{1,0:T(8,128)S(1)} %get-tuple-element.67), channel_id=1, source_target_pairs={{0,8},{1,25},{2,10},{3,27},{4,12},{5,29},{6,14},{7,31},{8,0},{9,17... | collective-permute-start | bytes 122888 | tf_op jit(solution)/shard_map/ppermute | solution.py:45
  44.4 4.8 %collective-permute-start.9 = (f32[16,512]{1,0:T(8,128)S(1)}, f32[16,512]{1,0:T(8,128)S(1)}, u32[]{:S(2)}, u32[]{:S(2)}) collective-permute-start(f32[16,512]{1,0:T(8,128)S(1)} %get-tuple-element.66.refs_0_), channel_id=1, source_target_pairs={{0,16},{1,17},{2,18},{3,19},{4,20},{5,21},{6,22},{7,23},{8,24},{9,... | collective-permute-start | bytes 98312 | tf_op jit(solution)/shard_map/ppermute | solution.py:45
  50.1 11.7 %collective-permute-start.13 = (f32[16,2560]{1,0:T(8,128)S(1)}, f32[16,2560]{1,0:T(8,128)S(1)}, u32[]{:S(2)}, u32[]{:S(2)}) collective-permute-start(f32[16,2560]{1,0:T(8,128)S(1)} %get-tuple-element.80.own_ref), channel_id=1, source_target_pairs={{0,1},{1,0},{2,3},{3,2},{4,5},{5,4},{6,7},{7,6},{8,9},{9,8},{10,11... | collective-permute-start | bytes 491528 | tf_op jit(solution)/shard_map/ppermute | solution.py:27
  50.1 11.7 %all-to-all-start = ((f32[32,1,128]{2,1,0:T(1,128)}), f32[32,1,128]{2,1,0:T(1,128)S(1)}, u32[]{:S(2)}, u32[]{:S(2)}) async-start(f32[32,1,128]{2,1,0:T(1,128)} %bitcast.3), calls=%async_computation | async-start | bytes 32768 | tf_op jit(solution)/shard_map/all_to_all | solution.py:514
